TPU v7x, 256 devices: a whole 4x4x8 slice. The times are simulated.
256 devices in a mesh: rep: 8 (over y, x_hi), blk: 32 (over z, x_lo, core).
Axes of the slice: x: 4 (x_hi: 2, x_lo: 2; x = x_hi * 2 + x_lo), y: 4, z: 8, core: 2. Of those that a mesh axis runs over, the one named last changes fastest.
Arguments:
- node_features: bfloat16 [65536, 256], P(('rep', 'blk')), may hold values from -6 to 6
- tile_values: bfloat16 [8, 32, 128, 128, 128], P('rep', 'blk'), may hold values from -0.09375 to 0.09375
- tile_row: int32 [8, 32, 128], P('rep', 'blk'), may hold values from 0 to 15, as said below
- tile_col: int32 [8, 32, 128], P('rep', 'blk'), may hold values from 0 to 63
- tile_count: int32 [8, 32], P('rep', 'blk'), may hold values from 16 to 128, as said below
- weight: bfloat16 [256, 256], replicated, may hold values from -0.375 to 0.375
- cotangent: bfloat16 [32, 8, 256, 256], P('blk', 'rep'), may hold values from -6 to 6
Outputs:
- layer_out: bfloat16 [32, 8, 256, 256], P('blk', 'rep')
- grad_weight: float32 [256, 256], replicated
- grad_features: bfloat16 [65536, 256], P(('rep', 'blk'))
Inputs may be any that keep to these rules, and one draw needn't show every extreme that they name: `tile_row`: within one device the live slots name distinct tile pairs. Slots 0 to tile_count - 1 of a device are live, the rest are ignored; some device has all 128 slots live.
All inputs are finite; a program needn't handle non-finite values.
Results may differ from a plain program's by a relative error of at most 0.03.
Values may be sent and summed in bfloat16 or wider, within the bound.
No kernel may reach another device: no remote copies, remote signals or barrier semaphores. Data moves between devices by JAX's collectives and lax.ppermute only.
A program may use at most 128 MiB of HBM per device.

v0:
```python
import jax
import jax.numpy as jnp
from jax import lax
from jax.sharding import PartitionSpec as P


def on_device(node_features, tile_values, tile_row, tile_col, tile_count, weight, cotangent):
    rows_dev, features = node_features.shape
    tile_block = tile_values[0, 0]
    slot_rows = tile_row[0, 0]
    slot_cols = tile_col[0, 0]
    live_count = tile_count[0, 0]
    slot_count = tile_block.shape[0]
    tile_size = tile_block.shape[1]
    rep_size = lax.axis_size("rep")
    slab_rows = rows_dev * rep_size
    slab_blocks = slab_rows // tile_size
    live_mask = (jnp.arange(slot_count, dtype=jnp.int32) < live_count).astype(jnp.float32)
    row_hot = (slot_rows[:, None] == jnp.arange(slab_blocks, dtype=jnp.int32)[None, :]).astype(
        jnp.float32
    ) * live_mask[:, None]
    gathered = lax.all_gather(node_features, "blk", axis=0, tiled=True)
    group_blocks = gathered.shape[0] // tile_size
    col_hot = (slot_cols[:, None] == jnp.arange(group_blocks, dtype=jnp.int32)[None, :]).astype(
        jnp.float32
    ) * live_mask[:, None]
    col_blocks = gathered.reshape(group_blocks, tile_size, features)
    picked = jnp.take(col_blocks, slot_cols, axis=0)
    products = jnp.einsum("tij,tjf->tif", tile_block, picked, preferred_element_type=jnp.float32)
    partial_value = (
        jnp.einsum("tk,tif->kif", row_hot, products)
        .reshape(slab_rows, features)
        .astype(jnp.bfloat16)
    )
    hidden_rows = (
        lax.psum_scatter(partial_value, "rep", scatter_dimension=0, tiled=True)
        .astype(jnp.float32)
        .astype(jnp.bfloat16)
    )
    preact = jnp.dot(hidden_rows, weight, preferred_element_type=jnp.float32)
    gating = jax.nn.sigmoid(preact)
    layer_out = (preact * gating).astype(jnp.bfloat16)
    slope_term = gating * (1.0 + preact * (1.0 - gating))
    grad_pre = (cotangent[0, 0].astype(jnp.float32) * slope_term).astype(jnp.bfloat16)
    weight_part = jnp.einsum("nf,ng->fg", hidden_rows, grad_pre, preferred_element_type=jnp.float32)
    grad_hidden = jnp.dot(grad_pre, weight.T, preferred_element_type=jnp.float32).astype(
        jnp.bfloat16
    )
    grad_slab = lax.all_gather(grad_hidden, "rep", axis=0, tiled=True)
    grad_weight = lax.psum(weight_part, ("rep", "blk"))
    grad_blocks = grad_slab.reshape(slab_blocks, tile_size, features)
    picked_rows = jnp.take(grad_blocks, slot_rows, axis=0)
    back_terms = jnp.einsum(
        "tij,tif->tjf", tile_block, picked_rows, preferred_element_type=jnp.float32
    )
    column_terms = (
        jnp.einsum("tk,tjf->kjf", col_hot, back_terms)
        .reshape(group_blocks * tile_size, features)
        .astype(jnp.bfloat16)
    )
    grad_features = (
        lax.psum_scatter(column_terms, "blk", scatter_dimension=0, tiled=True)
        .astype(jnp.float32)
        .astype(jnp.bfloat16)
    )
    return (layer_out.reshape(1, 1, rows_dev, features), grad_weight, grad_features)


def solution(mesh):
    placed = (
        P(("rep", "blk"), None),
        P("rep", "blk", None, None, None),
        P("rep", "blk", None),
        P("rep", "blk", None),
        P("rep", "blk"),
        P(),
        P("blk", "rep", None, None),
    )
    return jax.shard_map(
        on_device,
        mesh=mesh,
        in_specs=placed,
        out_specs=(P("blk", "rep", None, None), P(), P(("rep", "blk"), None)),
        check_vma=False,
    )
```

profile of v0, /device:TPU:1, one launch (start us, length us, event | category | flops | bytes accessed | tf_op | source)
XLA Modules:
  0.0 635.8 jit_solution(16897174415970150977)
XLA Ops:
  7.2 0.0 copy-start
  7.2 0.0 all-gather.3.cloned.1.call-start
  7.2 0.7 all-gather.3.cloned.1.call-update
  7.9 0.0 reduce-scatter.3.cloned.1.call-start
  8.6 0.7 fusion.32
  9.3 0.7 compare_and_fusion.1
  9.9 71.0 %all-gather.3.cloned.1.call-done = bf16[8192,256]{1,0:T(8,128)(2,1)} async-done(((bf16[256,256]{1,0:T(8,128)(2,1)}), bf16[8192,256]{1,0:T(8,128)(2,1)}) %all-gather.3.cloned.1.call-update) | async-done | bytes 4194320 | tf_op jit(solution)/shard_map/all_gather | solution.py:22
  80.9 8.7 %gather_fusion = bf16[128,128,256]{2,1,0:T(8,128)(2,1)} fusion(bf16[64,128,256]{2,1,0:T(8,128)(2,1)} %bitcast.51, s32[1024]{0:T(1024)S(1)} %pad_clamp_fusion.1), kind=kCustom, calls=%fused_computation | custom fusion | bytes 16777728 | tf_op jit(solution)/shard_map/jit(_take)/gather | solution.py:28
  89.7 11.9 %fusion.6 = bf16[128,256,128]{2,1,0:T(8,128)(2,1)} fusion(bf16[128,128,256]{2,1,0:T(8,128)(2,1)} %gather_fusion, pred[128]{0:T(512)(128)(4,1)S(1)} %compare_and_fusion.1, bf16[1,1,128,128,128]{4,3,2,1,0:T(8,128)(2,1)} %param.8), kind=kOutput, calls=%fused_computation.8 | convolution fusion | flops 1077936128 | bytes 20971648 | tf_op jit(solution)/shard_map/tij,tjf->tif/dot_general | solution.py:29
  101.6 12.4 %copy.12 = bf16[128,256,128]{1,0,2:T(8,128)(2,1)} copy(bf16[128,256,128]{2,1,0:T(8,128)(2,1)} %fusion.6) | data formatting | bytes 16777216 | tf_op jit(solution)/shard_map/tij,tjf->tif/dot_general | solution.py:29
  114.0 4.6 fusion.17
  118.6 1.4 copy.10
  119.9 0.0 reduce-scatter.3.cloned.1.call-update
  120.0 0.0 all-gather.5.cloned.1.call-start
  120.0 74.2 %reduce-scatter.3.cloned.1.call-done = bf16[256,256]{1,0:T(8,128)(2,1)} async-done(((bf16[2048,256]{1,0:T(8,128)(2,1)}), bf16[256,256]{1,0:T(8,128)(2,1)}) %reduce-scatter.3.cloned.1.call-update) | async-done | bytes 131088 | tf_op jit(solution)/shard_map/reduce_scatter | solution.py:36
  194.2 1.8 fusion.20
  196.1 0.9 convolution_convert_fusion
  197.0 0.0 all-gather.5.cloned.1.call-update
  197.0 0.0 all-reduce.2.cloned.1.call-start
  197.1 1.8 fusion.38
  198.9 0.0 all-reduce.2.cloned.1.call-update
  198.9 0.2 reduce-scatter.5.cloned.1.call-start
  199.2 49.7 %all-gather.5.cloned.1.call-done = bf16[2048,256]{1,0:T(8,128)(2,1)} async-done(((bf16[256,256]{1,0:T(8,128)(2,1)}), bf16[2048,256]{1,0:T(8,128)(2,1)}) %all-gather.5.cloned.1.call-update) | async-done | bytes 1048592 | tf_op jit(solution)/shard_map/all_gather | solution.py:49
  248.8 7.8 %gather_fusion.1 = bf16[128,128,256]{2,1,0:T(8,128)(2,1)} fusion(bf16[16,128,256]{2,1,0:T(8,128)(2,1)} %bitcast.50, s32[1024]{0:T(1024)S(1)} %pad_clamp_fusion), kind=kCustom, calls=%fused_computation.1 | custom fusion | bytes 16777728 | tf_op jit(solution)/shard_map/jit(_take)/gather | solution.py:52
  256.6 8.9 %fusion.4 = bf16[128,256,128]{2,1,0:T(8,128)(2,1)} fusion(bf16[128,128,256]{2,1,0:T(8,128)(2,1)} %gather_fusion.1, pred[128]{0:T(512)(128)(4,1)S(1)} %compare_and_fusion, bf16[1,1,128,128,128]{4,3,2,1,0:T(8,128)(2,1)} %param.8), kind=kOutput, calls=%fused_computation.6 | convolution fusion | flops 1077936128 | bytes 20971648 | tf_op jit(solution)/shard_map/tij,tif->tjf/dot_general | solution.py:53
  265.5 12.5 %copy.13 = bf16[128,256,128]{1,0,2:T(8,128)(2,1)} copy(bf16[128,256,128]{2,1,0:T(8,128)(2,1)} %fusion.4) | data formatting | bytes 16777216 | tf_op jit(solution)/shard_map/tij,tif->tjf/dot_general | solution.py:53
  278.0 4.7 fusion.14
  282.7 4.4 copy.11
  287.1 0.0 reduce-scatter.5.cloned.1.call-update
  287.1 217.6 %all-reduce.2.cloned.1.call-done = f32[256,256]{1,0:T(8,128)} async-done(((f32[256,256]{1,0:T(8,128)}), f32[256,256]{1,0:T(8,128)}) %all-reduce.2.cloned.1.call-update) | async-done | bytes 262160 | tf_op jit(solution)/shard_map/psum | solution.py:50
  504.7 122.8 %reduce-scatter.5.cloned.1.call-done = bf16[256,256]{1,0:T(8,128)(2,1)} async-done(((bf16[8192,256]{1,0:T(8,128)(2,1)}), bf16[256,256]{1,0:T(8,128)(2,1)}) %reduce-scatter.5.cloned.1.call-update) | async-done | bytes 131088 | tf_op jit(solution)/shard_map/reduce_scatter | solution.py:62
  627.6 1.7 copy.16
  (14 shorter events, 0.0 us)
Async XLA Ops:
  7.2 187.1 %copy-start = (bf16[256,256]{1,0:T(8,128)(2,1)S(1)}, bf16[256,256]{1,0:T(8,128)(2,1)}, u32[]{:S(2)}) copy-start(bf16[256,256]{1,0:T(8,128)(2,1)} %param.12) | copy-start | bytes 393220
  7.2 73.7 %all-gather.3.cloned.1.call-start = ((), (), s32[]{:S(2)}) async-start(), calls=%async_computation.2 | async-start | bytes 4325376 | tf_op jit(solution)/shard_map/all_gather | solution.py:22
  7.9 186.3 %reduce-scatter.3.cloned.1.call-start = ((), (), s32[]{:S(2)}) async-start(), calls=%async_computation.3 | async-start | bytes 1179648 | tf_op jit(solution)/shard_map/reduce_scatter | solution.py:36
  101.6 12.4 %copy-start.2 = (s32[1,1,128]{2,1,0:T(1,128)S(1)}, s32[1,1,128]{2,1,0:T(1,128)}, u32[]{:S(2)}) copy-start(s32[1,1,128]{2,1,0:T(1,128)} %param.9) | copy-start | bytes 1540
  114.0 80.3 %copy-start.4 = (bf16[1,1,256,256]{3,2,1,0:T(8,128)(2,1)S(1)}, bf16[1,1,256,256]{3,2,1,0:T(8,128)(2,1)}, u32[]{:S(2)}) copy-start(bf16[1,1,256,256]{3,2,1,0:T(8,128)(2,1)} %param.13) | copy-start | bytes 393220
  120.0 128.9 %all-gather.5.cloned.1.call-start = ((), (), s32[]{:S(2)}) async-start(), calls=%async_computation.5 | async-start | bytes 1179648 | tf_op jit(solution)/shard_map/all_gather | solution.py:49
  197.0 307.8 %all-reduce.2.cloned.1.call-start = ((), (), s32[]{:S(2)}) async-start(), calls=%async_computation.4 | async-start | bytes 524288 | tf_op jit(solution)/shard_map/psum | solution.py:50
  198.9 428.6 %reduce-scatter.5.cloned.1.call-start = ((), (), s32[]{:S(2)}) async-start(), calls=%async_computation.6 | async-start | bytes 4325376 | tf_op jit(solution)/shard_map/reduce_scatter | solution.py:62
  265.5 12.5 %copy-start.3 = (s32[1,1,128]{2,1,0:T(1,128)S(1)}, s32[1,1,128]{2,1,0:T(1,128)}, u32[]{:S(2)}) copy-start(s32[1,1,128]{2,1,0:T(1,128)} %param.10) | copy-start | bytes 1540
  278.0 351.3 %copy-start.1 = (bf16[256,256]{1,0:T(8,128)(2,1)S(1)}, bf16[256,256]{1,0:T(8,128)(2,1)}, u32[]{:S(2)}) copy-start(bf16[256,256]{1,0:T(8,128)(2,1)} %param.12) | copy-start | bytes 393220
Sparse Core Ops, SparseCore 0:
  9.9 71.0 all-gather.2
  120.1 74.1 reduce-scatter.2
  197.8 50.9 all-gather.4
  255.6 249.1 all-reduce.1
  507.8 119.6 reduce-scatter.4
where the time goes:
time: 639 us; the launch traced here: 636 us
  waiting for transfers between devices  536 us (84%)
  local copies, waits for them, and re-layouts  48.8 us (8%)
  matrix products  34.7 us (5%)
  between operations  14.5 us (2%)
    psum x1, waiting for transfers between devices, on_device(): grad_weight = lax.psum(weight_part, ('rep', 'blk'))  218 us
    reduce_scatter x1, waiting for transfers between devices, on_device(): lax.psum_scatter(column_terms, 'blk', scatter_dimension=0, tiled=True)  123 us
    reduce_scatter x1, waiting for transfers between devices, on_device(): lax.psum_scatter(partial_value, 'rep', scatter_dimension=0, tiled=True)  74.2 us
    all_gather x1, waiting for transfers between devices, on_device(): gathered = lax.all_gather(node_features, 'blk', axis=0, tiled=True)  71 us
    all_gather x1, waiting for transfers between devices, on_device(): grad_slab = lax.all_gather(grad_hidden, 'rep', axis=0, tiled=True)  49.7 us
  transfers between devices with their start and end apart: 5, of which 5 were waited for; matrix products, arithmetic and copies ran while one was open for 7% of the time, Pallas kernels for 0%

commit v1 on v0

v1 whole, which is shorter than its diff:
```python
import jax
import jax.numpy as jnp
import numpy as np
from jax import lax
from jax.experimental import pallas as pl
from jax.experimental.pallas import tpu as pltpu
from jax.sharding import Mesh
from jax.sharding import PartitionSpec as P

REP = ("y", "xh")
BLK = ("z", "xl", "core")
N_Z = 8
TILE = 128
F = 256
XR = 256
N_REP = 8
SLOTS = 128
ROW_BLOCKS = 16
WROWS = F // N_REP
PA = 176
PD = 160
QA = XR - PA
QD = XR - PD
T_CHUNKS = 8
UNROLL = 4

f32 = jnp.float32
bf16 = jnp.bfloat16
VMEM_LIMIT = 56 << 20


def pair_swap(x, axis):
    return lax.ppermute(x, axis, [(0, 1), (1, 0)])


def spread(x, axes, n):
    return lax.all_to_all(jnp.broadcast_to(x[None], (n,) + x.shape), axes, 0, 0, tiled=True)


def slot_loop(count, wait_chunk, one_slot):
    per_chunk = SLOTS // T_CHUNKS
    for chunk in range(T_CHUNKS):
        wait_chunk(chunk)
        left = jnp.clip(count - chunk * per_chunk, 0, per_chunk)

        def step(i, carry, base=chunk * per_chunk):
            for u in range(UNROLL):
                one_slot(base + i * UNROLL + u)
            return carry

        lax.fori_loop(0, (left + UNROLL - 1) // UNROLL, step, 0)


def tile_copies(tiles_hbm, tiles, sems, first):
    per_chunk = SLOTS // T_CHUNKS
    return [
        pltpu.make_async_copy(
            tiles_hbm.at[pl.ds(c * per_chunk, per_chunk)],
            tiles.at[pl.ds(c * per_chunk, per_chunk)],
            sems.at[first + c],
        )
        for c in range(T_CHUNKS)
    ]


def forward_kernel(rows, slots, count, tiles_hbm, p00, p01, p10, p11, q0, q1, out, x, tiles, acc, sems):
    copies = []
    for v, src in enumerate((p00, p01, p10, p11)):
        copies.append(pltpu.make_async_copy(src, x.at[pl.ds(v * N_Z, N_Z), pl.ds(0, PA)], sems.at[v]))
    for dc, src in enumerate((q0, q1)):
        for dx in range(2):
            v = 2 * dx + dc
            copies.append(
                pltpu.make_async_copy(
                    src.at[:, pl.ds(dx * QA, QA)], x.at[pl.ds(v * N_Z, N_Z), pl.ds(PA, QA)], sems.at[4 + v]
                )
            )
    tile_in = tile_copies(tiles_hbm, tiles, sems, 8)
    for c in copies:
        c.start()
    for c in tile_in:
        c.start()
    acc[...] = jnp.zeros_like(acc)
    for c in copies:
        c.wait()

    def one_slot(t):
        s = slots[t]
        row = rows[t]
        feats = x[s >> 1, pl.ds(pl.multiple_of((s & 1) * TILE, TILE), TILE), :]
        acc[row] += jnp.dot(tiles[t], feats, preferred_element_type=f32)

    slot_loop(count[0], lambda c: tile_in[c].wait(), one_slot)
    for r in range(N_REP):
        for h in range(2):
            out[r, pl.ds(h * TILE, TILE), :] = acc[2 * r + h].astype(bf16)


def backward_kernel(rows, slots, count, tiles_hbm, grads_hbm, p00, p01, p10, p11, q0, q1, grads, tiles, acc, sems):
    grads_in = pltpu.make_async_copy(grads_hbm.at[:, pl.ds(0, XR)], grads, sems.at[0])
    tile_in = tile_copies(tiles_hbm, tiles, sems, 1)
    grads_in.start()
    for c in tile_in:
        c.start()
    acc[...] = jnp.zeros_like(acc)
    grads_in.wait()

    def one_slot(t):
        s = slots[t]
        row = rows[t]
        here = (s >> 1, pl.ds(pl.multiple_of((s & 1) * TILE, TILE), TILE))
        g = grads[row >> 1, pl.ds(pl.multiple_of((row & 1) * TILE, TILE), TILE), :]
        acc[here[0], here[1], :] += lax.dot_general(
            tiles[t], g, (((0,), (0,)), ((), ())), preferred_element_type=f32
        )

    slot_loop(count[0], lambda c: tile_in[c].wait(), one_slot)
    for v, out in enumerate((p00, p01, p10, p11)):
        for z in range(N_Z):
            out[z] = acc[v * N_Z + z, pl.ds(0, PD), :].astype(bf16)
    for dc, out in enumerate((q0, q1)):
        for dx in range(2):
            for z in range(N_Z):
                out[z, pl.ds(dx * QD, QD), :] = acc[(2 * dx + dc) * N_Z + z, pl.ds(PD, QD), :].astype(bf16)


def dense_kernel(parts, weight, cot, layer_out, payload):
    total = parts[0].astype(f32)
    for r in range(1, N_REP):
        total += parts[r].astype(f32)
    hidden = total.astype(bf16)
    w = weight[...]
    preact = jnp.dot(hidden, w, preferred_element_type=f32)
    gating = jax.nn.sigmoid(preact)
    layer_out[...] = (preact * gating).astype(bf16)
    slope = gating * (1.0 + preact * (1.0 - gating))
    grad_pre = (cot[...].astype(f32) * slope).astype(bf16)
    grad_hidden = lax.dot_general(grad_pre, w, (((1,), (1,)), ((), ())), preferred_element_type=f32).astype(bf16)
    weight_part = lax.dot_general(hidden, grad_pre, (((0,), (0,)), ((), ())), preferred_element_type=f32).astype(bf16)
    for r in range(N_REP):
        payload[r, pl.ds(0, XR), :] = grad_hidden
        payload[r, pl.ds(XR, WROWS), :] = weight_part[r * WROWS : (r + 1) * WROWS]


def on_device(node_features, tile_values, tile_row, tile_col, tile_count, weight, cotangent):
    sds = jax.ShapeDtypeStruct
    smem = pl.BlockSpec(memory_space=pltpu.SMEM)
    hbm = pl.BlockSpec(memory_space=pl.ANY)
    params = pltpu.CompilerParams(vmem_limit_bytes=VMEM_LIMIT)
    tiles = tile_values[0, 0]
    count = tile_count[0]
    cols = tile_col[0, 0]
    my_xl = lax.axis_index("xl")
    my_core = lax.axis_index("core")
    owner = cols >> 1
    variant = 2 * (((owner >> 1) & 1) ^ my_xl) + ((owner & 1) ^ my_core)
    slots = ((variant * N_Z + (owner >> 2)) << 1) | (cols & 1)
    live = jnp.arange(SLOTS, dtype=jnp.int32) < count[0]
    rows_fwd = jnp.where(live, tile_row[0, 0], ROW_BLOCKS)
    slots_bwd = jnp.where(live, slots, 8 * N_Z)

    own_p = node_features[:PA]
    own_q = node_features[PA:]
    with jax.named_scope("gather_features"):
        other_q = pair_swap(own_q, "xl")
        p00 = spread(own_p, "z", N_Z)
        q0 = spread(jnp.concatenate([own_q, other_q], axis=0), "z", N_Z)
        p10 = pair_swap(p00, "xl")
        p01 = pair_swap(p00, "core")
        q1 = pair_swap(q0, "core")
        p11 = pair_swap(p10, "core")
    with jax.named_scope("tile_products"):
        partial = pl.pallas_call(
            forward_kernel,
            out_shape=sds((N_REP, XR, F), bf16),
            in_specs=[smem, smem, smem] + [hbm] * 7,
            scratch_shapes=[
                pltpu.VMEM((4 * N_Z, XR, F), bf16),
                pltpu.VMEM((SLOTS, TILE, TILE), bf16),
                pltpu.VMEM((ROW_BLOCKS + 1, TILE, F), f32),
                pltpu.SemaphoreType.DMA((8 + T_CHUNKS,)),
            ],
            compiler_params=params,
            name="tile_products",
        )(rows_fwd, slots, count, tiles, p00, p01, p10, p11, q0, q1)
    with jax.named_scope("sum_partials"):
        parts = lax.all_to_all(partial, REP, 0, 0, tiled=True)
    with jax.named_scope("dense"):
        layer_out, payload = pl.pallas_call(
            dense_kernel,
            out_shape=(sds((XR, F), bf16), sds((N_REP, XR + WROWS, F), bf16)),
            compiler_params=params,
            name="dense",
        )(parts, weight, cotangent[0, 0])
    with jax.named_scope("share_gradients"):
        grads = lax.all_to_all(payload, REP, 0, 0, tiled=True)
    with jax.named_scope("weight_sum"):
        w = jnp.sum(grads[:, XR:, :].astype(f32), axis=0)
        w = w + pair_swap(w, "core")
        w = w + pair_swap(w, "xl")
    with jax.named_scope("tile_products_back"):
        p00, p01, p10, p11, q0, q1 = pl.pallas_call(
            backward_kernel,
            out_shape=[sds((N_Z, PD, F), bf16)] * 4 + [sds((N_Z, 2 * QD, F), bf16)] * 2,
            in_specs=[smem, smem, smem] + [hbm] * 2,
            scratch_shapes=[
                pltpu.VMEM((N_REP, XR, F), bf16),
                pltpu.VMEM((SLOTS, TILE, TILE), bf16),
                pltpu.VMEM((4 * N_Z + 1, XR, F), f32),
                pltpu.SemaphoreType.DMA((1 + T_CHUNKS,)),
            ],
            compiler_params=params,
            name="tile_products_back",
        )(tile_row[0, 0], slots_bwd, count, tiles, grads)
    with jax.named_scope("scatter_gradients"):
        r10 = pair_swap(p11, "core")
        rq = pair_swap(q1, "core")
        r00 = pair_swap(p01, "core")
        far = pair_swap((p10.astype(f32) + r10.astype(f32)).astype(bf16), "xl")
        qz = lax.all_to_all((q0.astype(f32) + rq.astype(f32)).astype(bf16), "z", 0, 0, tiled=True)
        near = (p00.astype(f32) + r00.astype(f32) + far.astype(f32)).astype(bf16)
        pz = lax.all_to_all(near, "z", 0, 0, tiled=True)
        q_sum = jnp.sum(qz.astype(f32), axis=0)
        q_far = pair_swap(q_sum[QD:].astype(bf16), "xl")
        q_out = (q_sum[:QD] + q_far.astype(f32)).astype(bf16)
        p_out = jnp.sum(pz.astype(f32), axis=0).astype(bf16)
        grad_features = jnp.concatenate([p_out, q_out], axis=0)
    with jax.named_scope("weight_sum"):
        w = jnp.sum(spread(w, "z", N_Z), axis=0)
        grad_weight = spread(w, REP, N_REP).reshape(F, F)
    return layer_out.reshape(1, 1, XR, F), grad_weight, grad_features


def solution(mesh):
    fine = Mesh(np.asarray(mesh.devices).reshape(4, 2, 8, 2, 2), REP + BLK)
    placed = (
        P(REP + BLK, None),
        P(REP, BLK, None, None, None),
        P(REP, BLK, None),
        P(REP, BLK, None),
        P(REP, BLK),
        P(),
        P(BLK, REP, None, None),
    )
    return jax.shard_map(
        on_device,
        mesh=fine,
        in_specs=placed,
        out_specs=(P(BLK, REP, None, None), P(), P(REP + BLK, None)),
        check_vma=False,
    )
```

time: 639 us -> 223 us (0.35)
  waiting for transfers between devices: 536 us -> 91.6 us
  blocking collectives: 0 us -> 52.1 us
  starting transfers between devices: 0.38 us -> 52.1 us
  local copies, waits for them, and re-layouts: 48.8 us -> 6.81 us
  matrix products: 34.7 us -> 0 us
  Pallas kernels: 0 us -> 13.4 us
  between operations: 14.5 us -> 1.47 us
    psum x1 -> x0, waiting for transfers between devices: 218 us -> none  [on_device(): grad_weight = lax.psum(weight_part, ('rep', 'blk'))]
    reduce_scatter x2 -> x0, waiting for transfers between devices: 197 us -> none  [the longest x1 123 us: on_device(): lax.psum_scatter(column_terms, 'blk', scatter_dimension=0, tiled=True)]
    all_gather x2 -> x0, waiting for transfers between devices: 121 us -> none  [the longest x1 71 us: on_device(): gathered = lax.all_gather(node_features, 'blk', axis=0, tiled=True)]
    all_to_all x0 -> x6, waiting for transfers between devices: none -> 53.9 us  [the longest x4 36.3 us: spread(): lax.all_to_all(jnp.broadcast_to(x[None], (n,) + x.shape), axes, 0, 0, til...]
    all_to_all x0 -> x2, blocking collectives: none -> 52.1 us  [the longest x1 29.1 us: on_device(): parts = lax.all_to_all(partial, REP, 0, 0, tiled=True)]
    all_to_all x0 -> x6, starting transfers between devices: none -> 38 us  [the longest x4 27.7 us: spread(): lax.all_to_all(jnp.broadcast_to(x[None], (n,) + x.shape), axes, 0, 0, til...]
    ppermute x0 -> x12, waiting for transfers between devices: none -> 37.8 us  [pair_swap(): return lax.ppermute(x, axis, [(0, 1), (1, 0)])]
    dot_general x7 -> x0, matrix products: 34.7 us -> none  [the longest x1 11.9 us: on_device(): jnp.einsum('tij,tjf->tif', tile_block, picked, preferred_element_type=jnp...]
  transfers between devices with their start and end apart: 5 -> 18, of which waited for: 5 -> 13; matrix products, arithmetic and copies ran while one was open for 7% -> 3% of each run, Pallas kernels for 0% -> 0%
where the time goes in v1:
time: 223 us
  waiting for transfers between devices  91.6 us (41%)
  starting transfers between devices  52.1 us (23%)
  blocking collectives  52.1 us (23%)
  Pallas kernels  13.4 us (6%)
  local copies, waits for them, and re-layouts  6.81 us (3%)
  other arithmetic  5.33 us (2%)
    ppermute x12, waiting for transfers between devices, pair_swap(): return lax.ppermute(x, axis, [(0, 1), (1, 0)])  37.8 us
    all_to_all x4, waiting for transfers between devices, spread(): lax.all_to_all(jnp.broadcast_to(x[None], (n,) + x.shape), axes, 0, 0, til...  36.3 us
    all_to_all x1, blocking collectives, on_device(): parts = lax.all_to_all(partial, REP, 0, 0, tiled=True)  29.1 us
    all_to_all x4, starting transfers between devices, spread(): lax.all_to_all(jnp.broadcast_to(x[None], (n,) + x.shape), axes, 0, 0, til...  27.7 us
    all_to_all x1, blocking collectives, on_device(): grads = lax.all_to_all(payload, REP, 0, 0, tiled=True)  22.9 us
    all_to_all x1, waiting for transfers between devices, on_device(): pz = lax.all_to_all(near, 'z', 0, 0, tiled=True)  17.6 us
    ppermute x12, starting transfers between devices, pair_swap(): return lax.ppermute(x, axis, [(0, 1), (1, 0)])  14.1 us
    all_to_all x1, starting transfers between devices, on_device(): pz = lax.all_to_all(near, 'z', 0, 0, tiled=True)  6.76 us
  transfers between devices with their start and end apart: 18, of which 13 were waited for; matrix products, arithmetic and copies ran while one was open for 3% of the time, Pallas kernels for 0%

profile of v1, /device:TPU:1, one launch (start us, length us, event | category | flops | bytes accessed | tf_op | source)
XLA Modules:
  0.0 222.8 jit_solution(11335773849938107822)
XLA Ops:
  2.4 9.0 %all-to-all-start = ((bf16[8,176,256]{2,1,0:T(8,128)(2,1)}), bf16[8,176,256]{2,1,0:T(8,128)(2,1)S(1)}, u32[]{:S(2)}, u32[]{:S(2)}) async-start(bf16[8,176,256]{2,1,0:T(8,128)(2,1)} %broadcast_in_dim.16), calls=%async_computation | async-start | bytes 1441792 | tf_op jit(solution)/shard_map/gather_features/all_to_all | solution.py:37
  12.3 1.2 collective-permute-start.3
  13.5 1.6 collective-permute-done.3
  15.1 18.5 %all-to-all-done.p00 = bf16[8,176,256]{2,1,0:T(8,128)(2,1)S(1)} async-done(((bf16[8,176,256]{2,1,0:T(8,128)(2,1)}), bf16[8,176,256]{2,1,0:T(8,128)(2,1)S(1)}, u32[]{:S(2)}, u32[]{:S(2)}) %all-to-all-start) | async-done | bytes 720928 | tf_op jit(solution)/shard_map/gather_features/all_to_all | solution.py:37
  34.6 3.5 %all-to-all-start.1 = ((bf16[8,160,256]{2,1,0:T(8,128)(2,1)}), bf16[8,160,256]{2,1,0:T(8,128)(2,1)S(1)}, u32[]{:S(2)}, u32[]{:S(2)}) async-start(bf16[8,160,256]{2,1,0:T(8,128)(2,1)} %broadcast_in_dim.17), calls=%async_computation.1 | async-start | bytes 1310720 | tf_op jit(solution)/shard_map/gather_features/all_to_all | solution.py:37
  38.1 1.3 collective-permute-start.1
  40.2 15.2 %collective-permute-done.1.p10 = bf16[8,176,256]{2,1,0:T(8,128)(2,1)S(1)} collective-permute-done((bf16[8,176,256]{2,1,0:T(8,128)(2,1)S(1)}, bf16[8,176,256]{2,1,0:T(8,128)(2,1)S(1)}, u32[]{:S(2)}, u32[]{:S(2)}) %collective-permute-start.1) | collective-permute-done | bytes 720928 | tf_op jit(solution)/shard_map/gather_features/ppermute | solution.py:33
  55.4 1.3 collective-permute-start.2
  56.8 2.0 all-to-all-done.1.q0
  62.3 5.3 %tile_products.1 = bf16[8,256,256]{2,1,0:T(8,128)(2,1)} custom-call(s32[128]{0:T(128)} %compare_select_fusion.1.rows, s32[128]{0:T(128)} %get-tuple-element.20.slots, s32[1]{0:T(128)} %bitcast.13.count, bf16[128,128,128]{2,1,0:T(8,128)(2,1)} %bitcast.15, bf16[8,176,256]{2,1,0:T(8,128)(2,1)} %copy-done, bf16[8,176,256]{2,1,0:T(8,128)(2,1)} %copy-done.4, ...), custom_call_target="tpu_custom_call" | custom-call | tf_op jit(solution)/shard_map/tile_products/tile_products/pallas_call | solution.py:173
  67.6 29.1 %all_to_all.40.parts = bf16[8,256,256]{2,1,0:T(8,128)(2,1)} all-to-all(bf16[8,256,256]{2,1,0:T(8,128)(2,1)} %tile_products.1), channel_id=1, replica_groups=mesh['y'=4,'xh'=2,'z'=8,'xl'=2,'core'=2] {'y','xh'}, dimensions={0} | all-to-all | bytes 2097152 | tf_op jit(solution)/shard_map/sum_partials/all_to_all | solution.py:187
  96.7 2.8 %dense.1 = (bf16[256,256]{1,0:T(8,128)(2,1)}, bf16[8,288,256]{2,1,0:T(8,128)(2,1)}) custom-call(bf16[8,256,256]{2,1,0:T(8,128)(2,1)} %all_to_all.40.parts, bf16[256,256]{1,0:T(8,128)(2,1)} %weight.1, bf16[256,256]{1,0:T(8,128)(2,1)} %bitcast.18), custom_call_target="tpu_custom_call" | custom-call | tf_op jit(solution)/shard_map/dense/dense/pallas_call | solution.py:189
  99.4 22.9 %all_to_all.41.grads_hbm = bf16[8,288,256]{2,1,0:T(8,128)(2,1)} all-to-all(bf16[8,288,256]{2,1,0:T(8,128)(2,1)} %get-tuple-element.12), channel_id=1, replica_groups=mesh['y'=4,'xh'=2,'z'=8,'xl'=2,'core'=2] {'y','xh'}, dimensions={0} | all-to-all | bytes 2359296 | tf_op jit(solution)/shard_map/share_gradients/all_to_all | solution.py:196
  122.4 5.3 %tile_products_back.1 = (bf16[8,160,256]{2,1,0:T(8,128)(2,1)}, bf16[8,160,256]{2,1,0:T(8,128)(2,1)}, bf16[8,160,256]{2,1,0:T(8,128)(2,1)}, bf16[8,160,256]{2,1,0...) custom-call(s32[128]{0:T(128)} %bitcast.19, s32[128]{0:T(128)} %get-tuple-element.19.slots, ...), custom_call_target="tpu_custom_call" | custom-call | tf_op jit(solution)/shard_map/tile_products_back/tile_products_back/pallas_call | solution.py:202
  127.7 1.5 collective-permute-start.10
  130.4 1.1 collective-permute-done.5
  131.5 2.8 %collective-permute-done.6 = f32[32,256]{1,0:T(8,128)S(1)} collective-permute-done((f32[32,256]{1,0:T(8,128)S(1)}, f32[32,256]{1,0:T(8,128)S(1)}, u32[]{:S(2)}, u32[]{:S(2)}) %collective-permute-start.6) | collective-permute-done | bytes 32800 | tf_op jit(solution)/shard_map/weight_sum/ppermute | solution.py:33
  135.0 11.7 %all-to-all-start.4 = ((f32[8,32,256]{2,1,0:T(8,128)}), f32[8,32,256]{2,1,0:T(8,128)S(1)}, u32[]{:S(2)}, u32[]{:S(2)}) async-start(f32[8,32,256]{2,1,0:T(8,128)} %broadcast_in_dim.34), calls=%async_computation.4 | async-start | bytes 524288 | tf_op jit(solution)/shard_map/weight_sum/all_to_all | solution.py:37
  146.7 1.0 collective-permute-start.8
  147.7 9.2 %all-to-all-done.4 = f32[8,32,256]{2,1,0:T(8,128)S(1)} async-done(((f32[8,32,256]{2,1,0:T(8,128)}), f32[8,32,256]{2,1,0:T(8,128)S(1)}, u32[]{:S(2)}, u32[]{:S(2)}) %all-to-all-start.4) | async-done | bytes 262176 | tf_op jit(solution)/shard_map/weight_sum/all_to_all | solution.py:37
  157.6 3.4 %all-to-all-start.5 = ((f32[8,32,256]{2,1,0:T(8,128)}), f32[8,32,256]{2,1,0:T(8,128)S(1)}, u32[]{:S(2)}, u32[]{:S(2)}) async-start(f32[8,32,256]{2,1,0:T(8,128)} %broadcast_in_dim.35), calls=%async_computation.5 | async-start | bytes 524288 | tf_op jit(solution)/shard_map/weight_sum/all_to_all | solution.py:37
  161.1 1.1 add_convert_fusion
  162.1 6.6 %all-to-all-done.5 = f32[8,32,256]{2,1,0:T(8,128)S(1)} async-done(((f32[8,32,256]{2,1,0:T(8,128)}), f32[8,32,256]{2,1,0:T(8,128)S(1)}, u32[]{:S(2)}, u32[]{:S(2)}) %all-to-all-start.5) | async-done | bytes 262176 | tf_op jit(solution)/shard_map/weight_sum/all_to_all | solution.py:37
  168.7 3.5 %all-to-all-start.7 = ((bf16[8,192,256]{2,1,0:T(8,128)(2,1)}), bf16[8,192,256]{2,1,0:T(8,128)(2,1)S(1)}, u32[]{:S(2)}, u32[]{:S(2)}) async-start(bf16[8,192,256]{2,1,0:T(8,128)(2,1)} %add_convert_fusion), calls=%async_computation.7 | async-start | bytes 1572864 | tf_op jit(solution)/shard_map/scatter_gradients/all_to_all | solution.py:220
  172.3 3.8 %collective-permute-start.7 = (bf16[8,160,256]{2,1,0:T(8,128)(2,1)}, bf16[8,160,256]{2,1,0:T(8,128)(2,1)S(1)}, u32[]{:S(2)}, u32[]{:S(2)}) collective-permute-start(bf16[8,160,256]{2,1,0:T(8,128)(2,1)} %get-tuple-element.14), channel_id=1, source_target_pairs={{0,1},{1,0},{2,3},{3,2},{4,5},{5,4},{6,7},{7,6},{8,9},{9,8},{10,11... | collective-permute-start | bytes 1966088 | tf_op jit(solution)/shard_map/scatter_gradients/ppermute | solution.py:33
  176.3 1.2 collective-permute-start.9
  178.0 14.7 %collective-permute-done.9 = bf16[8,160,256]{2,1,0:T(8,128)(2,1)S(1)} collective-permute-done((bf16[8,160,256]{2,1,0:T(8,128)(2,1)S(1)}, bf16[8,160,256]{2,1,0:T(8,128)(2,1)S(1)}, u32[]{:S(2)}, u32[]{:S(2)}) %collective-permute-start.9) | collective-permute-done | bytes 655392 | tf_op jit(solution)/shard_map/scatter_gradients/ppermute | solution.py:33
  192.7 1.2 add_convert_fusion.1
  193.8 6.8 %all-to-all-start.6 = ((bf16[8,160,256]{2,1,0:T(8,128)(2,1)}), bf16[8,160,256]{2,1,0:T(8,128)(2,1)S(1)}, u32[]{:S(2)}, u32[]{:S(2)}) async-start(bf16[8,160,256]{2,1,0:T(8,128)(2,1)} %add_convert_fusion.1), calls=%async_computation.6 | async-start | bytes 1310720 | tf_op jit(solution)/shard_map/scatter_gradients/all_to_all | solution.py:222
  200.7 1.2 collective-permute-start.11
  202.0 1.8 collective-permute-done.11
  203.8 17.6 %all-to-all-done.6 = bf16[8,160,256]{2,1,0:T(8,128)(2,1)S(1)} async-done(((bf16[8,160,256]{2,1,0:T(8,128)(2,1)}), bf16[8,160,256]{2,1,0:T(8,128)(2,1)S(1)}, u32[]{:S(2)}, u32[]{:S(2)}) %all-to-all-start.6) | async-done | bytes 655392 | tf_op jit(solution)/shard_map/scatter_gradients/all_to_all | solution.py:222
  (51 shorter events, 12.0 us)
Async XLA Ops:
  2.4 31.2 %all-to-all-start = ((bf16[8,176,256]{2,1,0:T(8,128)(2,1)}), bf16[8,176,256]{2,1,0:T(8,128)(2,1)S(1)}, u32[]{:S(2)}, u32[]{:S(2)}) async-start(bf16[8,176,256]{2,1,0:T(8,128)(2,1)} %broadcast_in_dim.16), calls=%async_computation | async-start | bytes 1441792 | tf_op jit(solution)/shard_map/gather_features/all_to_all | solution.py:37
  11.4 48.5 %copy-start.8 = (s32[1,1,128]{2,1,0:T(1,128)S(1)}, s32[1,1,128]{2,1,0:T(1,128)}, u32[]{:S(2)}) copy-start(s32[1,1,128]{2,1,0:T(1,128)} %param.9) | copy-start | bytes 1540
  11.5 49.0 %copy-start.9 = (s32[1,1,128]{2,1,0:T(1,128)S(1)}, s32[1,1,128]{2,1,0:T(1,128)}, u32[]{:S(2)}) copy-start(s32[1,1,128]{2,1,0:T(1,128)} %param.10) | copy-start | bytes 1540
  12.3 2.9 %collective-permute-start.3 = (bf16[80,256]{1,0:T(8,128)(2,1)S(1)}, bf16[80,256]{1,0:T(8,128)(2,1)S(1)}, u32[]{:S(2)}, u32[]{:S(2)}) collective-permute-start(bf16[80,256]{1,0:T(8,128)(2,1)S(1)} %slice.17), channel_id=1, source_target_pairs={{0,2},{2,0},{1,3},{3,1},{4,6},{6,4},{5,7},{7,5},{8,10},{10,8},{9,1... | collective-permute-start | bytes 122888 | tf_op jit(solution)/shard_map/gather_features/ppermute | solution.py:33
  33.6 27.5 %copy-start = (bf16[8,176,256]{2,1,0:T(8,128)(2,1)}, bf16[8,176,256]{2,1,0:T(8,128)(2,1)S(1)}, u32[]{:S(2)}) copy-start(bf16[8,176,256]{2,1,0:T(8,128)(2,1)S(1)} %all-to-all-done.p00) | copy-start | bytes 2162692
  34.6 24.2 %all-to-all-start.1 = ((bf16[8,160,256]{2,1,0:T(8,128)(2,1)}), bf16[8,160,256]{2,1,0:T(8,128)(2,1)S(1)}, u32[]{:S(2)}, u32[]{:S(2)}) async-start(bf16[8,160,256]{2,1,0:T(8,128)(2,1)} %broadcast_in_dim.17), calls=%async_computation.1 | async-start | bytes 1310720 | tf_op jit(solution)/shard_map/gather_features/all_to_all | solution.py:37
  38.1 17.3 %collective-permute-start.1 = (bf16[8,176,256]{2,1,0:T(8,128)(2,1)S(1)}, bf16[8,176,256]{2,1,0:T(8,128)(2,1)S(1)}, u32[]{:S(2)}, u32[]{:S(2)}) collective-permute-start(bf16[8,176,256]{2,1,0:T(8,128)(2,1)S(1)} %all-to-all-done.p00), channel_id=1, source_target_pairs={{0,2},{2,0},{1,3},{3,1},{4,6},{6,4},{5,7},{7,5},{8,10},{10,8},{9,1... | collective-permute-start | bytes 2162696 | tf_op jit(solution)/shard_map/gather_features/ppermute | solution.py:33
  39.4 21.7 %collective-permute-start = (bf16[8,176,256]{2,1,0:T(8,128)(2,1)S(1)}, bf16[8,176,256]{2,1,0:T(8,128)(2,1)S(1)}, u32[]{:S(2)}, u32[]{:S(2)}) collective-permute-start(bf16[8,176,256]{2,1,0:T(8,128)(2,1)S(1)} %all-to-all-done.p00), channel_id=1, source_target_pairs={{0,1},{1,0},{2,3},{3,2},{4,5},{5,4},{6,7},{7,6},{8,9},{9,8},{10,11... | collective-permute-start | bytes 2162696 | tf_op jit(solution)/shard_map/gather_features/ppermute | solution.py:33
  55.4 5.8 %copy-start.3 = (bf16[8,176,256]{2,1,0:T(8,128)(2,1)}, bf16[8,176,256]{2,1,0:T(8,128)(2,1)S(1)}, u32[]{:S(2)}) copy-start(bf16[8,176,256]{2,1,0:T(8,128)(2,1)S(1)} %collective-permute-done.1.p10) | copy-start | bytes 2162692
  55.4 5.7 %collective-permute-start.2 = (bf16[8,176,256]{2,1,0:T(8,128)(2,1)S(1)}, bf16[8,176,256]{2,1,0:T(8,128)(2,1)S(1)}, u32[]{:S(2)}, u32[]{:S(2)}) collective-permute-start(bf16[8,176,256]{2,1,0:T(8,128)(2,1)S(1)} %collective-permute-done.1.p10), channel_id=1, source_target_pairs={{0,1},{1,0},{2,3},{3,2},{4,5},{5,4},{6,7},{7,6},{8,9},{9,8},{10,11... | collective-permute-start | bytes 2162696 | tf_op jit(solution)/shard_map/gather_features/ppermute | solution.py:33
  58.8 2.4 %copy-start.1 = (bf16[8,160,256]{2,1,0:T(8,128)(2,1)}, bf16[8,160,256]{2,1,0:T(8,128)(2,1)S(1)}, u32[]{:S(2)}) copy-start(bf16[8,160,256]{2,1,0:T(8,128)(2,1)S(1)} %all-to-all-done.1.q0) | copy-start | bytes 1966084
  58.8 2.3 %collective-permute-start.4 = (bf16[8,160,256]{2,1,0:T(8,128)(2,1)S(1)}, bf16[8,160,256]{2,1,0:T(8,128)(2,1)}, u32[]{:S(2)}, u32[]{:S(2)}) collective-permute-start(bf16[8,160,256]{2,1,0:T(8,128)(2,1)S(1)} %all-to-all-done.1.q0), channel_id=1, source_target_pairs={{0,1},{1,0},{2,3},{3,2},{4,5},{5,4},{6,7},{7,6},{8,9},{9,8},{10,11... | collective-permute-start | bytes 1966088 | tf_op jit(solution)/shard_map/gather_features/ppermute | solution.py:33
  61.1 0.9 copy-start.4
  61.2 1.1 copy-start.5
  127.7 33.3 %copy-start.2 = (bf16[8,192,256]{2,1,0:T(8,128)(2,1)S(1)}, bf16[8,192,256]{2,1,0:T(8,128)(2,1)}, u32[]{:S(2)}) copy-start(bf16[8,192,256]{2,1,0:T(8,128)(2,1)} %get-tuple-element.17) | copy-start | bytes 2359300
  127.7 33.3 %collective-permute-start.10 = (bf16[8,192,256]{2,1,0:T(8,128)(2,1)}, bf16[8,192,256]{2,1,0:T(8,128)(2,1)S(1)}, u32[]{:S(2)}, u32[]{:S(2)}) collective-permute-start(bf16[8,192,256]{2,1,0:T(8,128)(2,1)} %get-tuple-element.18), channel_id=1, source_target_pairs={{0,1},{1,0},{2,3},{3,2},{4,5},{5,4},{6,7},{7,6},{8,9},{9,8},{10,11... | collective-permute-start | bytes 2359304 | tf_op jit(solution)/shard_map/scatter_gradients/ppermute | solution.py:33
  130.2 1.3 collective-permute-start.5
  131.5 2.8 %collective-permute-start.6 = (f32[32,256]{1,0:T(8,128)S(1)}, f32[32,256]{1,0:T(8,128)S(1)}, u32[]{:S(2)}, u32[]{:S(2)}) collective-permute-start(f32[32,256]{1,0:T(8,128)S(1)} %add.29), channel_id=1, source_target_pairs={{0,2},{2,0},{1,3},{3,1},{4,6},{6,4},{5,7},{7,5},{8,10},{10,8},{9,1... | collective-permute-start | bytes 98312 | tf_op jit(solution)/shard_map/weight_sum/ppermute | solution.py:33
  135.0 21.9 %all-to-all-start.4 = ((f32[8,32,256]{2,1,0:T(8,128)}), f32[8,32,256]{2,1,0:T(8,128)S(1)}, u32[]{:S(2)}, u32[]{:S(2)}) async-start(f32[8,32,256]{2,1,0:T(8,128)} %broadcast_in_dim.34), calls=%async_computation.4 | async-start | bytes 524288 | tf_op jit(solution)/shard_map/weight_sum/all_to_all | solution.py:37
  146.7 29.4 %collective-permute-start.8 = (bf16[8,160,256]{2,1,0:T(8,128)(2,1)}, bf16[8,160,256]{2,1,0:T(8,128)(2,1)S(1)}, u32[]{:S(2)}, u32[]{:S(2)}) collective-permute-start(bf16[8,160,256]{2,1,0:T(8,128)(2,1)} %get-tuple-element.16), channel_id=1, source_target_pairs={{0,1},{1,0},{2,3},{3,2},{4,5},{5,4},{6,7},{7,6},{8,9},{9,8},{10,11... | collective-permute-start | bytes 1966088 | tf_op jit(solution)/shard_map/scatter_gradients/ppermute | solution.py:33
  157.6 11.1 %all-to-all-start.5 = ((f32[8,32,256]{2,1,0:T(8,128)}), f32[8,32,256]{2,1,0:T(8,128)S(1)}, u32[]{:S(2)}, u32[]{:S(2)}) async-start(f32[8,32,256]{2,1,0:T(8,128)} %broadcast_in_dim.35), calls=%async_computation.5 | async-start | bytes 524288 | tf_op jit(solution)/shard_map/weight_sum/all_to_all | solution.py:37
  162.1 13.9 %copy-start.7 = (bf16[8,160,256]{2,1,0:T(8,128)(2,1)S(1)}, bf16[8,160,256]{2,1,0:T(8,128)(2,1)}, u32[]{:S(2)}) copy-start(bf16[8,160,256]{2,1,0:T(8,128)(2,1)} %get-tuple-element.15) | copy-start | bytes 1966084
  168.7 25.1 %all-to-all-start.7 = ((bf16[8,192,256]{2,1,0:T(8,128)(2,1)}), bf16[8,192,256]{2,1,0:T(8,128)(2,1)S(1)}, u32[]{:S(2)}, u32[]{:S(2)}) async-start(bf16[8,192,256]{2,1,0:T(8,128)(2,1)} %add_convert_fusion), calls=%async_computation.7 | async-start | bytes 1572864 | tf_op jit(solution)/shard_map/scatter_gradients/all_to_all | solution.py:220
  172.3 20.4 %copy-start.6 = (bf16[8,160,256]{2,1,0:T(8,128)(2,1)S(1)}, bf16[8,160,256]{2,1,0:T(8,128)(2,1)}, u32[]{:S(2)}) copy-start(bf16[8,160,256]{2,1,0:T(8,128)(2,1)} %get-tuple-element.13) | copy-start | bytes 1966084
  172.3 5.7 %collective-permute-start.7 = (bf16[8,160,256]{2,1,0:T(8,128)(2,1)}, bf16[8,160,256]{2,1,0:T(8,128)(2,1)S(1)}, u32[]{:S(2)}, u32[]{:S(2)}) collective-permute-start(bf16[8,160,256]{2,1,0:T(8,128)(2,1)} %get-tuple-element.14), channel_id=1, source_target_pairs={{0,1},{1,0},{2,3},{3,2},{4,5},{5,4},{6,7},{7,6},{8,9},{9,8},{10,11... | collective-permute-start | bytes 1966088 | tf_op jit(solution)/shard_map/scatter_gradients/ppermute | solution.py:33
  176.3 16.4 %collective-permute-start.9 = (bf16[8,160,256]{2,1,0:T(8,128)(2,1)S(1)}, bf16[8,160,256]{2,1,0:T(8,128)(2,1)S(1)}, u32[]{:S(2)}, u32[]{:S(2)}) collective-permute-start(bf16[8,160,256]{2,1,0:T(8,128)(2,1)S(1)} %add_convert_fusion.2), channel_id=1, source_target_pairs={{0,2},{2,0},{1,3},{3,1},{4,6},{6,4},{5,7},{7,5},{8,10},{10,8},{9,1... | collective-permute-start | bytes 1966088 | tf_op jit(solution)/shard_map/scatter_gradients/ppermute | solution.py:33
  193.8 27.5 %all-to-all-start.6 = ((bf16[8,160,256]{2,1,0:T(8,128)(2,1)}), bf16[8,160,256]{2,1,0:T(8,128)(2,1)S(1)}, u32[]{:S(2)}, u32[]{:S(2)}) async-start(bf16[8,160,256]{2,1,0:T(8,128)(2,1)} %add_convert_fusion.1), calls=%async_computation.6 | async-start | bytes 1310720 | tf_op jit(solution)/shard_map/scatter_gradients/all_to_all | solution.py:222
  200.7 3.0 %collective-permute-start.11 = (bf16[96,256]{1,0:T(8,128)(2,1)S(1)}, bf16[96,256]{1,0:T(8,128)(2,1)S(1)}, u32[]{:S(2)}, u32[]{:S(2)}) collective-permute-start(bf16[96,256]{1,0:T(8,128)(2,1)S(1)} %slice.29), channel_id=1, source_target_pairs={{0,2},{2,0},{1,3},{3,1},{4,6},{6,4},{5,7},{7,5},{8,10},{10,8},{9,1... | collective-permute-start | bytes 147464 | tf_op jit(solution)/shard_map/scatter_gradients/ppermute | solution.py:33

commit v2 on v0

v2 whole, which is shorter than its diff:
```python
import jax
import jax.numpy as jnp
import numpy as np
from jax import lax
from jax.experimental import pallas as pl
from jax.experimental.pallas import tpu as pltpu
from jax.sharding import Mesh
from jax.sharding import PartitionSpec as P

REP = ("y", "xh")
BLK = ("z", "xl", "core")
PLANE = ("z", "xl")
N_PLANE = 16
N_Z = 8
N_Y = 4
TILE = 128
F = 256
XR = 256
N_REP = 8
SLOTS = 128
ROW_BLOCKS = 16
WROWS = F // N_REP
UNROLL = 4

f32 = jnp.float32
bf16 = jnp.bfloat16
VMEM_LIMIT = 24 << 20


def xor_swap(x, axis, n, bit):
    return lax.ppermute(x, axis, [(i, i ^ bit) for i in range(n)])


def half(ref, i):
    return ref[i >> 1, pl.ds(pl.multiple_of((i & 1) * TILE, TILE), TILE), :]


def slot_loop(table, side, one_slot):
    live = table[6, side]

    def step(i, carry):
        for u in range(UNROLL):
            t = i * UNROLL + u
            one_slot(t < live, table[3 * side, t], table[3 * side + 1, t], table[3 * side + 2, t])
        return carry

    lax.fori_loop(0, (live + UNROLL - 1) // UNROLL, step, 0)


def add_products(table, side, tiles, feats, acc):
    acc[...] = jnp.zeros_like(acc)

    def one_slot(ok, row, place, tile):
        r = jnp.where(ok, row, ROW_BLOCKS)
        acc[r] += jnp.dot(tiles[tile], half(feats, place), preferred_element_type=f32)

    slot_loop(table, side, one_slot)


def forward_near_kernel(table, tiles, feats, acc):
    add_products(table, 0, tiles, feats, acc)


def forward_far_kernel(table, tiles, feats, near, out, acc):
    add_products(table, 1, tiles, feats, acc)
    for r in range(N_REP):
        for h in range(2):
            out[r, pl.ds(h * TILE, TILE), :] = (near[2 * r + h] + acc[2 * r + h]).astype(bf16)


def backward_kernel(side, table, tiles, grads, out, acc):
    acc[...] = jnp.zeros_like(acc)

    def one_slot(ok, row, place, tile):
        p = jnp.where(ok, place, 2 * N_PLANE)
        acc[p] += lax.dot_general(
            tiles[tile], half(grads, row), (((0,), (0,)), ((), ())), preferred_element_type=f32
        )

    slot_loop(table, side, one_slot)
    for k in range(N_PLANE):
        for h in range(2):
            out[k, pl.ds(h * TILE, TILE), :] = acc[2 * k + h].astype(bf16)


def dense_kernel(parts, weight, cot, layer_out, payload):
    total = parts[0].astype(f32)
    for r in range(1, N_REP):
        total += parts[r].astype(f32)
    hidden = total.astype(bf16)
    w = weight[...]
    preact = jnp.dot(hidden, w, preferred_element_type=f32)
    gating = jax.nn.sigmoid(preact)
    layer_out[...] = (preact * gating).astype(bf16)
    slope = gating * (1.0 + preact * (1.0 - gating))
    grad_pre = (cot[...].astype(f32) * slope).astype(bf16)
    grad_hidden = lax.dot_general(grad_pre, w, (((1,), (1,)), ((), ())), preferred_element_type=f32).astype(bf16)
    weight_part = lax.dot_general(hidden, grad_pre, (((0,), (0,)), ((), ())), preferred_element_type=f32).astype(bf16)
    for r in range(N_REP):
        payload[r, pl.ds(0, XR), :] = grad_hidden
        payload[r, pl.ds(XR, WROWS), :] = weight_part[r * WROWS : (r + 1) * WROWS]


def slot_table(rows, cols, count, my_core):
    owner = cols >> 1
    place = ((owner >> 1) << 1) | (cols & 1)
    position = jnp.arange(SLOTS, dtype=jnp.int32)
    live = position < count
    far = (owner & 1) != my_core
    lists = []
    totals = []
    for side in (live & ~far, live & far):
        rank = jnp.cumsum(side.astype(jnp.int32)) - 1
        pick = (side[None, :] & (rank[None, :] == position[:, None])).astype(jnp.int32)
        for values in (rows, place, position):
            lists.append(jnp.sum(pick * values[None, :], axis=1))
        totals.append(jnp.sum(side.astype(jnp.int32)))
    last = jnp.where(position == 0, totals[0], jnp.where(position == 1, totals[1], 0))
    return jnp.stack(lists + [last, jnp.zeros_like(last)])


def on_device(node_features, tile_values, tile_row, tile_col, tile_count, weight, cotangent):
    sds = jax.ShapeDtypeStruct
    smem = pl.BlockSpec(memory_space=pltpu.SMEM)
    vmem = pl.BlockSpec(memory_space=pltpu.VMEM)
    params = pltpu.CompilerParams(vmem_limit_bytes=VMEM_LIMIT)
    tiles = tile_values[0, 0]
    my_core = lax.axis_index("core")

    with jax.named_scope("slot_table"):
        table = slot_table(tile_row[0, 0], tile_col[0, 0], tile_count[0, 0], my_core)
    with jax.named_scope("gather_features"):
        near_feats = lax.all_to_all(
            jnp.broadcast_to(node_features[None], (N_PLANE, XR, F)), PLANE, 0, 0, tiled=True
        )
        near_feats, table = lax.optimization_barrier((near_feats, table))
        far_feats = xor_swap(near_feats, "core", 2, 1)
    with jax.named_scope("tile_products"):
        near = pl.pallas_call(
            forward_near_kernel,
            out_shape=sds((ROW_BLOCKS + 1, TILE, F), f32),
            in_specs=[smem, vmem, vmem],
            out_specs=vmem,
            compiler_params=params,
            name="tile_products_near",
        )(table, tiles, near_feats)
        partial = pl.pallas_call(
            forward_far_kernel,
            out_shape=sds((N_REP, XR, F), bf16),
            in_specs=[smem, vmem, vmem, vmem],
            out_specs=vmem,
            scratch_shapes=[pltpu.VMEM((ROW_BLOCKS + 1, TILE, F), f32)],
            compiler_params=params,
            name="tile_products_far",
        )(table, tiles, far_feats, near)
    with jax.named_scope("sum_partials"):
        parts = lax.all_to_all(partial, REP, 0, 0, tiled=True)
    with jax.named_scope("dense"):
        layer_out, payload = pl.pallas_call(
            dense_kernel,
            out_shape=(sds((XR, F), bf16), sds((N_REP, XR + WROWS, F), bf16)),
            in_specs=[vmem] * 3,
            out_specs=[vmem] * 2,
            compiler_params=params,
            name="dense",
        )(parts, weight, cotangent[0, 0])
    with jax.named_scope("share_gradients"):
        grads = lax.all_to_all(payload, REP, 0, 0, tiled=True)

    def backward(side, name):
        return pl.pallas_call(
            lambda *refs: backward_kernel(side, *refs),
            out_shape=sds((N_PLANE, XR, F), bf16),
            in_specs=[smem, vmem, vmem],
            out_specs=vmem,
            scratch_shapes=[pltpu.VMEM((2 * N_PLANE + 1, TILE, F), f32)],
            compiler_params=params,
            name=name,
        )(table, tiles, grads)

    with jax.named_scope("tile_products_back"):
        far_back = backward(1, "tile_products_back_far")
        from_core = xor_swap(far_back, "core", 2, 1)
        near_back = backward(0, "tile_products_back_near")
        back = (near_back.astype(f32) + from_core.astype(f32)).astype(bf16)
    with jax.named_scope("scatter_gradients"):
        returned = lax.all_to_all(back, PLANE, 0, 0, tiled=True)
        grad_features = jnp.sum(returned.astype(f32), axis=0).astype(bf16)
    with jax.named_scope("weight_sum"):
        terms, _ = lax.optimization_barrier((grads[:, XR:, :], back))
        w = jnp.sum(terms.astype(f32), axis=0)
        w = w + xor_swap(w, "core", 2, 1)
        w = w + xor_swap(w, "xl", 2, 1)
        for bit in (1, 2, 4):
            w = w + xor_swap(w, "z", N_Z, bit)
        for axis, n, bit in (("xh", 2, 1), ("y", N_Y, 1), ("y", N_Y, 2)):
            other = xor_swap(w, axis, n, bit)
            upper = (lax.axis_index(axis) & bit) != 0
            w = jnp.where(upper, jnp.concatenate([other, w], axis=0), jnp.concatenate([w, other], axis=0))
    return layer_out.reshape(1, 1, XR, F), w, grad_features


def solution(mesh):
    fine = Mesh(np.asarray(mesh.devices).reshape(N_Y, 2, N_Z, 2, 2), REP + BLK)
    placed = (
        P(REP + BLK, None),
        P(REP, BLK, None, None, None),
        P(REP, BLK, None),
        P(REP, BLK, None),
        P(REP, BLK),
        P(),
        P(BLK, REP, None, None),
    )
    return jax.shard_map(
        on_device,
        mesh=fine,
        in_specs=placed,
        out_specs=(P(BLK, REP, None, None), P(), P(REP + BLK, None)),
        check_vma=False,
    )
```

time: 639 us -> 218 us (0.34)
  the two profiles are of different devices: /device:TPU:1 before, /device:TPU:2 now
where the time goes in v2:
time: 218 us; the launch traced here: 219 us
  waiting for transfers between devices  115 us (53%)
  blocking collectives  47.7 us (22%)
  starting transfers between devices  33.2 us (15%)
  Pallas kernels  9.26 us (4%)
  other arithmetic  6.97 us (3%)
  local copies, waits for them, and re-layouts  4.94 us (2%)
    ppermute x10, waiting for transfers between devices, xor_swap(): return lax.ppermute(x, axis, [(i, i ^ bit) for i in range(n)])  70.2 us
    all_to_all x1, waiting for transfers between devices, on_device(): lax.all_to_all(jnp.broadcast_to(node_features[None], (N_PLANE, XR, F)), P...  45 us
    all_to_all x1, blocking collectives, on_device(): parts = lax.all_to_all(partial, REP, 0, 0, tiled=True)  26.2 us
    all_to_all x1, blocking collectives, on_device(): grads = lax.all_to_all(payload, REP, 0, 0, tiled=True)  21.5 us
    all_to_all x1, starting transfers between devices, on_device(): returned = lax.all_to_all(back, PLANE, 0, 0, tiled=True)  12.8 us
    ppermute x10, starting transfers between devices, xor_swap(): return lax.ppermute(x, axis, [(i, i ^ bit) for i in range(n)])  10.4 us
    all_to_all x1, starting transfers between devices, on_device(): lax.all_to_all(jnp.broadcast_to(node_features[None], (N_PLANE, XR, F)), P...  10.1 us
    pallas_call x2, Pallas kernels, backward(): pl.pallas_call(lambda *refs: backward_kernel(side, *refs), out_shape=sds(...  4.56 us
  transfers between devices with their start and end apart: 12, of which 11 were waited for; matrix products, arithmetic and copies ran while one was open for 2% of the time, Pallas kernels for 2%

profile of v2, /device:TPU:2, one launch (start us, length us, event | category | flops | bytes accessed | tf_op | source)
XLA Modules:
  0.0 218.8 jit_solution(14782734864260040579)
XLA Ops:
  0.6 2.5 %broadcast_in_dim.9 = bf16[16,256,256]{2,1,0:T(8,128)(2,1)} broadcast(bf16[256,256]{1,0:T(8,128)(2,1)} %param.7), dimensions={1,2} | broadcast | bytes 2228224 | tf_op jit(solution)/shard_map/gather_features/broadcast_in_dim | solution.py:134
  3.1 10.1 %all-to-all-start = ((bf16[16,256,256]{2,1,0:T(8,128)(2,1)}), bf16[16,256,256]{2,1,0:T(8,128)(2,1)S(1)}, u32[]{:S(2)}, u32[]{:S(2)}) async-start(bf16[16,256,256]{2,1,0:T(8,128)(2,1)} %broadcast_in_dim.9), calls=%async_computation | async-start | bytes 4194304 | tf_op jit(solution)/shard_map/gather_features/all_to_all | solution.py:133
  13.8 0.6 convert_reduce_fusion.2
  15.0 0.6 convert_reduce_fusion.1
  15.7 1.3 compare_select_fusion.1
  17.3 45.0 %all-to-all-done.feats = bf16[16,256,256]{2,1,0:T(8,128)(2,1)S(1)} async-done(((bf16[16,256,256]{2,1,0:T(8,128)(2,1)}), bf16[16,256,256]{2,1,0:T(8,128)(2,1)S(1)}, u32[]{:S(2)}, u32[]{:S(2)}) %all-to-all-start) | async-done | bytes 2097184 | tf_op jit(solution)/shard_map/gather_features/all_to_all | solution.py:133
  62.4 2.2 copy-done
  64.5 1.7 tile_products_near.1.near
  66.2 0.3 collective-permute-done.feats
  66.5 2.1 tile_products_far.1
  68.6 26.2 %all_to_all.20.parts = bf16[8,256,256]{2,1,0:T(8,128)(2,1)S(1)} all-to-all(bf16[8,256,256]{2,1,0:T(8,128)(2,1)S(1)} %tile_products_far.1), channel_id=1, replica_groups=mesh['y'=4,'xh'=2,'z'=8,'xl'=2,'core'=2] {'y','xh'}, dimensions={0} | all-to-all | bytes 2097152 | tf_op jit(solution)/shard_map/sum_partials/all_to_all | solution.py:157
  94.9 0.9 dense.1
  95.8 21.5 %all_to_all.21.refs_2_ = bf16[8,288,256]{2,1,0:T(8,128)(2,1)S(1)} all-to-all(bf16[8,288,256]{2,1,0:T(8,128)(2,1)S(1)} %get-tuple-element.11), channel_id=1, replica_groups=mesh['y'=4,'xh'=2,'z'=8,'xl'=2,'core'=2] {'y','xh'}, dimensions={0} | all-to-all | bytes 2359296 | tf_op jit(solution)/shard_map/share_gradients/all_to_all | solution.py:168
  117.2 2.4 %tile_products_back_far.1 = bf16[16,256,256]{2,1,0:T(8,128)(2,1)S(1)} custom-call(s32[8,128]{1,0:T(8,128)S(1)} %stack.28.table.refs_0_, bf16[128,128,128]{2,1,0:T(8,128)(2,1)S(1)} %bitcast.34, bf16[8,288,256]{2,1,0:T(8,128)(2,1)S(1)} %all_to_all.21.refs_2_), custom_call_target="tpu_custom_call" | custom-call | tf_op jit(solution)/shard_map/tile_products_back/tile_products_back_far/pallas_call | solution.py:171
  119.8 2.1 tile_products_back_near.1
  121.9 2.0 collective-permute-done.1
  123.9 2.0 add_convert_fusion
  125.9 12.8 %all-to-all-start.3 = ((bf16[16,256,256]{2,1,0:T(8,128)(2,1)}), bf16[16,256,256]{2,1,0:T(8,128)(2,1)S(1)}, u32[]{:S(2)}, u32[]{:S(2)}) async-start(bf16[16,256,256]{2,1,0:T(8,128)(2,1)} %add_convert_fusion), calls=%async_computation.3 | async-start | bytes 4194304 | tf_op jit(solution)/shard_map/scatter_gradients/all_to_all | solution.py:187
  138.9 1.2 collective-permute-done.2
  140.2 3.8 %collective-permute-done.3 = f32[32,256]{1,0:T(8,128)S(1)} collective-permute-done((f32[32,256]{1,0:T(8,128)S(1)}, f32[32,256]{1,0:T(8,128)S(1)}, u32[]{:S(2)}, u32[]{:S(2)}) %collective-permute-start.3) | collective-permute-done | bytes 32800 | tf_op jit(solution)/shard_map/weight_sum/ppermute | solution.py:31
  144.0 1.5 collective-permute-start.4
  145.5 42.1 %collective-permute-done.4 = f32[32,256]{1,0:T(8,128)S(1)} collective-permute-done((f32[32,256]{1,0:T(8,128)S(1)}, f32[32,256]{1,0:T(8,128)S(1)}, u32[]{:S(2)}, u32[]{:S(2)}) %collective-permute-start.4) | collective-permute-done | bytes 32800 | tf_op jit(solution)/shard_map/weight_sum/ppermute | solution.py:31
  187.5 3.0 %collective-permute-start.5 = (f32[32,256]{1,0:T(8,128)S(1)}, f32[32,256]{1,0:T(8,128)S(1)}, u32[]{:S(2)}, u32[]{:S(2)}) collective-permute-start(f32[32,256]{1,0:T(8,128)S(1)} %add.33), channel_id=1, source_target_pairs={{0,8},{4,12},{8,0},{12,4},{16,24},{20,28},{24,16},{28,20},{1,9},{5... | collective-permute-start | bytes 98312 | tf_op jit(solution)/shard_map/weight_sum/ppermute | solution.py:31
  190.5 1.9 collective-permute-done.5
  192.4 4.9 %collective-permute-start.6 = (f32[32,256]{1,0:T(8,128)S(1)}, f32[32,256]{1,0:T(8,128)S(1)}, u32[]{:S(2)}, u32[]{:S(2)}) collective-permute-start(f32[32,256]{1,0:T(8,128)S(1)} %add.34), channel_id=1, source_target_pairs={{0,16},{4,20},{8,24},{12,28},{16,0},{20,4},{24,8},{28,12},{1,17},{... | collective-permute-start | bytes 98312 | tf_op jit(solution)/shard_map/weight_sum/ppermute | solution.py:31
  197.4 3.3 %collective-permute-done.6 = f32[32,256]{1,0:T(8,128)S(1)} collective-permute-done((f32[32,256]{1,0:T(8,128)S(1)}, f32[32,256]{1,0:T(8,128)S(1)}, u32[]{:S(2)}, u32[]{:S(2)}) %collective-permute-start.6) | collective-permute-done | bytes 32800 | tf_op jit(solution)/shard_map/weight_sum/ppermute | solution.py:31
  200.7 5.4 %collective-permute-done.7 = f32[32,256]{1,0:T(8,128)S(1)} collective-permute-done((f32[32,256]{1,0:T(8,128)S(1)}, f32[32,256]{1,0:T(8,128)S(1)}, u32[]{:S(2)}, u32[]{:S(2)}) %collective-permute-start.7) | collective-permute-done | bytes 32800 | tf_op jit(solution)/shard_map/weight_sum/ppermute | solution.py:31
  206.1 0.6 collective-permute-start.8
  206.7 3.8 %collective-permute-done.8 = f32[64,256]{1,0:T(8,128)S(1)} collective-permute-done((f32[64,256]{1,0:T(8,128)S(1)}, f32[64,256]{1,0:T(8,128)S(1)}, u32[]{:S(2)}, u32[]{:S(2)}) %collective-permute-start.8) | collective-permute-done | bytes 65568 | tf_op jit(solution)/shard_map/weight_sum/ppermute | solution.py:31
  210.6 6.5 %collective-permute-done.9 = f32[128,256]{1,0:T(8,128)S(1)} collective-permute-done((f32[128,256]{1,0:T(8,128)S(1)}, f32[128,256]{1,0:T(8,128)S(1)}, u32[]{:S(2)}, u32[]{:S(2)}) %collective-permute-start.9) | collective-permute-done | bytes 131104 | tf_op jit(solution)/shard_map/weight_sum/ppermute | solution.py:31
  217.1 0.7 maximum_select_fusion
  217.8 1.0 reduce_sum.102
  (37 shorter events, 1.4 us)
Async XLA Ops:
  3.1 10.7 %copy-start.5 = (s32[1,1,128]{2,1,0:T(1,128)S(1)}, s32[1,1,128]{2,1,0:T(1,128)}, u32[]{:S(2)}) copy-start(s32[1,1,128]{2,1,0:T(1,128)} %param.10) | copy-start | bytes 1540
  3.1 14.0 %copy-start.4 = (s32[1,1,128]{2,1,0:T(1,128)S(1)}, s32[1,1,128]{2,1,0:T(1,128)}, u32[]{:S(2)}) copy-start(s32[1,1,128]{2,1,0:T(1,128)} %param.9) | copy-start | bytes 1540
  3.1 59.3 %all-to-all-start = ((bf16[16,256,256]{2,1,0:T(8,128)(2,1)}), bf16[16,256,256]{2,1,0:T(8,128)(2,1)S(1)}, u32[]{:S(2)}, u32[]{:S(2)}) async-start(bf16[16,256,256]{2,1,0:T(8,128)(2,1)} %broadcast_in_dim.9), calls=%async_computation | async-start | bytes 4194304 | tf_op jit(solution)/shard_map/gather_features/all_to_all | solution.py:133
  62.4 4.2 %collective-permute-start = (bf16[16,256,256]{2,1,0:T(8,128)(2,1)S(1)}, bf16[16,256,256]{2,1,0:T(8,128)(2,1)S(1)}, u32[]{:S(2)}, u32[]{:S(2)}) collective-permute-start(bf16[16,256,256]{2,1,0:T(8,128)(2,1)S(1)} %all-to-all-done.feats), channel_id=1, source_target_pairs={{0,1},{1,0},{2,3},{3,2},{4,5},{5,4},{6,7},{7,6},{8,9},{9,8},{10,11... | collective-permute-start | bytes 6291464 | tf_op jit(solution)/shard_map/gather_features/ppermute | solution.py:31
  62.4 2.2 %copy-start = (bf16[1,1,128,128,128]{4,3,2,1,0:T(8,128)(2,1)S(1)}, bf16[1,1,128,128,128]{4,3,2,1,0:T(8,128)(2,1)}, u32[]{:S(2)}) copy-start(bf16[1,1,128,128,128]{4,3,2,1,0:T(8,128)(2,1)} %param.8) | copy-start | bytes 12582916
  66.5 28.3 %copy-start.2 = (bf16[256,256]{1,0:T(8,128)(2,1)S(1)}, bf16[256,256]{1,0:T(8,128)(2,1)}, u32[]{:S(2)}) copy-start(bf16[256,256]{1,0:T(8,128)(2,1)} %weight.1) | copy-start | bytes 393220
  66.5 28.3 %copy-start.3 = (bf16[1,1,256,256]{3,2,1,0:T(8,128)(2,1)S(1)}, bf16[1,1,256,256]{3,2,1,0:T(8,128)(2,1)}, u32[]{:S(2)}) copy-start(bf16[1,1,256,256]{3,2,1,0:T(8,128)(2,1)} %param.13) | copy-start | bytes 393220
  68.6 48.6 %copy-start.1 = (bf16[1,1,128,128,128]{4,3,2,1,0:T(8,128)(2,1)S(1)}, bf16[1,1,128,128,128]{4,3,2,1,0:T(8,128)(2,1)}, u32[]{:S(2)}) copy-start(bf16[1,1,128,128,128]{4,3,2,1,0:T(8,128)(2,1)} %param.8) | copy-start | bytes 12582916
  119.7 4.2 %collective-permute-start.1 = (bf16[16,256,256]{2,1,0:T(8,128)(2,1)S(1)}, bf16[16,256,256]{2,1,0:T(8,128)(2,1)S(1)}, u32[]{:S(2)}, u32[]{:S(2)}) collective-permute-start(bf16[16,256,256]{2,1,0:T(8,128)(2,1)S(1)} %tile_products_back_far.1), channel_id=1, source_target_pairs={{0,1},{1,0},{2,3},{3,2},{4,5},{5,4},{6,7},{7,6},{8,9},{9,8},{10,11... | collective-permute-start | bytes 6291464 | tf_op jit(solution)/shard_map/tile_products_back/ppermute | solution.py:31
  125.9 91.9 %all-to-all-start.3 = ((bf16[16,256,256]{2,1,0:T(8,128)(2,1)}), bf16[16,256,256]{2,1,0:T(8,128)(2,1)S(1)}, u32[]{:S(2)}, u32[]{:S(2)}) async-start(bf16[16,256,256]{2,1,0:T(8,128)(2,1)} %add_convert_fusion), calls=%async_computation.3 | async-start | bytes 4194304 | tf_op jit(solution)/shard_map/scatter_gradients/all_to_all | solution.py:187
  138.8 1.3 collective-permute-start.2
  140.1 3.9 %collective-permute-start.3 = (f32[32,256]{1,0:T(8,128)S(1)}, f32[32,256]{1,0:T(8,128)S(1)}, u32[]{:S(2)}, u32[]{:S(2)}) collective-permute-start(f32[32,256]{1,0:T(8,128)S(1)} %add.31), channel_id=1, source_target_pairs={{0,2},{2,0},{1,3},{3,1},{4,6},{6,4},{5,7},{7,5},{8,10},{10,8},{9,1... | collective-permute-start | bytes 98312 | tf_op jit(solution)/shard_map/weight_sum/ppermute | solution.py:31
  144.0 43.5 %collective-permute-start.4 = (f32[32,256]{1,0:T(8,128)S(1)}, f32[32,256]{1,0:T(8,128)S(1)}, u32[]{:S(2)}, u32[]{:S(2)}) collective-permute-start(f32[32,256]{1,0:T(8,128)S(1)} %add.32), channel_id=1, source_target_pairs={{0,4},{4,0},{8,12},{12,8},{16,20},{20,16},{24,28},{28,24},{1,5},{5... | collective-permute-start | bytes 98312 | tf_op jit(solution)/shard_map/weight_sum/ppermute | solution.py:31
  187.5 4.9 %collective-permute-start.5 = (f32[32,256]{1,0:T(8,128)S(1)}, f32[32,256]{1,0:T(8,128)S(1)}, u32[]{:S(2)}, u32[]{:S(2)}) collective-permute-start(f32[32,256]{1,0:T(8,128)S(1)} %add.33), channel_id=1, source_target_pairs={{0,8},{4,12},{8,0},{12,4},{16,24},{20,28},{24,16},{28,20},{1,9},{5... | collective-permute-start | bytes 98312 | tf_op jit(solution)/shard_map/weight_sum/ppermute | solution.py:31
  192.4 8.3 %collective-permute-start.6 = (f32[32,256]{1,0:T(8,128)S(1)}, f32[32,256]{1,0:T(8,128)S(1)}, u32[]{:S(2)}, u32[]{:S(2)}) collective-permute-start(f32[32,256]{1,0:T(8,128)S(1)} %add.34), channel_id=1, source_target_pairs={{0,16},{4,20},{8,24},{12,28},{16,0},{20,4},{24,8},{28,12},{1,17},{... | collective-permute-start | bytes 98312 | tf_op jit(solution)/shard_map/weight_sum/ppermute | solution.py:31
  200.7 5.4 %collective-permute-start.7 = (f32[32,256]{1,0:T(8,128)S(1)}, f32[32,256]{1,0:T(8,128)S(1)}, u32[]{:S(2)}, u32[]{:S(2)}) collective-permute-start(f32[32,256]{1,0:T(8,128)S(1)} %add.35), channel_id=1, source_target_pairs={{0,32},{32,0},{1,33},{33,1},{2,34},{34,2},{3,35},{35,3},{4,36},{36... | collective-permute-start | bytes 98312 | tf_op jit(solution)/shard_map/weight_sum/ppermute | solution.py:31
  206.1 4.4 %collective-permute-start.8 = (f32[64,256]{1,0:T(8,128)S(1)}, f32[64,256]{1,0:T(8,128)S(1)}, u32[]{:S(2)}, u32[]{:S(2)}) collective-permute-start(f32[64,256]{1,0:T(8,128)S(1)} %maximum_select_fusion.2), channel_id=1, source_target_pairs={{0,64},{64,0},{128,192},{192,128},{1,65},{65,1},{129,193},{193,129... | collective-permute-start | bytes 196616 | tf_op jit(solution)/shard_map/weight_sum/ppermute | solution.py:31
  210.5 6.6 %collective-permute-start.9 = (f32[128,256]{1,0:T(8,128)S(1)}, f32[128,256]{1,0:T(8,128)S(1)}, u32[]{:S(2)}, u32[]{:S(2)}) collective-permute-start(f32[128,256]{1,0:T(8,128)S(1)} %maximum_select_fusion.1), channel_id=1, source_target_pairs={{0,128},{64,192},{128,0},{192,64},{1,129},{65,193},{129,1},{193,65... | collective-permute-start | bytes 393224 | tf_op jit(solution)/shard_map/weight_sum/ppermute | solution.py:31

commit v3 on v2

v3 whole, which is shorter than its diff:
```python
import jax
import jax.numpy as jnp
import numpy as np
from jax import lax
from jax.experimental import pallas as pl
from jax.experimental.pallas import tpu as pltpu
from jax.sharding import Mesh
from jax.sharding import PartitionSpec as P

REP = ("y", "xh")
BLK = ("z", "xl", "core")
N_Z = 8
N_Y = 4
TILE = 128
F = 256
XR = 256
N_REP = 8
SLOTS = 128
ROW_BLOCKS = 16
UNROLL = 4
CLASSES = 6

f32 = jnp.float32
bf16 = jnp.bfloat16
VMEM_LIMIT = 12 << 20


def xor_swap(x, axis, n, bit):
    return lax.ppermute(x, axis, [(i, i ^ bit) for i in range(n)])


def add_swapped(x, axis, n, bit):
    return (x.astype(f32) + xor_swap(x, axis, n, bit).astype(f32)).astype(bf16)


def slot_table(rows, cols, count, my_xl, my_core):
    owner = cols >> 1
    z = owner >> 2
    dx = ((owner >> 1) & 1) ^ my_xl
    dc = (owner & 1) ^ my_core
    second = (cols & 1) == 1
    position = jnp.arange(SLOTS, dtype=jnp.int32)
    kind = jnp.where(position < count, jnp.where(second, 4 + dc, 2 * dc + dx), CLASSES)
    place = jnp.where(second, z * 2 + dx, dx * N_Z + z)
    packed = rows | (place << 8) | (position << 16)
    key = kind * SLOTS + position
    rank = jnp.sum((key[None, :] < key[:, None]).astype(jnp.int32), axis=1)
    ordered = jnp.sum(jnp.where(rank[None, :] == position[:, None], packed[None, :], 0), axis=1)
    starts = jnp.sum((kind[None, :] < position[:, None]).astype(jnp.int32), axis=1)
    return jnp.concatenate([jnp.stack([ordered, starts]), jnp.zeros((2, SLOTS), jnp.int32)], axis=1)


def slot_range(table, first, last):
    return table[1, first], table[1, last]


def tile_copy(table, tiles_hbm, tiles, sems, t):
    return pltpu.make_async_copy(tiles_hbm.at[table[0, t] >> 16], tiles.at[t], sems.at[t])


def start_tiles(table, first, last, tiles_hbm, tiles, sems):
    begin, end = slot_range(table, first, last)

    def start(t, carry):
        tile_copy(table, tiles_hbm, tiles, sems, t).start()
        return carry

    lax.fori_loop(begin, end, start, 0)


def slot_loop(table, first, last, tiles_hbm, tiles, sems, one_slot):
    begin, end = slot_range(table, first, last)

    def several(n):
        def step(i, carry):
            t0 = carry
            for u in range(n):
                tile_copy(table, tiles_hbm, tiles, sems, t0 + u).wait()
            for u in range(n):
                packed = table[0, t0 + u]
                one_slot(t0 + u, packed & 255, (packed >> 8) & 255)
            return t0 + n

        return step

    rounds = (end - begin) // UNROLL
    t0 = lax.fori_loop(0, rounds, several(UNROLL), begin)
    lax.fori_loop(0, end - begin - rounds * UNROLL, several(1), t0)


def add_products(table, first, tiles_hbm, feats, mask, acc, tiles, sems):
    def one_slot(t, row, place):
        acc[row] += jnp.dot(tiles[t], feats[place & mask], preferred_element_type=f32)

    slot_loop(table, first, first + 1, tiles_hbm, tiles, sems, one_slot)


def forward_first_kernel(table, tiles_hbm, near0, near1, far0, far1, acc, tiles, sems):
    start_tiles(table, 0, 4, tiles_hbm, tiles, sems)
    acc[...] = jnp.zeros_like(acc)
    for k, feats in enumerate((near0, near1, far0, far1)):
        add_products(table, k, tiles_hbm, feats, N_Z - 1, acc, tiles, sems)


def forward_second_kernel(table, tiles_hbm, feats, before, acc, tiles, sems):
    start_tiles(table, 4, 5, tiles_hbm, tiles, sems)
    acc[...] = before[...]
    add_products(table, 4, tiles_hbm, feats, 2 * N_Z - 1, acc, tiles, sems)


def forward_last_kernel(table, tiles_hbm, feats, before, out, tiles, sems, acc):
    start_tiles(table, 5, 6, tiles_hbm, tiles, sems)
    acc[...] = before[...]
    add_products(table, 5, tiles_hbm, feats, 2 * N_Z - 1, acc, tiles, sems)
    for r in range(N_REP):
        for h in range(2):
            out[r, pl.ds(h * TILE, TILE), :] = acc[2 * r + h].astype(bf16)


def backward_kernel(first, last, table, tiles_hbm, grads, out, tiles, sems, acc):
    start_tiles(table, first, last, tiles_hbm, tiles, sems)
    acc[...] = jnp.zeros_like(acc)

    def one_slot(t, row, place):
        g = grads[row >> 1, pl.ds(pl.multiple_of((row & 1) * TILE, TILE), TILE), :]
        acc[place] += lax.dot_general(tiles[t], g, (((0,), (0,)), ((), ())), preferred_element_type=f32)

    slot_loop(table, first, last, tiles_hbm, tiles, sems, one_slot)
    for k in range(2 * N_Z):
        out[k] = acc[k].astype(bf16)


def dense_kernel(parts, weight, cot, layer_out, payload, weight_part):
    total = parts[0].astype(f32)
    for r in range(1, N_REP):
        total += parts[r].astype(f32)
    hidden = total.astype(bf16)
    w = weight[...]
    preact = jnp.dot(hidden, w, preferred_element_type=f32)
    gating = jax.nn.sigmoid(preact)
    layer_out[...] = (preact * gating).astype(bf16)
    slope = gating * (1.0 + preact * (1.0 - gating))
    grad_pre = (cot[...].astype(f32) * slope).astype(bf16)
    grad_hidden = lax.dot_general(grad_pre, w, (((1,), (1,)), ((), ())), preferred_element_type=f32).astype(bf16)
    for r in range(N_REP):
        payload[r] = grad_hidden
    weight_part[...] = lax.dot_general(
        hidden, grad_pre, (((0,), (0,)), ((), ())), preferred_element_type=f32
    ).astype(bf16)


def on_device(node_features, tile_values, tile_row, tile_col, tile_count, weight, cotangent):
    sds = jax.ShapeDtypeStruct
    smem = pl.BlockSpec(memory_space=pltpu.SMEM)
    vmem = pl.BlockSpec(memory_space=pltpu.VMEM)
    params = pltpu.CompilerParams(vmem_limit_bytes=VMEM_LIMIT)
    acc_rows = sds((ROW_BLOCKS, TILE, F), f32)
    hbm = pl.BlockSpec(memory_space=pltpu.HBM)
    tile_room = [pltpu.VMEM((SLOTS, TILE, TILE), bf16), pltpu.SemaphoreType.DMA((SLOTS,))]
    tiles = pltpu.with_memory_space_constraint(tile_values[0, 0], pltpu.HBM)
    my_core = lax.axis_index("core")
    my_xl = lax.axis_index("xl")

    def call(kernel, name, out_shape, *args, scratch=()):
        return pl.pallas_call(
            kernel,
            out_shape=out_shape,
            in_specs=[smem, hbm] + [vmem] * (len(args) - 2),
            out_specs=vmem,
            scratch_shapes=tile_room + list(scratch),
            compiler_params=params,
            cost_estimate=pl.CostEstimate(flops=1, transcendentals=0, bytes_accessed=1),
            name=name,
        )(*args)

    with jax.named_scope("slot_table"):
        table = slot_table(tile_row[0, 0], tile_col[0, 0], tile_count[0, 0], my_xl, my_core)
    with jax.named_scope("gather_features"):
        first = jnp.broadcast_to(node_features[None, :TILE], (N_Z, TILE, F))
        near0 = lax.all_to_all(first, "z", 0, 0, tiled=True)
        own = node_features[TILE:]
        other = xor_swap(own, "xl", 2, 1)
        pair = jnp.broadcast_to(jnp.stack([own, other])[None], (N_Z, 2, TILE, F))
        near0, pair, table = lax.optimization_barrier((near0, pair, table))
        near_pair = lax.all_to_all(pair, "z", 0, 0, tiled=True).reshape(2 * N_Z, TILE, F)
        near1 = xor_swap(near0, "xl", 2, 1)
        far0 = xor_swap(near0, "core", 2, 1)
        far1 = xor_swap(near1, "core", 2, 1)
    with jax.named_scope("tile_products"):
        acc = call(forward_first_kernel, "tile_products_first", acc_rows, table, tiles, near0, near1, far0, far1)
        near_pair, acc = lax.optimization_barrier((near_pair, acc))
        far_pair = xor_swap(near_pair, "core", 2, 1)
        acc = call(forward_second_kernel, "tile_products_second", acc_rows, table, tiles, near_pair, acc)
        partial = call(
            forward_last_kernel,
            "tile_products_last",
            sds((N_REP, XR, F), bf16),
            table,
            tiles,
            far_pair,
            acc,
            scratch=[pltpu.VMEM((ROW_BLOCKS, TILE, F), f32)],
        )
    with jax.named_scope("sum_partials"):
        parts = lax.all_to_all(partial, REP, 0, 0, tiled=True)
    with jax.named_scope("dense"):
        layer_out, payload, weight_part = pl.pallas_call(
            dense_kernel,
            out_shape=(sds((XR, F), bf16), sds((N_REP, XR, F), bf16), sds((F, F), bf16)),
            in_specs=[vmem] * 3,
            out_specs=[vmem] * 3,
            compiler_params=params,
            name="dense",
        )(parts, weight, cotangent[0, 0])
    with jax.named_scope("share_gradients"):
        grads = lax.all_to_all(payload, REP, 0, 0, tiled=True)
    with jax.named_scope("weight_z"):
        w = weight_part
        for bit in (1, 2, 4):
            w = add_swapped(w, "z", N_Z, bit)
        grads, w = lax.optimization_barrier((grads, w))

    def backward(first, last, name):
        return call(
            lambda *refs: backward_kernel(first, last, *refs),
            name,
            sds((2 * N_Z, TILE, F), bf16),
            table,
            tiles,
            grads,
            scratch=[pltpu.VMEM((2 * N_Z, TILE, F), f32)],
        )

    with jax.named_scope("back_second"):
        far_back = backward(5, 6, "back_second_far")
        got = xor_swap(far_back, "core", 2, 1)
        near_back = backward(4, 5, "back_second_near")
        pair = (near_back.astype(f32) + got.astype(f32)).astype(bf16)
        pair, table, w = lax.optimization_barrier((pair, table, w))
        pair_got = lax.all_to_all(pair.reshape(N_Z, 2, TILE, F), "z", 0, 0, tiled=True)
    with jax.named_scope("back_first"):
        far_back = backward(2, 4, "back_first_far")
        got = xor_swap(far_back, "core", 2, 1)
        near_back = backward(0, 2, "back_first_near")
        away = (near_back[N_Z:].astype(f32) + got[N_Z:].astype(f32)).astype(bf16)
        back = xor_swap(away, "xl", 2, 1)
        for bit in (1, 2):
            w = add_swapped(w, "y", N_Y, bit)
        home = (near_back[:N_Z].astype(f32) + got[:N_Z].astype(f32) + back.astype(f32)).astype(bf16)
        home, w = lax.optimization_barrier((home, w))
        home_got = lax.all_to_all(home, "z", 0, 0, tiled=True)
    with jax.named_scope("grad_features"):
        pair_sum = jnp.sum(pair_got.astype(f32), axis=0)
        back = xor_swap(pair_sum[1].astype(bf16), "xl", 2, 1)
        second_sum = (pair_sum[0] + back.astype(f32)).astype(bf16)
        first_sum = jnp.sum(home_got.astype(f32), axis=0).astype(bf16)
        grad_features = jnp.concatenate([first_sum, second_sum], axis=0)
    with jax.named_scope("weight_rest"):
        w, _ = lax.optimization_barrier((w, pair_sum))
        w = add_swapped(w, "xl", 2, 1)
        w = add_swapped(w, "xh", 2, 1)
        grad_weight = w.astype(f32) + xor_swap(w, "core", 2, 1).astype(f32)
    return layer_out.reshape(1, 1, XR, F), grad_weight, grad_features


def solution(mesh):
    fine = Mesh(np.asarray(mesh.devices).reshape(N_Y, 2, N_Z, 2, 2), REP + BLK)
    placed = (
        P(REP + BLK, None),
        P(REP, BLK, None, None, None),
        P(REP, BLK, None),
        P(REP, BLK, None),
        P(REP, BLK),
        P(),
        P(BLK, REP, None, None),
    )
    return jax.shard_map(
        on_device,
        mesh=fine,
        in_specs=placed,
        out_specs=(P(BLK, REP, None, None), P(), P(REP + BLK, None)),
        check_vma=False,
    )
```

time: 218 us -> 195 us (0.89)
  the two profiles are of different devices: /device:TPU:2 before, /device:TPU:1 now
where the time goes in v3:
time: 195 us; the launch traced here: 193 us
  waiting for transfers between devices  68.7 us (35%)
  starting transfers between devices  53.3 us (27%)
  Pallas kernels  38.2 us (20%)
  blocking collectives  20.4 us (10%)
  other arithmetic  7.39 us (4%)
  local copies, waits for them, and re-layouts  3.95 us (2%)
    pallas_call x7, Pallas kernels, call(): pl.pallas_call(kernel, out_shape=out_shape, in_specs=[smem, hbm] + [vmem]...  36.8 us
    ppermute x17, waiting for transfers between devices, xor_swap(): return lax.ppermute(x, axis, [(i, i ^ bit) for i in range(n)])  33.8 us
    ppermute x17, starting transfers between devices, xor_swap(): return lax.ppermute(x, axis, [(i, i ^ bit) for i in range(n)])  30.1 us
    all_to_all x1, blocking collectives, on_device(): parts = lax.all_to_all(partial, REP, 0, 0, tiled=True)  20.4 us
    all_to_all x1, waiting for transfers between devices, on_device(): near0 = lax.all_to_all(first, 'z', 0, 0, tiled=True)  14.8 us
    all_to_all x1, starting transfers between devices, on_device(): near0 = lax.all_to_all(first, 'z', 0, 0, tiled=True)  9.01 us
    all_to_all x1, waiting for transfers between devices, on_device(): home_got = lax.all_to_all(home, 'z', 0, 0, tiled=True)  7.77 us
    all_to_all x1, waiting for transfers between devices, on_device(): lax.all_to_all(pair.reshape(N_Z, 2, TILE, F), 'z', 0, 0, tiled=True)  6.93 us
  transfers between devices with their start and end apart: 22, of which 16 were waited for; matrix products, arithmetic and copies ran while one was open for 3% of the time, Pallas kernels for 12%

profile of v3, /device:TPU:1, one launch (start us, length us, event | category | flops | bytes accessed | tf_op | source)
XLA Modules:
  0.0 193.5 jit_solution(13949015375967463073)
XLA Ops:
  2.3 9.0 %all-to-all-start = ((bf16[8,128,256]{2,1,0:T(8,128)(2,1)}), bf16[8,128,256]{2,1,0:T(8,128)(2,1)S(1)}, u32[]{:S(2)}, u32[]{:S(2)}) async-start(bf16[8,128,256]{2,1,0:T(8,128)(2,1)} %broadcast_in_dim.20), calls=%async_computation | async-start | bytes 1048576 | tf_op jit(solution)/shard_map/gather_features/all_to_all | solution.py:180
  14.5 14.8 %all-to-all-done.near0 = bf16[8,128,256]{2,1,0:T(8,128)(2,1)S(1)} async-done(((bf16[8,128,256]{2,1,0:T(8,128)(2,1)}), bf16[8,128,256]{2,1,0:T(8,128)(2,1)S(1)}, u32[]{:S(2)}, u32[]{:S(2)}) %all-to-all-start) | async-done | bytes 524320 | tf_op jit(solution)/shard_map/gather_features/all_to_all | solution.py:180
  30.5 3.6 %all-to-all-start.1 = ((bf16[8,2,128,256]{3,2,1,0:T(8,128)(2,1)}), bf16[8,2,128,256]{3,2,1,0:T(8,128)(2,1)S(1)}, u32[]{:S(2)}, u32[]{:S(2)}) async-start(bf16[8,2,128,256]{3,2,1,0:T(8,128)(2,1)} %broadcast_in_dim.21), calls=%async_computation.1 | async-start | bytes 2097152 | tf_op jit(solution)/shard_map/gather_features/all_to_all | solution.py:185
  36.1 11.0 %collective-permute-done.1.near1 = bf16[8,128,256]{2,1,0:T(8,128)(2,1)S(1)} collective-permute-done((bf16[8,128,256]{2,1,0:T(8,128)(2,1)S(1)}, bf16[8,128,256]{2,1,0:T(8,128)(2,1)S(1)}, u32[]{:S(2)}, u32[]{:S(2)}) %collective-permute-start.1) | collective-permute-done | bytes 524320 | tf_op jit(solution)/shard_map/gather_features/ppermute | solution.py:29
  48.5 1.5 collective-permute-done.3.far1
  51.1 7.2 %tile_products_first.1.before = f32[16,128,256]{2,1,0:T(8,128)S(1)} custom-call(s32[2,256]{1,0:T(2,128)S(1)} %concatenate.6.table.refs_0_, bf16[128,128,128]{2,1,0:T(8,128)(2,1)} %bitcast.67, bf16[8,128,256]{2,1,0:T(8,128)(2,1)S(1)} %copy-done.1, bf16[8,128,256]{2,1,0:T(8,128)(2,1)S(1)} %collective-permute-done.1.near1, ...), custom_call_target="tpu_custom_call" | custom-call | flops 1 | bytes 1 | tf_op jit(solution)/shard_map/tile_products/tile_products_first/pallas_call | solution.py:165
  58.2 5.0 %all-to-all-done.1 = bf16[8,2,128,256]{3,2,1,0:T(8,128)(2,1)S(1)} async-done(((bf16[8,2,128,256]{3,2,1,0:T(8,128)(2,1)}), bf16[8,2,128,256]{3,2,1,0:T(8,128)(2,1)S(1)}, u32[]{:S(2)}, u32[]{:S(2)}) %all-to-all-start.1) | async-done | bytes 1048608 | tf_op jit(solution)/shard_map/gather_features/all_to_all | solution.py:185
  63.7 5.0 %tile_products_second.1.before = f32[16,128,256]{2,1,0:T(8,128)S(1)} custom-call(s32[2,256]{1,0:T(2,128)S(1)} %concatenate.6.table.refs_0_, bf16[128,128,128]{2,1,0:T(8,128)(2,1)} %bitcast.68, bf16[16,128,256]{2,1,0:T(8,128)(2,1)S(1)} %bitcast.65, f32[16,128,256]{2,1,0:T(8,128)S(1)} %tile_products_first.1.before), custom_call_target="tpu_custom_call" | custom-call | flops 1 | bytes 1 | tf_op jit(solution)/shard_map/tile_products/tile_products_second/pallas_call | solution.py:165
  68.7 4.4 %tile_products_last.1 = bf16[8,256,256]{2,1,0:T(8,128)(2,1)S(1)} custom-call(s32[2,256]{1,0:T(2,128)S(1)} %concatenate.6.table.refs_0_, bf16[128,128,128]{2,1,0:T(8,128)(2,1)} %bitcast.69, bf16[16,128,256]{2,1,0:T(8,128)(2,1)S(1)} %collective-permute-done.4.feats, f32[16,128,256]{2,1,0:T(8,128)S(1)} %tile_products_second.1.before), custom_call_target="tpu_custom_call" | custom-call | flops 1 | bytes 1 | tf_op jit(solution)/shard_map/tile_products/tile_products_last/pallas_call | solution.py:165
  73.1 20.4 %all_to_all.30.parts = bf16[8,256,256]{2,1,0:T(8,128)(2,1)S(1)} all-to-all(bf16[8,256,256]{2,1,0:T(8,128)(2,1)S(1)} %tile_products_last.1), channel_id=1, replica_groups=mesh['y'=4,'xh'=2,'z'=8,'xl'=2,'core'=2] {'y','xh'}, dimensions={0} | all-to-all | bytes 2097152 | tf_op jit(solution)/shard_map/sum_partials/all_to_all | solution.py:205
  95.1 3.6 %all-to-all-start.3 = ((bf16[8,256,256]{2,1,0:T(8,128)(2,1)}), bf16[8,256,256]{2,1,0:T(8,128)(2,1)S(1)}, u32[]{:S(2)}, u32[]{:S(2)}) async-start(bf16[8,256,256]{2,1,0:T(8,128)(2,1)} %get-tuple-element.25), calls=%async_computation.3 | async-start | bytes 2097152 | tf_op jit(solution)/shard_map/share_gradients/all_to_all | solution.py:216
  98.8 1.9 collective-permute-start.6
  100.7 4.3 %collective-permute-done.6 = bf16[256,256]{1,0:T(8,128)(2,1)S(1)} collective-permute-done((bf16[256,256]{1,0:T(8,128)(2,1)S(1)}, bf16[256,256]{1,0:T(8,128)(2,1)S(1)}, u32[]{:S(2)}, u32[]{:S(2)}) %collective-permute-start.6) | collective-permute-done | bytes 131104 | tf_op jit(solution)/shard_map/weight_z/ppermute | solution.py:29
  105.0 5.3 %collective-permute-start.7 = (bf16[256,256]{1,0:T(8,128)(2,1)S(1)}, bf16[256,256]{1,0:T(8,128)(2,1)S(1)}, u32[]{:S(2)}, u32[]{:S(2)}) collective-permute-start(bf16[256,256]{1,0:T(8,128)(2,1)S(1)} %add_convert_fusion.8), channel_id=1, source_target_pairs={{0,16},{4,20},{8,24},{12,28},{16,0},{20,4},{24,8},{28,12},{1,17},{... | collective-permute-start | bytes 393224 | tf_op jit(solution)/shard_map/weight_z/ppermute | solution.py:29
  110.4 2.8 %collective-permute-done.7 = bf16[256,256]{1,0:T(8,128)(2,1)S(1)} collective-permute-done((bf16[256,256]{1,0:T(8,128)(2,1)S(1)}, bf16[256,256]{1,0:T(8,128)(2,1)S(1)}, u32[]{:S(2)}, u32[]{:S(2)}) %collective-permute-start.7) | collective-permute-done | bytes 131104 | tf_op jit(solution)/shard_map/weight_z/ppermute | solution.py:29
  113.6 4.7 %back_second_far.1 = bf16[16,128,256]{2,1,0:T(8,128)(2,1)S(1)} custom-call(s32[2,256]{1,0:T(2,128)S(1)} %concatenate.6.table.refs_0_, bf16[128,128,128]{2,1,0:T(8,128)(2,1)} %bitcast.70, bf16[8,256,256]{2,1,0:T(8,128)(2,1)S(1)} %all-to-all-done.3.refs_2_), custom_call_target="tpu_custom_call" | custom-call | flops 1 | bytes 1 | tf_op jit(solution)/shard_map/back_second/back_second_far/pallas_call | solution.py:165
  118.3 5.5 %collective-permute-start.8 = (bf16[16,128,256]{2,1,0:T(8,128)(2,1)S(1)}, bf16[16,128,256]{2,1,0:T(8,128)(2,1)S(1)}, u32[]{:S(2)}, u32[]{:S(2)}) collective-permute-start(bf16[16,128,256]{2,1,0:T(8,128)(2,1)S(1)} %back_second_far.1), channel_id=1, source_target_pairs={{0,1},{1,0},{2,3},{3,2},{4,5},{5,4},{6,7},{7,6},{8,9},{9,8},{10,11... | collective-permute-start | bytes 3145736 | tf_op jit(solution)/shard_map/back_second/ppermute | solution.py:29
  123.8 5.5 %back_second_near.1 = bf16[16,128,256]{2,1,0:T(8,128)(2,1)S(1)} custom-call(s32[2,256]{1,0:T(2,128)S(1)} %concatenate.6.table.refs_0_, bf16[128,128,128]{2,1,0:T(8,128)(2,1)} %bitcast.71, bf16[8,256,256]{2,1,0:T(8,128)(2,1)S(1)} %all-to-all-done.3.refs_2_), custom_call_target="tpu_custom_call" | custom-call | flops 1 | bytes 1 | tf_op jit(solution)/shard_map/back_second/back_second_near/pallas_call | solution.py:165
  130.6 5.1 %back_first_far.1 = bf16[16,128,256]{2,1,0:T(8,128)(2,1)S(1)} custom-call(s32[2,256]{1,0:T(2,128)S(1)} %concatenate.6.table.refs_0_, bf16[128,128,128]{2,1,0:T(8,128)(2,1)} %bitcast.72, bf16[8,256,256]{2,1,0:T(8,128)(2,1)S(1)} %all-to-all-done.3.refs_2_), custom_call_target="tpu_custom_call" | custom-call | flops 1 | bytes 1 | tf_op jit(solution)/shard_map/back_first/back_first_far/pallas_call | solution.py:165
  136.0 3.6 %all-to-all-start.4 = ((bf16[8,2,128,256]{3,2,1,0:T(8,128)(2,1)}), bf16[8,2,128,256]{3,2,1,0:T(8,128)(2,1)S(1)}, u32[]{:S(2)}, u32[]{:S(2)}) async-start(bf16[8,2,128,256]{3,2,1,0:T(8,128)(2,1)} %bitcast.15), calls=%async_computation.4 | async-start | bytes 2097152 | tf_op jit(solution)/shard_map/back_second/all_to_all | solution.py:240
  139.6 5.0 %back_first_near.1 = bf16[16,128,256]{2,1,0:T(8,128)(2,1)S(1)} custom-call(s32[2,256]{1,0:T(2,128)S(1)} %concatenate.6.table.refs_0_, bf16[128,128,128]{2,1,0:T(8,128)(2,1)} %bitcast.73, bf16[8,256,256]{2,1,0:T(8,128)(2,1)S(1)} %all-to-all-done.3.refs_2_), custom_call_target="tpu_custom_call" | custom-call | flops 1 | bytes 1 | tf_op jit(solution)/shard_map/back_first/back_first_near/pallas_call | solution.py:165
  147.3 1.9 collective-permute-done.11
  149.3 3.2 %collective-permute-start.12 = (bf16[256,256]{1,0:T(8,128)(2,1)S(1)}, bf16[256,256]{1,0:T(8,128)(2,1)S(1)}, u32[]{:S(2)}, u32[]{:S(2)}) collective-permute-start(bf16[256,256]{1,0:T(8,128)(2,1)S(1)} %add_convert_fusion.6), channel_id=1, source_target_pairs={{0,128},{64,192},{128,0},{192,64},{1,129},{65,193},{129,1},{193,65... | collective-permute-start | bytes 393224 | tf_op jit(solution)/shard_map/back_first/ppermute | solution.py:29
  152.5 2.5 %collective-permute-done.12 = bf16[256,256]{1,0:T(8,128)(2,1)S(1)} collective-permute-done((bf16[256,256]{1,0:T(8,128)(2,1)S(1)}, bf16[256,256]{1,0:T(8,128)(2,1)S(1)}, u32[]{:S(2)}, u32[]{:S(2)}) %collective-permute-start.12) | collective-permute-done | bytes 131104 | tf_op jit(solution)/shard_map/back_first/ppermute | solution.py:29
  155.0 4.8 %collective-permute-done.10 = bf16[8,128,256]{2,1,0:T(8,128)(2,1)S(1)} collective-permute-done((bf16[8,128,256]{2,1,0:T(8,128)(2,1)S(1)}, bf16[8,128,256]{2,1,0:T(8,128)(2,1)S(1)}, u32[]{:S(2)}, u32[]{:S(2)}) %collective-permute-start.10) | collective-permute-done | bytes 524320 | tf_op jit(solution)/shard_map/back_first/ppermute | solution.py:29
  159.8 2.0 %add_convert_fusion.1 = bf16[8,128,256]{2,1,0:T(8,128)(2,1)} fusion(bf16[8,128,256]{2,1,0:T(8,128)(2,1)S(1)} %collective-permute-done.10, bf16[16,128,256]{2,1,0:T(8,128)(2,1)} %collective-permute-done.9, bf16[16,128,256]{2,1,0:T(8,128)(2,1)S(1)} %back_first_near.1), kind=kLoop, calls=%fused_computation.2 | loop fusion | flops 1572864 | bytes 2097152 | tf_op jit(solution)/shard_map/back_first/convert_element_type | solution.py:249
  161.8 6.9 %all-to-all-done.4 = bf16[8,2,128,256]{3,2,1,0:T(8,128)(2,1)S(1)} async-done(((bf16[8,2,128,256]{3,2,1,0:T(8,128)(2,1)}), bf16[8,2,128,256]{3,2,1,0:T(8,128)(2,1)S(1)}, u32[]{:S(2)}, u32[]{:S(2)}) %all-to-all-start.4) | async-done | bytes 1048608 | tf_op jit(solution)/shard_map/back_second/all_to_all | solution.py:240
  168.9 2.5 %collective-permute-start.13 = (bf16[256,256]{1,0:T(8,128)(2,1)S(1)}, bf16[256,256]{1,0:T(8,128)(2,1)S(1)}, u32[]{:S(2)}, u32[]{:S(2)}) collective-permute-start(bf16[256,256]{1,0:T(8,128)(2,1)S(1)} %add_convert_fusion.5), channel_id=1, source_target_pairs={{0,2},{2,0},{1,3},{3,1},{4,6},{6,4},{5,7},{7,5},{8,10},{10,8},{9,1... | collective-permute-start | bytes 393224 | tf_op jit(solution)/shard_map/weight_rest/ppermute | solution.py:29
  171.4 3.5 %all-to-all-start.5 = ((bf16[8,128,256]{2,1,0:T(8,128)(2,1)}), bf16[8,128,256]{2,1,0:T(8,128)(2,1)S(1)}, u32[]{:S(2)}, u32[]{:S(2)}) async-start(bf16[8,128,256]{2,1,0:T(8,128)(2,1)} %add_convert_fusion.1), calls=%async_computation.5 | async-start | bytes 1048576 | tf_op jit(solution)/shard_map/back_first/all_to_all | solution.py:251
  176.6 3.7 %collective-permute-done.14 = bf16[256,256]{1,0:T(8,128)(2,1)S(1)} collective-permute-done((bf16[256,256]{1,0:T(8,128)(2,1)S(1)}, bf16[256,256]{1,0:T(8,128)(2,1)S(1)}, u32[]{:S(2)}, u32[]{:S(2)}) %collective-permute-start.14) | collective-permute-done | bytes 131104 | tf_op jit(solution)/shard_map/weight_rest/ppermute | solution.py:29
  180.4 2.9 %collective-permute-start.15 = (bf16[256,256]{1,0:T(8,128)(2,1)S(1)}, bf16[256,256]{1,0:T(8,128)(2,1)S(1)}, u32[]{:S(2)}, u32[]{:S(2)}) collective-permute-start(bf16[256,256]{1,0:T(8,128)(2,1)S(1)} %add_convert_fusion.3), channel_id=1, source_target_pairs={{0,1},{1,0},{2,3},{3,2},{4,5},{5,4},{6,7},{7,6},{8,9},{9,8},{10,11... | collective-permute-start | bytes 393224 | tf_op jit(solution)/shard_map/weight_rest/ppermute | solution.py:29
  185.0 7.8 %all-to-all-done.5 = bf16[8,128,256]{2,1,0:T(8,128)(2,1)S(1)} async-done(((bf16[8,128,256]{2,1,0:T(8,128)(2,1)}), bf16[8,128,256]{2,1,0:T(8,128)(2,1)S(1)}, u32[]{:S(2)}, u32[]{:S(2)}) %all-to-all-start.5) | async-done | bytes 524320 | tf_op jit(solution)/shard_map/back_first/all_to_all | solution.py:251
  (54 shorter events, 21.2 us)
Async XLA Ops:
  2.3 27.0 %all-to-all-start = ((bf16[8,128,256]{2,1,0:T(8,128)(2,1)}), bf16[8,128,256]{2,1,0:T(8,128)(2,1)S(1)}, u32[]{:S(2)}, u32[]{:S(2)}) async-start(bf16[8,128,256]{2,1,0:T(8,128)(2,1)} %broadcast_in_dim.20), calls=%async_computation | async-start | bytes 1048576 | tf_op jit(solution)/shard_map/gather_features/all_to_all | solution.py:180
  11.4 3.1 %collective-permute-start = (bf16[128,256]{1,0:T(8,128)(2,1)S(1)}, bf16[128,256]{1,0:T(8,128)(2,1)S(1)}, u32[]{:S(2)}, u32[]{:S(2)}) collective-permute-start(bf16[128,256]{1,0:T(8,128)(2,1)S(1)} %get-tuple-element.38), channel_id=1, source_target_pairs={{0,2},{2,0},{1,3},{3,1},{4,6},{6,4},{5,7},{7,5},{8,10},{10,8},{9,1... | collective-permute-start | bytes 196616 | tf_op jit(solution)/shard_map/gather_features/ppermute | solution.py:29
  29.3 20.7 %copy-start = (bf16[8,128,256]{2,1,0:T(8,128)(2,1)}, bf16[8,128,256]{2,1,0:T(8,128)(2,1)S(1)}, u32[]{:S(2)}) copy-start(bf16[8,128,256]{2,1,0:T(8,128)(2,1)S(1)} %all-to-all-done.near0) | copy-start | bytes 1572868
  30.5 32.7 %all-to-all-start.1 = ((bf16[8,2,128,256]{3,2,1,0:T(8,128)(2,1)}), bf16[8,2,128,256]{3,2,1,0:T(8,128)(2,1)S(1)}, u32[]{:S(2)}, u32[]{:S(2)}) async-start(bf16[8,2,128,256]{3,2,1,0:T(8,128)(2,1)} %broadcast_in_dim.21), calls=%async_computation.1 | async-start | bytes 2097152 | tf_op jit(solution)/shard_map/gather_features/all_to_all | solution.py:185
  34.0 13.1 %collective-permute-start.1 = (bf16[8,128,256]{2,1,0:T(8,128)(2,1)S(1)}, bf16[8,128,256]{2,1,0:T(8,128)(2,1)S(1)}, u32[]{:S(2)}, u32[]{:S(2)}) collective-permute-start(bf16[8,128,256]{2,1,0:T(8,128)(2,1)S(1)} %all-to-all-done.near0), channel_id=1, source_target_pairs={{0,2},{2,0},{1,3},{3,1},{4,6},{6,4},{5,7},{7,5},{8,10},{10,8},{9,1... | collective-permute-start | bytes 1572872 | tf_op jit(solution)/shard_map/gather_features/ppermute | solution.py:29
  35.3 13.1 %collective-permute-start.2 = (bf16[8,128,256]{2,1,0:T(8,128)(2,1)S(1)}, bf16[8,128,256]{2,1,0:T(8,128)(2,1)S(1)}, u32[]{:S(2)}, u32[]{:S(2)}) collective-permute-start(bf16[8,128,256]{2,1,0:T(8,128)(2,1)S(1)} %all-to-all-done.near0), channel_id=1, source_target_pairs={{0,1},{1,0},{2,3},{3,2},{4,5},{5,4},{6,7},{7,6},{8,9},{9,8},{10,11... | collective-permute-start | bytes 1572872 | tf_op jit(solution)/shard_map/gather_features/ppermute | solution.py:29
  47.1 2.9 %collective-permute-start.3 = (bf16[8,128,256]{2,1,0:T(8,128)(2,1)S(1)}, bf16[8,128,256]{2,1,0:T(8,128)(2,1)S(1)}, u32[]{:S(2)}, u32[]{:S(2)}) collective-permute-start(bf16[8,128,256]{2,1,0:T(8,128)(2,1)S(1)} %collective-permute-done.1.near1), channel_id=1, source_target_pairs={{0,1},{1,0},{2,3},{3,2},{4,5},{5,4},{6,7},{7,6},{8,9},{9,8},{10,11... | collective-permute-start | bytes 1572872 | tf_op jit(solution)/shard_map/gather_features/ppermute | solution.py:29
  50.0 1.0 copy-start.1
  63.2 5.5 %collective-permute-start.4 = (bf16[16,128,256]{2,1,0:T(8,128)(2,1)S(1)}, bf16[16,128,256]{2,1,0:T(8,128)(2,1)S(1)}, u32[]{:S(2)}, u32[]{:S(2)}) collective-permute-start(bf16[16,128,256]{2,1,0:T(8,128)(2,1)S(1)} %bitcast.64), channel_id=1, source_target_pairs={{0,1},{1,0},{2,3},{3,2},{4,5},{5,4},{6,7},{7,6},{8,9},{9,8},{10,11... | collective-permute-start | bytes 3145736 | tf_op jit(solution)/shard_map/tile_products/ppermute | solution.py:29
  73.1 20.4 %copy-start.2 = (bf16[256,256]{1,0:T(8,128)(2,1)S(1)}, bf16[256,256]{1,0:T(8,128)(2,1)}, u32[]{:S(2)}) copy-start(bf16[256,256]{1,0:T(8,128)(2,1)} %weight.1) | copy-start | bytes 393220
  73.1 20.4 %copy-start.3 = (bf16[1,1,256,256]{3,2,1,0:T(8,128)(2,1)S(1)}, bf16[1,1,256,256]{3,2,1,0:T(8,128)(2,1)}, u32[]{:S(2)}) copy-start(bf16[1,1,256,256]{3,2,1,0:T(8,128)(2,1)} %param.13) | copy-start | bytes 393220
  94.9 3.8 %collective-permute-start.5 = (bf16[256,256]{1,0:T(8,128)(2,1)S(1)}, bf16[256,256]{1,0:T(8,128)(2,1)S(1)}, u32[]{:S(2)}, u32[]{:S(2)}) collective-permute-start(bf16[256,256]{1,0:T(8,128)(2,1)S(1)} %get-tuple-element.26), channel_id=1, source_target_pairs={{0,4},{4,0},{8,12},{12,8},{16,20},{20,16},{24,28},{28,24},{1,5},{5... | collective-permute-start | bytes 393224 | tf_op jit(solution)/shard_map/weight_z/ppermute | solution.py:29
  95.1 18.5 %all-to-all-start.3 = ((bf16[8,256,256]{2,1,0:T(8,128)(2,1)}), bf16[8,256,256]{2,1,0:T(8,128)(2,1)S(1)}, u32[]{:S(2)}, u32[]{:S(2)}) async-start(bf16[8,256,256]{2,1,0:T(8,128)(2,1)} %get-tuple-element.25), calls=%async_computation.3 | async-start | bytes 2097152 | tf_op jit(solution)/shard_map/share_gradients/all_to_all | solution.py:216
  98.8 6.2 %collective-permute-start.6 = (bf16[256,256]{1,0:T(8,128)(2,1)S(1)}, bf16[256,256]{1,0:T(8,128)(2,1)S(1)}, u32[]{:S(2)}, u32[]{:S(2)}) collective-permute-start(bf16[256,256]{1,0:T(8,128)(2,1)S(1)} %add_convert_fusion.9), channel_id=1, source_target_pairs={{0,8},{4,12},{8,0},{12,4},{16,24},{20,28},{24,16},{28,20},{1,9},{5... | collective-permute-start | bytes 393224 | tf_op jit(solution)/shard_map/weight_z/ppermute | solution.py:29
  105.0 8.1 %collective-permute-start.7 = (bf16[256,256]{1,0:T(8,128)(2,1)S(1)}, bf16[256,256]{1,0:T(8,128)(2,1)S(1)}, u32[]{:S(2)}, u32[]{:S(2)}) collective-permute-start(bf16[256,256]{1,0:T(8,128)(2,1)S(1)} %add_convert_fusion.8), channel_id=1, source_target_pairs={{0,16},{4,20},{8,24},{12,28},{16,0},{20,4},{24,8},{28,12},{1,17},{... | collective-permute-start | bytes 393224 | tf_op jit(solution)/shard_map/weight_z/ppermute | solution.py:29
  118.3 11.0 %collective-permute-start.8 = (bf16[16,128,256]{2,1,0:T(8,128)(2,1)S(1)}, bf16[16,128,256]{2,1,0:T(8,128)(2,1)S(1)}, u32[]{:S(2)}, u32[]{:S(2)}) collective-permute-start(bf16[16,128,256]{2,1,0:T(8,128)(2,1)S(1)} %back_second_far.1), channel_id=1, source_target_pairs={{0,1},{1,0},{2,3},{3,2},{4,5},{5,4},{6,7},{7,6},{8,9},{9,8},{10,11... | collective-permute-start | bytes 3145736 | tf_op jit(solution)/shard_map/back_second/ppermute | solution.py:29
  135.7 10.3 %collective-permute-start.9 = (bf16[16,128,256]{2,1,0:T(8,128)(2,1)S(1)}, bf16[16,128,256]{2,1,0:T(8,128)(2,1)}, u32[]{:S(2)}, u32[]{:S(2)}) collective-permute-start(bf16[16,128,256]{2,1,0:T(8,128)(2,1)S(1)} %back_first_far.1), channel_id=1, source_target_pairs={{0,1},{1,0},{2,3},{3,2},{4,5},{5,4},{6,7},{7,6},{8,9},{9,8},{10,11... | collective-permute-start | bytes 3145736 | tf_op jit(solution)/shard_map/back_first/ppermute | solution.py:29
  136.0 32.7 %all-to-all-start.4 = ((bf16[8,2,128,256]{3,2,1,0:T(8,128)(2,1)}), bf16[8,2,128,256]{3,2,1,0:T(8,128)(2,1)S(1)}, u32[]{:S(2)}, u32[]{:S(2)}) async-start(bf16[8,2,128,256]{3,2,1,0:T(8,128)(2,1)} %bitcast.15), calls=%async_computation.4 | async-start | bytes 2097152 | tf_op jit(solution)/shard_map/back_second/all_to_all | solution.py:240
  144.6 4.7 %collective-permute-start.11 = (bf16[256,256]{1,0:T(8,128)(2,1)S(1)}, bf16[256,256]{1,0:T(8,128)(2,1)S(1)}, u32[]{:S(2)}, u32[]{:S(2)}) collective-permute-start(bf16[256,256]{1,0:T(8,128)(2,1)S(1)} %add_convert_fusion.7), channel_id=1, source_target_pairs={{0,64},{64,0},{128,192},{192,128},{1,65},{65,1},{129,193},{193,129... | collective-permute-start | bytes 393224 | tf_op jit(solution)/shard_map/back_first/ppermute | solution.py:29
  147.2 12.5 %collective-permute-start.10 = (bf16[8,128,256]{2,1,0:T(8,128)(2,1)S(1)}, bf16[8,128,256]{2,1,0:T(8,128)(2,1)S(1)}, u32[]{:S(2)}, u32[]{:S(2)}) collective-permute-start(bf16[8,128,256]{2,1,0:T(8,128)(2,1)S(1)} %add_convert_fusion.2), channel_id=1, source_target_pairs={{0,2},{2,0},{1,3},{3,1},{4,6},{6,4},{5,7},{7,5},{8,10},{10,8},{9,1... | collective-permute-start | bytes 1572872 | tf_op jit(solution)/shard_map/back_first/ppermute | solution.py:29
  149.3 5.7 %collective-permute-start.12 = (bf16[256,256]{1,0:T(8,128)(2,1)S(1)}, bf16[256,256]{1,0:T(8,128)(2,1)S(1)}, u32[]{:S(2)}, u32[]{:S(2)}) collective-permute-start(bf16[256,256]{1,0:T(8,128)(2,1)S(1)} %add_convert_fusion.6), channel_id=1, source_target_pairs={{0,128},{64,192},{128,0},{192,64},{1,129},{65,193},{129,1},{193,65... | collective-permute-start | bytes 393224 | tf_op jit(solution)/shard_map/back_first/ppermute | solution.py:29
  168.9 6.0 %collective-permute-start.13 = (bf16[256,256]{1,0:T(8,128)(2,1)S(1)}, bf16[256,256]{1,0:T(8,128)(2,1)S(1)}, u32[]{:S(2)}, u32[]{:S(2)}) collective-permute-start(bf16[256,256]{1,0:T(8,128)(2,1)S(1)} %add_convert_fusion.5), channel_id=1, source_target_pairs={{0,2},{2,0},{1,3},{3,1},{4,6},{6,4},{5,7},{7,5},{8,10},{10,8},{9,1... | collective-permute-start | bytes 393224 | tf_op jit(solution)/shard_map/weight_rest/ppermute | solution.py:29
  171.4 21.4 %all-to-all-start.5 = ((bf16[8,128,256]{2,1,0:T(8,128)(2,1)}), bf16[8,128,256]{2,1,0:T(8,128)(2,1)S(1)}, u32[]{:S(2)}, u32[]{:S(2)}) async-start(bf16[8,128,256]{2,1,0:T(8,128)(2,1)} %add_convert_fusion.1), calls=%async_computation.5 | async-start | bytes 1048576 | tf_op jit(solution)/shard_map/back_first/all_to_all | solution.py:251
  174.9 5.4 %collective-permute-start.14 = (bf16[256,256]{1,0:T(8,128)(2,1)S(1)}, bf16[256,256]{1,0:T(8,128)(2,1)S(1)}, u32[]{:S(2)}, u32[]{:S(2)}) collective-permute-start(bf16[256,256]{1,0:T(8,128)(2,1)S(1)} %add_convert_fusion.4), channel_id=1, source_target_pairs={{0,32},{32,0},{1,33},{33,1},{2,34},{34,2},{3,35},{35,3},{4,36},{36... | collective-permute-start | bytes 393224 | tf_op jit(solution)/shard_map/weight_rest/ppermute | solution.py:29
  176.0 7.2 %collective-permute-start.16 = (bf16[128,256]{1,0:T(8,128)(2,1)S(1)}, bf16[128,256]{1,0:T(8,128)(2,1)S(1)}, u32[]{:S(2)}, u32[]{:S(2)}) collective-permute-start(bf16[128,256]{1,0:T(8,128)(2,1)S(1)} %fusion.2), channel_id=1, source_target_pairs={{0,2},{2,0},{1,3},{3,1},{4,6},{6,4},{5,7},{7,5},{8,10},{10,8},{9,1... | collective-permute-start | bytes 196616 | tf_op jit(solution)/shard_map/grad_features/ppermute | solution.py:29
  180.4 3.9 %collective-permute-start.15 = (bf16[256,256]{1,0:T(8,128)(2,1)S(1)}, bf16[256,256]{1,0:T(8,128)(2,1)S(1)}, u32[]{:S(2)}, u32[]{:S(2)}) collective-permute-start(bf16[256,256]{1,0:T(8,128)(2,1)S(1)} %add_convert_fusion.3), channel_id=1, source_target_pairs={{0,1},{1,0},{2,3},{3,2},{4,5},{5,4},{6,7},{7,6},{8,9},{9,8},{10,11... | collective-permute-start | bytes 393224 | tf_op jit(solution)/shard_map/weight_rest/ppermute | solution.py:29

commit v4 on v3

--- a/solution.py
+++ b/solution.py
@@ -17,12 +17,12 @@
 N_REP = 8
 SLOTS = 128
 ROW_BLOCKS = 16
-UNROLL = 4
+UNROLL = 8
 CLASSES = 6
 
 f32 = jnp.float32
 bf16 = jnp.bfloat16
-VMEM_LIMIT = 12 << 20
+VMEM_LIMIT = 16 << 20
 
 
 def xor_swap(x, axis, n, bit):
@@ -31,6 +31,10 @@
 
 def add_swapped(x, axis, n, bit):
     return (x.astype(f32) + xor_swap(x, axis, n, bit).astype(f32)).astype(bf16)
+
+
+def hold(operand, value):
+    return lax.optimization_barrier((operand.reshape(-1, F)[:16], value))
 
 
 def slot_table(rows, cols, count, my_xl, my_core):
@@ -51,83 +55,113 @@
 
 
 def slot_range(table, first, last):
-    return table[1, first], table[1, last]
-
-
-def tile_copy(table, tiles_hbm, tiles, sems, t):
-    return pltpu.make_async_copy(tiles_hbm.at[table[0, t] >> 16], tiles.at[t], sems.at[t])
+    begin = table[1, first]
+    return begin, (table[1, last] - begin + UNROLL - 1) // UNROLL
 
 
 def start_tiles(table, first, last, tiles_hbm, tiles, sems):
-    begin, end = slot_range(table, first, last)
-
-    def start(t, carry):
-        tile_copy(table, tiles_hbm, tiles, sems, t).start()
+    begin, rounds = slot_range(table, first, last)
+
+    def start(i, carry):
+        for u in range(UNROLL):
+            at = i * UNROLL + u
+            pltpu.make_async_copy(tiles_hbm.at[table[0, begin + at] >> 16], tiles.at[at], sems.at[i]).start()
         return carry
 
-    lax.fori_loop(begin, end, start, 0)
+    lax.fori_loop(0, rounds, start, 0)
 
 
 def slot_loop(table, first, last, tiles_hbm, tiles, sems, one_slot):
-    begin, end = slot_range(table, first, last)
-
-    def several(n):
-        def step(i, carry):
-            t0 = carry
-            for u in range(n):
-                tile_copy(table, tiles_hbm, tiles, sems, t0 + u).wait()
-            for u in range(n):
-                packed = table[0, t0 + u]
-                one_slot(t0 + u, packed & 255, (packed >> 8) & 255)
-            return t0 + n
-
-        return step
-
-    rounds = (end - begin) // UNROLL
-    t0 = lax.fori_loop(0, rounds, several(UNROLL), begin)
-    lax.fori_loop(0, end - begin - rounds * UNROLL, several(1), t0)
-
-
-def add_products(table, first, tiles_hbm, feats, mask, acc, tiles, sems):
-    def one_slot(t, row, place):
-        acc[row] += jnp.dot(tiles[t], feats[place & mask], preferred_element_type=f32)
-
-    slot_loop(table, first, first + 1, tiles_hbm, tiles, sems, one_slot)
+    begin, rounds = slot_range(table, first, last)
+    end = table[1, last]
+
+    def step(i, carry):
+        pltpu.make_async_copy(
+            tiles_hbm.at[pl.ds(0, UNROLL)], tiles.at[pl.ds(i * UNROLL, UNROLL)], sems.at[i]
+        ).wait()
+        for u in range(UNROLL):
+            t = begin + i * UNROLL + u
+            packed = table[0, t]
+            one_slot(t < end, packed & 255, (packed >> 8) & 255, tiles[i * UNROLL + u])
+        return carry
+
+    lax.fori_loop(0, rounds, step, 0)
+
+
+def add_products(table, first, feats, mask, acc, room):
+    def one_slot(live, row, place, tile):
+        target = jnp.where(live, row, ROW_BLOCKS)
+        acc[target] += jnp.dot(tile, feats[place & mask], preferred_element_type=f32)
+
+    slot_loop(table, first, first + 1, *room, one_slot)
 
 
 def forward_first_kernel(table, tiles_hbm, near0, near1, far0, far1, acc, tiles, sems):
+    begin = table[1, 0]
     start_tiles(table, 0, 4, tiles_hbm, tiles, sems)
     acc[...] = jnp.zeros_like(acc)
+    _, rounds = slot_range(table, 0, 4)
+
+    def wait(i, carry):
+        pltpu.make_async_copy(
+            tiles_hbm.at[pl.ds(0, UNROLL)], tiles.at[pl.ds(i * UNROLL, UNROLL)], sems.at[i]
+        ).wait()
+        return carry
+
+    lax.fori_loop(0, rounds, wait, 0)
     for k, feats in enumerate((near0, near1, far0, far1)):
-        add_products(table, k, tiles_hbm, feats, N_Z - 1, acc, tiles, sems)
+        first, steps = slot_range(table, k, k + 1)
+        end = table[1, k + 1]
+
+        def step(i, carry):
+            for u in range(UNROLL):
+                t = first + i * UNROLL + u
+                packed = table[0, t]
+                target = jnp.where(t < end, packed & 255, ROW_BLOCKS)
+                at = jnp.minimum(t - begin, SLOTS - 1)
+                acc[target] += jnp.dot(
+                    tiles[at], feats[(packed >> 8) & (N_Z - 1)], preferred_element_type=f32
+                )
+            return carry
+
+        lax.fori_loop(0, steps, step, 0)
 
 
 def forward_second_kernel(table, tiles_hbm, feats, before, acc, tiles, sems):
     start_tiles(table, 4, 5, tiles_hbm, tiles, sems)
     acc[...] = before[...]
-    add_products(table, 4, tiles_hbm, feats, 2 * N_Z - 1, acc, tiles, sems)
+    add_products(table, 4, feats, 2 * N_Z - 1, acc, (tiles_hbm, tiles, sems))
 
 
 def forward_last_kernel(table, tiles_hbm, feats, before, out, tiles, sems, acc):
     start_tiles(table, 5, 6, tiles_hbm, tiles, sems)
     acc[...] = before[...]
-    add_products(table, 5, tiles_hbm, feats, 2 * N_Z - 1, acc, tiles, sems)
+    add_products(table, 5, feats, 2 * N_Z - 1, acc, (tiles_hbm, tiles, sems))
     for r in range(N_REP):
         for h in range(2):
             out[r, pl.ds(h * TILE, TILE), :] = acc[2 * r + h].astype(bf16)
 
 
-def backward_kernel(first, last, table, tiles_hbm, grads, out, tiles, sems, acc):
-    start_tiles(table, first, last, tiles_hbm, tiles, sems)
-    acc[...] = jnp.zeros_like(acc)
-
-    def one_slot(t, row, place):
-        g = grads[row >> 1, pl.ds(pl.multiple_of((row & 1) * TILE, TILE), TILE), :]
-        acc[place] += lax.dot_general(tiles[t], g, (((0,), (0,)), ((), ())), preferred_element_type=f32)
-
-    slot_loop(table, first, last, tiles_hbm, tiles, sems, one_slot)
-    for k in range(2 * N_Z):
-        out[k] = acc[k].astype(bf16)
+def backward_kernel(ranges, table, tiles_hbm, grads, *rest):
+    tiles, sems, acc = rest[-3:]
+    outs = rest[-3 - len(ranges) : -3]
+    for n, (first, last) in enumerate(ranges):
+        start_tiles(table, first, last, tiles_hbm, tiles.at[n], sems.at[n])
+    for n, ((first, last), out) in enumerate(zip(ranges, outs)):
+        acc[...] = jnp.zeros_like(acc)
+
+        def one_slot(live, row, place, tile):
+            target = jnp.where(live, place, 2 * N_Z)
+            g = grads[row >> 1, pl.ds(pl.multiple_of((row & 1) * TILE, TILE), TILE), :]
+            acc[target] += lax.dot_general(tile, g, (((0,), (0,)), ((), ())), preferred_element_type=f32)
+
+        slot_loop(table, first, last, tiles_hbm, tiles.at[n], sems.at[n], one_slot)
+        for k in range(2 * N_Z):
+            out[k] = acc[k].astype(bf16)
+
+
+def final_weight_kernel(mine, other, small, out):
+    out[...] = mine[...].astype(f32) + other[...].astype(f32)
 
 
 def dense_kernel(parts, weight, cot, layer_out, payload, weight_part):
@@ -154,10 +188,10 @@
     smem = pl.BlockSpec(memory_space=pltpu.SMEM)
     vmem = pl.BlockSpec(memory_space=pltpu.VMEM)
     params = pltpu.CompilerParams(vmem_limit_bytes=VMEM_LIMIT)
-    acc_rows = sds((ROW_BLOCKS, TILE, F), f32)
+    acc_rows = sds((ROW_BLOCKS + 1, TILE, F), f32)
     hbm = pl.BlockSpec(memory_space=pltpu.HBM)
-    tile_room = [pltpu.VMEM((SLOTS, TILE, TILE), bf16), pltpu.SemaphoreType.DMA((SLOTS,))]
     tiles = pltpu.with_memory_space_constraint(tile_values[0, 0], pltpu.HBM)
+    tile_room = [pltpu.VMEM((SLOTS, TILE, TILE), bf16), pltpu.SemaphoreType.DMA((SLOTS // UNROLL,))]
     my_core = lax.axis_index("core")
     my_xl = lax.axis_index("xl")
 
@@ -199,7 +233,7 @@
             tiles,
             far_pair,
             acc,
-            scratch=[pltpu.VMEM((ROW_BLOCKS, TILE, F), f32)],
+            scratch=[pltpu.VMEM((ROW_BLOCKS + 1, TILE, F), f32)],
         )
     with jax.named_scope("sum_partials"):
         parts = lax.all_to_all(partial, REP, 0, 0, tiled=True)
@@ -220,34 +254,40 @@
             w = add_swapped(w, "z", N_Z, bit)
         grads, w = lax.optimization_barrier((grads, w))
 
-    def backward(first, last, name):
-        return call(
-            lambda *refs: backward_kernel(first, last, *refs),
-            name,
-            sds((2 * N_Z, TILE, F), bf16),
-            table,
-            tiles,
-            grads,
-            scratch=[pltpu.VMEM((2 * N_Z, TILE, F), f32)],
-        )
+    def backward(ranges, name, *holders):
+        n = len(ranges)
+        return pl.pallas_call(
+            lambda *refs: backward_kernel(ranges, *refs),
+            out_shape=[sds((2 * N_Z, TILE, F), bf16)] * n,
+            in_specs=[smem, hbm] + [vmem] * (1 + len(holders)),
+            out_specs=[vmem] * n,
+            scratch_shapes=[
+                pltpu.VMEM((n, SLOTS, TILE, TILE), bf16),
+                pltpu.SemaphoreType.DMA((n, SLOTS // UNROLL)),
+                pltpu.VMEM((2 * N_Z + 1, TILE, F), f32),
+            ],
+            compiler_params=pltpu.CompilerParams(vmem_limit_bytes=VMEM_LIMIT),
+            cost_estimate=pl.CostEstimate(flops=1, transcendentals=0, bytes_accessed=1),
+            name=name,
+        )(table, tiles, grads, *holders)
 
     with jax.named_scope("back_second"):
-        far_back = backward(5, 6, "back_second_far")
-        got = xor_swap(far_back, "core", 2, 1)
-        near_back = backward(4, 5, "back_second_near")
+        far_second, far_first = backward(((5, 6), (2, 4)), "back_far")
+        got = xor_swap(far_second, "core", 2, 1)
+        first_got = xor_swap(far_first, "core", 2, 1)
+        (near_back,) = backward(((4, 5),), "back_second_near")
         pair = (near_back.astype(f32) + got.astype(f32)).astype(bf16)
-        pair, table, w = lax.optimization_barrier((pair, table, w))
+        pair_small, w = hold(pair, w)
         pair_got = lax.all_to_all(pair.reshape(N_Z, 2, TILE, F), "z", 0, 0, tiled=True)
     with jax.named_scope("back_first"):
-        far_back = backward(2, 4, "back_first_far")
-        got = xor_swap(far_back, "core", 2, 1)
-        near_back = backward(0, 2, "back_first_near")
+        got = first_got
+        (near_back,) = backward(((0, 2),), "back_first_near", pair_small)
         away = (near_back[N_Z:].astype(f32) + got[N_Z:].astype(f32)).astype(bf16)
         back = xor_swap(away, "xl", 2, 1)
-        for bit in (1, 2):
-            w = add_swapped(w, "y", N_Y, bit)
+        w1, w2, w3 = (xor_swap(w, "y", N_Y, bit).astype(f32) for bit in (1, 2, 3))
+        w = ((w.astype(f32) + w1) + (w2 + w3)).astype(bf16)
         home = (near_back[:N_Z].astype(f32) + got[:N_Z].astype(f32) + back.astype(f32)).astype(bf16)
-        home, w = lax.optimization_barrier((home, w))
+        home, w, pair_got = lax.optimization_barrier((home, w, pair_got))
         home_got = lax.all_to_all(home, "z", 0, 0, tiled=True)
     with jax.named_scope("grad_features"):
         pair_sum = jnp.sum(pair_got.astype(f32), axis=0)
@@ -256,10 +296,17 @@
         first_sum = jnp.sum(home_got.astype(f32), axis=0).astype(bf16)
         grad_features = jnp.concatenate([first_sum, second_sum], axis=0)
     with jax.named_scope("weight_rest"):
-        w, _ = lax.optimization_barrier((w, pair_sum))
+        home_small, w = hold(pair_got, w)
         w = add_swapped(w, "xl", 2, 1)
         w = add_swapped(w, "xh", 2, 1)
-        grad_weight = w.astype(f32) + xor_swap(w, "core", 2, 1).astype(f32)
+        grad_weight = pl.pallas_call(
+            final_weight_kernel,
+            out_shape=sds((F, F), f32),
+            in_specs=[vmem] * 3,
+            out_specs=vmem,
+            compiler_params=params,
+            name="final_weight",
+        )(w, xor_swap(w, "core", 2, 1), home_small)
     return layer_out.reshape(1, 1, XR, F), grad_weight, grad_features
 
 

time: 195 us -> 183 us (0.938)
  Pallas kernels: 38.2 us -> 16.3 us
  waiting for transfers between devices: 68.7 us -> 83 us
  starting transfers between devices: 53.3 us -> 46.9 us
  blocking collectives: 20.4 us -> 22.9 us
    pallas_call x7 -> x3, Pallas kernels: 36.8 us -> 7 us  [call(): pl.pallas_call(kernel, out_shape=out_shape, in_specs=[smem, hbm] + [vmem]...]
    ppermute x17 -> x18, waiting for transfers between devices: 33.8 us -> 46.6 us  [xor_swap(): return lax.ppermute(x, axis, [(i, i ^ bit) for i in range(n)])]
    ppermute x17 -> x18, starting transfers between devices: 30.1 us -> 21.4 us  [xor_swap(): return lax.ppermute(x, axis, [(i, i ^ bit) for i in range(n)])]
    pallas_call x0 -> x4, Pallas kernels: none -> 7.89 us  [the longest x3 7.15 us: backward(): pl.pallas_call(lambda *refs: backward_kernel(ranges, *refs), out_shape=[s...]
    all_to_all x1, waiting for transfers between devices: 7.77 us -> 3.09 us  [on_device(): home_got = lax.all_to_all(home, 'z', 0, 0, tiled=True)]
    all_to_all x1, waiting for transfers between devices: 4.96 us -> 9.04 us  [on_device(): lax.all_to_all(pair, 'z', 0, 0, tiled=True).reshape(2 * N_Z, TILE, F)]
    all_to_all x1, blocking collectives: 20.4 us -> 22.9 us  [on_device(): parts = lax.all_to_all(partial, REP, 0, 0, tiled=True)]
    all_to_all x1, starting transfers between devices: 3.57 us -> 5.95 us  [on_device(): lax.all_to_all(pair.reshape(N_Z, 2, TILE, F), 'z', 0, 0, tiled=True)]
  transfers between devices with their start and end apart: 22 -> 23, of which waited for: 16 -> 18; matrix products, arithmetic and copies ran while one was open for 3% -> 4% of each run, Pallas kernels for 12% -> 6%
where the time goes in v4:
time: 183 us; the launch traced here: 182 us
  waiting for transfers between devices  83 us (45%)
  starting transfers between devices  46.9 us (26%)
  blocking collectives  22.9 us (13%)
  Pallas kernels  16.3 us (9%)
  other arithmetic  6.71 us (4%)
  local copies, waits for them, and re-layouts  4.67 us (3%)
    ppermute x18, waiting for transfers between devices, xor_swap(): return lax.ppermute(x, axis, [(i, i ^ bit) for i in range(n)])  46.6 us
    all_to_all x1, blocking collectives, on_device(): parts = lax.all_to_all(partial, REP, 0, 0, tiled=True)  22.9 us
    ppermute x18, starting transfers between devices, xor_swap(): return lax.ppermute(x, axis, [(i, i ^ bit) for i in range(n)])  21.4 us
    all_to_all x1, waiting for transfers between devices, on_device(): near0 = lax.all_to_all(first, 'z', 0, 0, tiled=True)  14.8 us
    all_to_all x1, waiting for transfers between devices, on_device(): lax.all_to_all(pair.reshape(N_Z, 2, TILE, F), 'z', 0, 0, tiled=True)  9.29 us
    all_to_all x1, waiting for transfers between devices, on_device(): lax.all_to_all(pair, 'z', 0, 0, tiled=True).reshape(2 * N_Z, TILE, F)  9.04 us
    all_to_all x1, starting transfers between devices, on_device(): near0 = lax.all_to_all(first, 'z', 0, 0, tiled=True)  9.01 us
    pallas_call x3, Pallas kernels, backward(): pl.pallas_call(lambda *refs: backward_kernel(ranges, *refs), out_shape=[s...  7.15 us
  transfers between devices with their start and end apart: 23, of which 18 were waited for; matrix products, arithmetic and copies ran while one was open for 4% of the time, Pallas kernels for 6%

profile of v4, /device:TPU:1, one launch (start us, length us, event | category | flops | bytes accessed | tf_op | source)
XLA Modules:
  0.0 182.0 jit_solution(9741989948425445985)
XLA Ops:
  2.4 9.0 %all-to-all-start = ((bf16[8,128,256]{2,1,0:T(8,128)(2,1)}), bf16[8,128,256]{2,1,0:T(8,128)(2,1)S(1)}, u32[]{:S(2)}, u32[]{:S(2)}) async-start(bf16[8,128,256]{2,1,0:T(8,128)(2,1)} %broadcast_in_dim.20), calls=%async_computation | async-start | bytes 1048576 | tf_op jit(solution)/shard_map/gather_features/all_to_all | solution.py:214
  14.5 14.8 %all-to-all-done.near0 = bf16[8,128,256]{2,1,0:T(8,128)(2,1)S(1)} async-done(((bf16[8,128,256]{2,1,0:T(8,128)(2,1)}), bf16[8,128,256]{2,1,0:T(8,128)(2,1)S(1)}, u32[]{:S(2)}, u32[]{:S(2)}) %all-to-all-start) | async-done | bytes 524320 | tf_op jit(solution)/shard_map/gather_features/all_to_all | solution.py:214
  30.5 3.6 %all-to-all-start.1 = ((bf16[8,2,128,256]{3,2,1,0:T(8,128)(2,1)}), bf16[8,2,128,256]{3,2,1,0:T(8,128)(2,1)S(1)}, u32[]{:S(2)}, u32[]{:S(2)}) async-start(bf16[8,2,128,256]{3,2,1,0:T(8,128)(2,1)} %broadcast_in_dim.21), calls=%async_computation.1 | async-start | bytes 2097152 | tf_op jit(solution)/shard_map/gather_features/all_to_all | solution.py:219
  36.1 11.0 %collective-permute-done.1.near1 = bf16[8,128,256]{2,1,0:T(8,128)(2,1)S(1)} collective-permute-done((bf16[8,128,256]{2,1,0:T(8,128)(2,1)S(1)}, bf16[8,128,256]{2,1,0:T(8,128)(2,1)S(1)}, u32[]{:S(2)}, u32[]{:S(2)}) %collective-permute-start.1) | collective-permute-done | bytes 524320 | tf_op jit(solution)/shard_map/gather_features/ppermute | solution.py:29
  48.5 1.5 collective-permute-done.3.far1
  51.1 3.1 %tile_products_first.1.before = f32[17,128,256]{2,1,0:T(8,128)S(1)} custom-call(s32[2,256]{1,0:T(2,128)S(1)} %concatenate.6.table.refs_0_, bf16[128,128,128]{2,1,0:T(8,128)(2,1)} %bitcast.69, bf16[8,128,256]{2,1,0:T(8,128)(2,1)S(1)} %copy-done.1, bf16[8,128,256]{2,1,0:T(8,128)(2,1)S(1)} %collective-permute-done.1.near1, ...), custom_call_target="tpu_custom_call" | custom-call | flops 1 | bytes 1 | tf_op jit(solution)/shard_map/tile_products/tile_products_first/pallas_call | solution.py:199
  54.2 9.0 %all-to-all-done.1 = bf16[8,2,128,256]{3,2,1,0:T(8,128)(2,1)S(1)} async-done(((bf16[8,2,128,256]{3,2,1,0:T(8,128)(2,1)}), bf16[8,2,128,256]{3,2,1,0:T(8,128)(2,1)S(1)}, u32[]{:S(2)}, u32[]{:S(2)}) %all-to-all-start.1) | async-done | bytes 1048608 | tf_op jit(solution)/shard_map/gather_features/all_to_all | solution.py:219
  63.7 1.9 %tile_products_second.1.before = f32[17,128,256]{2,1,0:T(8,128)S(1)} custom-call(s32[2,256]{1,0:T(2,128)S(1)} %concatenate.6.table.refs_0_, bf16[128,128,128]{2,1,0:T(8,128)(2,1)} %bitcast.70, bf16[16,128,256]{2,1,0:T(8,128)(2,1)S(1)} %bitcast.67, f32[17,128,256]{2,1,0:T(8,128)S(1)} %tile_products_first.1.before), custom_call_target="tpu_custom_call" | custom-call | flops 1 | bytes 1 | tf_op jit(solution)/shard_map/tile_products/tile_products_second/pallas_call | solution.py:199
  66.0 2.0 %tile_products_last.1 = bf16[8,256,256]{2,1,0:T(8,128)(2,1)S(1)} custom-call(s32[2,256]{1,0:T(2,128)S(1)} %concatenate.6.table.refs_0_, bf16[128,128,128]{2,1,0:T(8,128)(2,1)} %bitcast.71, bf16[16,128,256]{2,1,0:T(8,128)(2,1)S(1)} %collective-permute-done.4.feats, f32[17,128,256]{2,1,0:T(8,128)S(1)} %tile_products_second.1.before), custom_call_target="tpu_custom_call" | custom-call | flops 1 | bytes 1 | tf_op jit(solution)/shard_map/tile_products/tile_products_last/pallas_call | solution.py:199
  68.0 22.9 %all_to_all.30.parts = bf16[8,256,256]{2,1,0:T(8,128)(2,1)S(1)} all-to-all(bf16[8,256,256]{2,1,0:T(8,128)(2,1)S(1)} %tile_products_last.1), channel_id=1, replica_groups=mesh['y'=4,'xh'=2,'z'=8,'xl'=2,'core'=2] {'y','xh'}, dimensions={0} | all-to-all | bytes 2097152 | tf_op jit(solution)/shard_map/sum_partials/all_to_all | solution.py:239
  92.3 2.6 %collective-permute-start.5 = (bf16[256,256]{1,0:T(8,128)(2,1)S(1)}, bf16[256,256]{1,0:T(8,128)(2,1)S(1)}, u32[]{:S(2)}, u32[]{:S(2)}) collective-permute-start(bf16[256,256]{1,0:T(8,128)(2,1)S(1)} %get-tuple-element.29), channel_id=1, source_target_pairs={{0,4},{4,0},{8,12},{12,8},{16,20},{20,16},{24,28},{28,24},{1,5},{5... | collective-permute-start | bytes 393224 | tf_op jit(solution)/shard_map/weight_z/ppermute | solution.py:29
  94.9 3.6 %all-to-all-start.3 = ((bf16[8,256,256]{2,1,0:T(8,128)(2,1)}), bf16[8,256,256]{2,1,0:T(8,128)(2,1)S(1)}, u32[]{:S(2)}, u32[]{:S(2)}) async-start(bf16[8,256,256]{2,1,0:T(8,128)(2,1)} %get-tuple-element.28), calls=%async_computation.3 | async-start | bytes 2097152 | tf_op jit(solution)/shard_map/share_gradients/all_to_all | solution.py:250
  98.5 1.7 collective-permute-start.6
  100.2 6.2 %collective-permute-done.6 = bf16[256,256]{1,0:T(8,128)(2,1)S(1)} collective-permute-done((bf16[256,256]{1,0:T(8,128)(2,1)S(1)}, bf16[256,256]{1,0:T(8,128)(2,1)S(1)}, u32[]{:S(2)}, u32[]{:S(2)}) %collective-permute-start.6) | collective-permute-done | bytes 131104 | tf_op jit(solution)/shard_map/weight_z/ppermute | solution.py:29
  106.6 8.6 %collective-permute-done.7 = bf16[256,256]{1,0:T(8,128)(2,1)S(1)} collective-permute-done((bf16[256,256]{1,0:T(8,128)(2,1)S(1)}, bf16[256,256]{1,0:T(8,128)(2,1)S(1)}, u32[]{:S(2)}, u32[]{:S(2)}) %collective-permute-start.7) | collective-permute-done | bytes 131104 | tf_op jit(solution)/shard_map/weight_z/ppermute | solution.py:29
  115.4 2.7 %back_far.1 = (bf16[16,128,256]{2,1,0:T(8,128)(2,1)S(1)}, bf16[16,128,256]{2,1,0:T(8,128)(2,1)S(1)}) custom-call(s32[2,256]{1,0:T(2,128)S(1)} %concatenate.6.table.refs_0_, bf16[128,128,128]{2,1,0:T(8,128)(2,1)} %bitcast.72, bf16[8,256,256]{2,1,0:T(8,128)(2,1)S(1)} %all-to-all-done.3.refs_2_), custom_call_target="tpu_custom_call" | custom-call | flops 1 | bytes 1 | tf_op jit(solution)/shard_map/back_second/back_far/pallas_call | solution.py:259
  118.1 2.7 %collective-permute-start.8 = (bf16[16,128,256]{2,1,0:T(8,128)(2,1)S(1)}, bf16[16,128,256]{2,1,0:T(8,128)(2,1)S(1)}, u32[]{:S(2)}, u32[]{:S(2)}) collective-permute-start(bf16[16,128,256]{2,1,0:T(8,128)(2,1)S(1)} %get-tuple-element.31), channel_id=1, source_target_pairs={{0,1},{1,0},{2,3},{3,2},{4,5},{5,4},{6,7},{7,6},{8,9},{9,8},{10,11... | collective-permute-start | bytes 3145736 | tf_op jit(solution)/shard_map/back_second/ppermute | solution.py:29
  120.8 2.0 %back_second_near.1 = bf16[16,128,256]{2,1,0:T(8,128)(2,1)S(1)} custom-call(s32[2,256]{1,0:T(2,128)S(1)} %concatenate.6.table.refs_0_, bf16[128,128,128]{2,1,0:T(8,128)(2,1)} %bitcast.73, bf16[8,256,256]{2,1,0:T(8,128)(2,1)S(1)} %all-to-all-done.3.refs_2_), custom_call_target="tpu_custom_call" | custom-call | flops 1 | bytes 1 | tf_op jit(solution)/shard_map/back_second/back_second_near/pallas_call | solution.py:259
  124.6 5.9 %all-to-all-start.4 = ((bf16[8,2,128,256]{3,2,1,0:T(8,128)(2,1)}), bf16[8,2,128,256]{3,2,1,0:T(8,128)(2,1)S(1)}, u32[]{:S(2)}, u32[]{:S(2)}) async-start(bf16[8,2,128,256]{3,2,1,0:T(8,128)(2,1)} %bitcast.16), calls=%async_computation.4 | async-start | bytes 2097152 | tf_op jit(solution)/shard_map/back_second/all_to_all | solution.py:281
  131.2 2.4 %back_first_near.1 = bf16[16,128,256]{2,1,0:T(8,128)(2,1)S(1)} custom-call(s32[2,256]{1,0:T(2,128)S(1)} %concatenate.6.table.refs_0_, bf16[128,128,128]{2,1,0:T(8,128)(2,1)} %bitcast.74, bf16[8,256,256]{2,1,0:T(8,128)(2,1)S(1)} %all-to-all-done.3.refs_2_, bf16[16,256]{1,0:T(8,128)(2,1)S(1)} %slice.41.refs_3_), custom_call_target="tpu_custom_call" | custom-call | flops 1 | bytes 1 | tf_op jit(solution)/shard_map/back_first/back_first_near/pallas_call | solution.py:259
  134.9 1.9 %collective-permute-start.11 = (bf16[256,256]{1,0:T(8,128)(2,1)S(1)}, bf16[256,256]{1,0:T(8,128)(2,1)S(1)}, u32[]{:S(2)}, u32[]{:S(2)}) collective-permute-start(bf16[256,256]{1,0:T(8,128)(2,1)S(1)} %add_convert_fusion.6), channel_id=1, source_target_pairs={{0,64},{64,0},{128,192},{192,128},{1,65},{65,1},{129,193},{193,129... | collective-permute-start | bytes 393224 | tf_op jit(solution)/shard_map/back_first/ppermute | solution.py:29
  136.8 1.9 %collective-permute-start.12 = (bf16[256,256]{1,0:T(8,128)(2,1)S(1)}, bf16[256,256]{1,0:T(8,128)(2,1)S(1)}, u32[]{:S(2)}, u32[]{:S(2)}) collective-permute-start(bf16[256,256]{1,0:T(8,128)(2,1)S(1)} %add_convert_fusion.6), channel_id=1, source_target_pairs={{0,128},{64,192},{128,0},{192,64},{1,129},{65,193},{129,1},{193,65... | collective-permute-start | bytes 393224 | tf_op jit(solution)/shard_map/back_first/ppermute | solution.py:29
  139.5 4.3 %collective-permute-done.12 = bf16[256,256]{1,0:T(8,128)(2,1)S(1)} collective-permute-done((bf16[256,256]{1,0:T(8,128)(2,1)S(1)}, bf16[256,256]{1,0:T(8,128)(2,1)S(1)}, u32[]{:S(2)}, u32[]{:S(2)}) %collective-permute-start.12) | collective-permute-done | bytes 131104 | tf_op jit(solution)/shard_map/back_first/ppermute | solution.py:29
  143.8 2.6 %collective-permute-done.13 = bf16[256,256]{1,0:T(8,128)(2,1)S(1)} collective-permute-done((bf16[256,256]{1,0:T(8,128)(2,1)S(1)}, bf16[256,256]{1,0:T(8,128)(2,1)S(1)}, u32[]{:S(2)}, u32[]{:S(2)}) %collective-permute-start.13) | collective-permute-done | bytes 131104 | tf_op jit(solution)/shard_map/back_first/ppermute | solution.py:29
  146.5 2.0 %collective-permute-done.10 = bf16[8,128,256]{2,1,0:T(8,128)(2,1)S(1)} collective-permute-done((bf16[8,128,256]{2,1,0:T(8,128)(2,1)S(1)}, bf16[8,128,256]{2,1,0:T(8,128)(2,1)S(1)}, u32[]{:S(2)}, u32[]{:S(2)}) %collective-permute-start.10) | collective-permute-done | bytes 524320 | tf_op jit(solution)/shard_map/back_first/ppermute | solution.py:29
  148.5 2.0 %add_convert_fusion.1 = bf16[8,128,256]{2,1,0:T(8,128)(2,1)} fusion(bf16[8,128,256]{2,1,0:T(8,128)(2,1)S(1)} %collective-permute-done.10, bf16[16,128,256]{2,1,0:T(8,128)(2,1)} %collective-permute-done.9, bf16[16,128,256]{2,1,0:T(8,128)(2,1)S(1)} %back_first_near.1), kind=kLoop, calls=%fused_computation.2 | loop fusion | flops 1572864 | bytes 2097152 | tf_op jit(solution)/shard_map/back_first/convert_element_type | solution.py:289
  150.6 9.3 %all-to-all-done.4 = bf16[8,2,128,256]{3,2,1,0:T(8,128)(2,1)S(1)} async-done(((bf16[8,2,128,256]{3,2,1,0:T(8,128)(2,1)}), bf16[8,2,128,256]{3,2,1,0:T(8,128)(2,1)S(1)}, u32[]{:S(2)}, u32[]{:S(2)}) %all-to-all-start.4) | async-done | bytes 1048608 | tf_op jit(solution)/shard_map/back_second/all_to_all | solution.py:281
  159.8 3.5 %all-to-all-start.5 = ((bf16[8,128,256]{2,1,0:T(8,128)(2,1)}), bf16[8,128,256]{2,1,0:T(8,128)(2,1)S(1)}, u32[]{:S(2)}, u32[]{:S(2)}) async-start(bf16[8,128,256]{2,1,0:T(8,128)(2,1)} %add_convert_fusion.1), calls=%async_computation.5 | async-start | bytes 1048576 | tf_op jit(solution)/shard_map/back_first/all_to_all | solution.py:291
  163.6 4.4 %collective-permute-done.14 = bf16[256,256]{1,0:T(8,128)(2,1)S(1)} collective-permute-done((bf16[256,256]{1,0:T(8,128)(2,1)S(1)}, bf16[256,256]{1,0:T(8,128)(2,1)S(1)}, u32[]{:S(2)}, u32[]{:S(2)}) %collective-permute-start.14) | collective-permute-done | bytes 131104 | tf_op jit(solution)/shard_map/weight_rest/ppermute | solution.py:29
  169.7 4.0 %collective-permute-done.15 = bf16[256,256]{1,0:T(8,128)(2,1)S(1)} collective-permute-done((bf16[256,256]{1,0:T(8,128)(2,1)S(1)}, bf16[256,256]{1,0:T(8,128)(2,1)S(1)}, u32[]{:S(2)}, u32[]{:S(2)}) %collective-permute-start.15) | collective-permute-done | bytes 131104 | tf_op jit(solution)/shard_map/weight_rest/ppermute | solution.py:29
  173.7 2.7 %collective-permute-start.16 = (bf16[256,256]{1,0:T(8,128)(2,1)S(1)}, bf16[256,256]{1,0:T(8,128)(2,1)S(1)}, u32[]{:S(2)}, u32[]{:S(2)}) collective-permute-start(bf16[256,256]{1,0:T(8,128)(2,1)S(1)} %add_convert_fusion.3.mine), channel_id=1, source_target_pairs={{0,1},{1,0},{2,3},{3,2},{4,5},{5,4},{6,7},{7,6},{8,9},{9,8},{10,11... | collective-permute-start | bytes 393224 | tf_op jit(solution)/shard_map/weight_rest/ppermute | solution.py:29
  178.1 3.1 %all-to-all-done.5 = bf16[8,128,256]{2,1,0:T(8,128)(2,1)S(1)} async-done(((bf16[8,128,256]{2,1,0:T(8,128)(2,1)}), bf16[8,128,256]{2,1,0:T(8,128)(2,1)S(1)}, u32[]{:S(2)}, u32[]{:S(2)}) %all-to-all-start.5) | async-done | bytes 524320 | tf_op jit(solution)/shard_map/back_first/all_to_all | solution.py:291
  (56 shorter events, 21.4 us)
Async XLA Ops:
  2.4 27.0 %all-to-all-start = ((bf16[8,128,256]{2,1,0:T(8,128)(2,1)}), bf16[8,128,256]{2,1,0:T(8,128)(2,1)S(1)}, u32[]{:S(2)}, u32[]{:S(2)}) async-start(bf16[8,128,256]{2,1,0:T(8,128)(2,1)} %broadcast_in_dim.20), calls=%async_computation | async-start | bytes 1048576 | tf_op jit(solution)/shard_map/gather_features/all_to_all | solution.py:214
  11.4 3.1 %collective-permute-start = (bf16[128,256]{1,0:T(8,128)(2,1)S(1)}, bf16[128,256]{1,0:T(8,128)(2,1)S(1)}, u32[]{:S(2)}, u32[]{:S(2)}) collective-permute-start(bf16[128,256]{1,0:T(8,128)(2,1)S(1)} %get-tuple-element.44), channel_id=1, source_target_pairs={{0,2},{2,0},{1,3},{3,1},{4,6},{6,4},{5,7},{7,5},{8,10},{10,8},{9,1... | collective-permute-start | bytes 196616 | tf_op jit(solution)/shard_map/gather_features/ppermute | solution.py:29
  29.3 20.7 %copy-start = (bf16[8,128,256]{2,1,0:T(8,128)(2,1)}, bf16[8,128,256]{2,1,0:T(8,128)(2,1)S(1)}, u32[]{:S(2)}) copy-start(bf16[8,128,256]{2,1,0:T(8,128)(2,1)S(1)} %all-to-all-done.near0) | copy-start | bytes 1572868
  30.5 32.7 %all-to-all-start.1 = ((bf16[8,2,128,256]{3,2,1,0:T(8,128)(2,1)}), bf16[8,2,128,256]{3,2,1,0:T(8,128)(2,1)S(1)}, u32[]{:S(2)}, u32[]{:S(2)}) async-start(bf16[8,2,128,256]{3,2,1,0:T(8,128)(2,1)} %broadcast_in_dim.21), calls=%async_computation.1 | async-start | bytes 2097152 | tf_op jit(solution)/shard_map/gather_features/all_to_all | solution.py:219
  34.1 13.1 %collective-permute-start.1 = (bf16[8,128,256]{2,1,0:T(8,128)(2,1)S(1)}, bf16[8,128,256]{2,1,0:T(8,128)(2,1)S(1)}, u32[]{:S(2)}, u32[]{:S(2)}) collective-permute-start(bf16[8,128,256]{2,1,0:T(8,128)(2,1)S(1)} %all-to-all-done.near0), channel_id=1, source_target_pairs={{0,2},{2,0},{1,3},{3,1},{4,6},{6,4},{5,7},{7,5},{8,10},{10,8},{9,1... | collective-permute-start | bytes 1572872 | tf_op jit(solution)/shard_map/gather_features/ppermute | solution.py:29
  35.4 13.1 %collective-permute-start.2 = (bf16[8,128,256]{2,1,0:T(8,128)(2,1)S(1)}, bf16[8,128,256]{2,1,0:T(8,128)(2,1)S(1)}, u32[]{:S(2)}, u32[]{:S(2)}) collective-permute-start(bf16[8,128,256]{2,1,0:T(8,128)(2,1)S(1)} %all-to-all-done.near0), channel_id=1, source_target_pairs={{0,1},{1,0},{2,3},{3,2},{4,5},{5,4},{6,7},{7,6},{8,9},{9,8},{10,11... | collective-permute-start | bytes 1572872 | tf_op jit(solution)/shard_map/gather_features/ppermute | solution.py:29
  47.2 2.9 %collective-permute-start.3 = (bf16[8,128,256]{2,1,0:T(8,128)(2,1)S(1)}, bf16[8,128,256]{2,1,0:T(8,128)(2,1)S(1)}, u32[]{:S(2)}, u32[]{:S(2)}) collective-permute-start(bf16[8,128,256]{2,1,0:T(8,128)(2,1)S(1)} %collective-permute-done.1.near1), channel_id=1, source_target_pairs={{0,1},{1,0},{2,3},{3,2},{4,5},{5,4},{6,7},{7,6},{8,9},{9,8},{10,11... | collective-permute-start | bytes 1572872 | tf_op jit(solution)/shard_map/gather_features/ppermute | solution.py:29
  50.0 1.0 copy-start.1
  63.2 2.8 %collective-permute-start.4 = (bf16[16,128,256]{2,1,0:T(8,128)(2,1)S(1)}, bf16[16,128,256]{2,1,0:T(8,128)(2,1)S(1)}, u32[]{:S(2)}, u32[]{:S(2)}) collective-permute-start(bf16[16,128,256]{2,1,0:T(8,128)(2,1)S(1)} %bitcast.66), channel_id=1, source_target_pairs={{0,1},{1,0},{2,3},{3,2},{4,5},{5,4},{6,7},{7,6},{8,9},{9,8},{10,11... | collective-permute-start | bytes 3145736 | tf_op jit(solution)/shard_map/tile_products/ppermute | solution.py:29
  68.0 22.9 %copy-start.2 = (bf16[256,256]{1,0:T(8,128)(2,1)S(1)}, bf16[256,256]{1,0:T(8,128)(2,1)}, u32[]{:S(2)}) copy-start(bf16[256,256]{1,0:T(8,128)(2,1)} %weight.1) | copy-start | bytes 393220
  68.0 22.9 %copy-start.3 = (bf16[1,1,256,256]{3,2,1,0:T(8,128)(2,1)S(1)}, bf16[1,1,256,256]{3,2,1,0:T(8,128)(2,1)}, u32[]{:S(2)}) copy-start(bf16[1,1,256,256]{3,2,1,0:T(8,128)(2,1)} %param.13) | copy-start | bytes 393220
  92.3 6.1 %collective-permute-start.5 = (bf16[256,256]{1,0:T(8,128)(2,1)S(1)}, bf16[256,256]{1,0:T(8,128)(2,1)S(1)}, u32[]{:S(2)}, u32[]{:S(2)}) collective-permute-start(bf16[256,256]{1,0:T(8,128)(2,1)S(1)} %get-tuple-element.29), channel_id=1, source_target_pairs={{0,4},{4,0},{8,12},{12,8},{16,20},{20,16},{24,28},{28,24},{1,5},{5... | collective-permute-start | bytes 393224 | tf_op jit(solution)/shard_map/weight_z/ppermute | solution.py:29
  94.9 20.5 %all-to-all-start.3 = ((bf16[8,256,256]{2,1,0:T(8,128)(2,1)}), bf16[8,256,256]{2,1,0:T(8,128)(2,1)S(1)}, u32[]{:S(2)}, u32[]{:S(2)}) async-start(bf16[8,256,256]{2,1,0:T(8,128)(2,1)} %get-tuple-element.28), calls=%async_computation.3 | async-start | bytes 2097152 | tf_op jit(solution)/shard_map/share_gradients/all_to_all | solution.py:250
  98.5 8.0 %collective-permute-start.6 = (bf16[256,256]{1,0:T(8,128)(2,1)S(1)}, bf16[256,256]{1,0:T(8,128)(2,1)S(1)}, u32[]{:S(2)}, u32[]{:S(2)}) collective-permute-start(bf16[256,256]{1,0:T(8,128)(2,1)S(1)} %add_convert_fusion.8), channel_id=1, source_target_pairs={{0,8},{4,12},{8,0},{12,4},{16,24},{20,28},{24,16},{28,20},{1,9},{5... | collective-permute-start | bytes 393224 | tf_op jit(solution)/shard_map/weight_z/ppermute | solution.py:29
  106.5 8.7 %collective-permute-start.7 = (bf16[256,256]{1,0:T(8,128)(2,1)S(1)}, bf16[256,256]{1,0:T(8,128)(2,1)S(1)}, u32[]{:S(2)}, u32[]{:S(2)}) collective-permute-start(bf16[256,256]{1,0:T(8,128)(2,1)S(1)} %add_convert_fusion.7), channel_id=1, source_target_pairs={{0,16},{4,20},{8,24},{12,28},{16,0},{20,4},{24,8},{28,12},{1,17},{... | collective-permute-start | bytes 393224 | tf_op jit(solution)/shard_map/weight_z/ppermute | solution.py:29
  118.1 5.2 %collective-permute-start.8 = (bf16[16,128,256]{2,1,0:T(8,128)(2,1)S(1)}, bf16[16,128,256]{2,1,0:T(8,128)(2,1)S(1)}, u32[]{:S(2)}, u32[]{:S(2)}) collective-permute-start(bf16[16,128,256]{2,1,0:T(8,128)(2,1)S(1)} %get-tuple-element.31), channel_id=1, source_target_pairs={{0,1},{1,0},{2,3},{3,2},{4,5},{5,4},{6,7},{7,6},{8,9},{9,8},{10,11... | collective-permute-start | bytes 3145736 | tf_op jit(solution)/shard_map/back_second/ppermute | solution.py:29
  122.8 10.8 %collective-permute-start.9 = (bf16[16,128,256]{2,1,0:T(8,128)(2,1)S(1)}, bf16[16,128,256]{2,1,0:T(8,128)(2,1)}, u32[]{:S(2)}, u32[]{:S(2)}) collective-permute-start(bf16[16,128,256]{2,1,0:T(8,128)(2,1)S(1)} %get-tuple-element.34), channel_id=1, source_target_pairs={{0,1},{1,0},{2,3},{3,2},{4,5},{5,4},{6,7},{7,6},{8,9},{9,8},{10,11... | collective-permute-start | bytes 3145736 | tf_op jit(solution)/shard_map/back_second/ppermute | solution.py:29
  124.6 35.3 %all-to-all-start.4 = ((bf16[8,2,128,256]{3,2,1,0:T(8,128)(2,1)}), bf16[8,2,128,256]{3,2,1,0:T(8,128)(2,1)S(1)}, u32[]{:S(2)}, u32[]{:S(2)}) async-start(bf16[8,2,128,256]{3,2,1,0:T(8,128)(2,1)} %bitcast.16), calls=%async_computation.4 | async-start | bytes 2097152 | tf_op jit(solution)/shard_map/back_second/all_to_all | solution.py:281
  134.8 13.7 %collective-permute-start.10 = (bf16[8,128,256]{2,1,0:T(8,128)(2,1)S(1)}, bf16[8,128,256]{2,1,0:T(8,128)(2,1)S(1)}, u32[]{:S(2)}, u32[]{:S(2)}) collective-permute-start(bf16[8,128,256]{2,1,0:T(8,128)(2,1)S(1)} %add_convert_fusion.2), channel_id=1, source_target_pairs={{0,2},{2,0},{1,3},{3,1},{4,6},{6,4},{5,7},{7,5},{8,10},{10,8},{9,1... | collective-permute-start | bytes 1572872 | tf_op jit(solution)/shard_map/back_first/ppermute | solution.py:29
  134.9 4.6 %collective-permute-start.11 = (bf16[256,256]{1,0:T(8,128)(2,1)S(1)}, bf16[256,256]{1,0:T(8,128)(2,1)S(1)}, u32[]{:S(2)}, u32[]{:S(2)}) collective-permute-start(bf16[256,256]{1,0:T(8,128)(2,1)S(1)} %add_convert_fusion.6), channel_id=1, source_target_pairs={{0,64},{64,0},{128,192},{192,128},{1,65},{65,1},{129,193},{193,129... | collective-permute-start | bytes 393224 | tf_op jit(solution)/shard_map/back_first/ppermute | solution.py:29
  136.8 7.0 %collective-permute-start.12 = (bf16[256,256]{1,0:T(8,128)(2,1)S(1)}, bf16[256,256]{1,0:T(8,128)(2,1)S(1)}, u32[]{:S(2)}, u32[]{:S(2)}) collective-permute-start(bf16[256,256]{1,0:T(8,128)(2,1)S(1)} %add_convert_fusion.6), channel_id=1, source_target_pairs={{0,128},{64,192},{128,0},{192,64},{1,129},{65,193},{129,1},{193,65... | collective-permute-start | bytes 393224 | tf_op jit(solution)/shard_map/back_first/ppermute | solution.py:29
  138.6 7.8 %collective-permute-start.13 = (bf16[256,256]{1,0:T(8,128)(2,1)S(1)}, bf16[256,256]{1,0:T(8,128)(2,1)S(1)}, u32[]{:S(2)}, u32[]{:S(2)}) collective-permute-start(bf16[256,256]{1,0:T(8,128)(2,1)S(1)} %add_convert_fusion.6), channel_id=1, source_target_pairs={{0,192},{64,128},{128,64},{192,0},{1,193},{65,129},{129,65},{193,1... | collective-permute-start | bytes 393224 | tf_op jit(solution)/shard_map/back_first/ppermute | solution.py:29
  159.8 21.4 %all-to-all-start.5 = ((bf16[8,128,256]{2,1,0:T(8,128)(2,1)}), bf16[8,128,256]{2,1,0:T(8,128)(2,1)S(1)}, u32[]{:S(2)}, u32[]{:S(2)}) async-start(bf16[8,128,256]{2,1,0:T(8,128)(2,1)} %add_convert_fusion.1), calls=%async_computation.5 | async-start | bytes 1048576 | tf_op jit(solution)/shard_map/back_first/all_to_all | solution.py:291
  163.4 4.7 %collective-permute-start.14 = (bf16[256,256]{1,0:T(8,128)(2,1)S(1)}, bf16[256,256]{1,0:T(8,128)(2,1)S(1)}, u32[]{:S(2)}, u32[]{:S(2)}) collective-permute-start(bf16[256,256]{1,0:T(8,128)(2,1)S(1)} %add_convert_fusion.5), channel_id=1, source_target_pairs={{0,2},{2,0},{1,3},{3,1},{4,6},{6,4},{5,7},{7,5},{8,10},{10,8},{9,1... | collective-permute-start | bytes 393224 | tf_op jit(solution)/shard_map/weight_rest/ppermute | solution.py:29
  168.1 5.5 %collective-permute-start.15 = (bf16[256,256]{1,0:T(8,128)(2,1)S(1)}, bf16[256,256]{1,0:T(8,128)(2,1)S(1)}, u32[]{:S(2)}, u32[]{:S(2)}) collective-permute-start(bf16[256,256]{1,0:T(8,128)(2,1)S(1)} %add_convert_fusion.4), channel_id=1, source_target_pairs={{0,32},{32,0},{1,33},{33,1},{2,34},{34,2},{3,35},{35,3},{4,36},{36... | collective-permute-start | bytes 393224 | tf_op jit(solution)/shard_map/weight_rest/ppermute | solution.py:29
  169.6 6.8 %collective-permute-start.17 = (bf16[128,256]{1,0:T(8,128)(2,1)S(1)}, bf16[128,256]{1,0:T(8,128)(2,1)S(1)}, u32[]{:S(2)}, u32[]{:S(2)}) collective-permute-start(bf16[128,256]{1,0:T(8,128)(2,1)S(1)} %fusion.2), channel_id=1, source_target_pairs={{0,2},{2,0},{1,3},{3,1},{4,6},{6,4},{5,7},{7,5},{8,10},{10,8},{9,1... | collective-permute-start | bytes 196616 | tf_op jit(solution)/shard_map/grad_features/ppermute | solution.py:29
  173.7 3.7 %collective-permute-start.16 = (bf16[256,256]{1,0:T(8,128)(2,1)S(1)}, bf16[256,256]{1,0:T(8,128)(2,1)S(1)}, u32[]{:S(2)}, u32[]{:S(2)}) collective-permute-start(bf16[256,256]{1,0:T(8,128)(2,1)S(1)} %add_convert_fusion.3.mine), channel_id=1, source_target_pairs={{0,1},{1,0},{2,3},{3,2},{4,5},{5,4},{6,7},{7,6},{8,9},{9,8},{10,11... | collective-permute-start | bytes 393224 | tf_op jit(solution)/shard_map/weight_rest/ppermute | solution.py:29

commit v5 on v4

--- a/solution.py
+++ b/solution.py
@@ -160,11 +160,22 @@
             out[k] = acc[k].astype(bf16)
 
 
-def final_weight_kernel(mine, other, small, out):
-    out[...] = mine[...].astype(f32) + other[...].astype(f32)
-
-
-def dense_kernel(parts, weight, cot, layer_out, payload, weight_part):
+def half_of(core, which):
+    return pl.ds(pl.multiple_of((core[0] if which == 0 else 1 - core[0]) * TILE, TILE), TILE)
+
+
+def final_weight_kernel(core, mine, other, holder, out):
+    out[half_of(core, 0), :] = mine[...].astype(f32)
+    out[half_of(core, 1), :] = other[...].astype(f32)
+
+
+def pair_copies_kernel(own, other, out):
+    for z in range(N_Z):
+        out[z, 0] = own[...]
+        out[z, 1] = other[...]
+
+
+def dense_kernel(core, parts, weight, cot, layer_out, payload, keep, give, terms):
     total = parts[0].astype(f32)
     for r in range(1, N_REP):
         total += parts[r].astype(f32)
@@ -178,9 +189,9 @@
     grad_hidden = lax.dot_general(grad_pre, w, (((1,), (1,)), ((), ())), preferred_element_type=f32).astype(bf16)
     for r in range(N_REP):
         payload[r] = grad_hidden
-    weight_part[...] = lax.dot_general(
-        hidden, grad_pre, (((0,), (0,)), ((), ())), preferred_element_type=f32
-    ).astype(bf16)
+    terms[...] = lax.dot_general(hidden, grad_pre, (((0,), (0,)), ((), ())), preferred_element_type=f32)
+    keep[...] = terms[half_of(core, 0), :].astype(bf16)
+    give[...] = terms[half_of(core, 1), :].astype(bf16)
 
 
 def on_device(node_features, tile_values, tile_row, tile_col, tile_count, weight, cotangent):
@@ -214,7 +225,14 @@
         near0 = lax.all_to_all(first, "z", 0, 0, tiled=True)
         own = node_features[TILE:]
         other = xor_swap(own, "xl", 2, 1)
-        pair = jnp.broadcast_to(jnp.stack([own, other])[None], (N_Z, 2, TILE, F))
+        pair = pl.pallas_call(
+            pair_copies_kernel,
+            out_shape=sds((N_Z, 2, TILE, F), bf16),
+            in_specs=[vmem] * 2,
+            out_specs=vmem,
+            compiler_params=params,
+            name="pair_copies",
+        )(own, other)
         near0, pair, table = lax.optimization_barrier((near0, pair, table))
         near_pair = lax.all_to_all(pair, "z", 0, 0, tiled=True).reshape(2 * N_Z, TILE, F)
         near1 = xor_swap(near0, "xl", 2, 1)
@@ -238,19 +256,30 @@
     with jax.named_scope("sum_partials"):
         parts = lax.all_to_all(partial, REP, 0, 0, tiled=True)
     with jax.named_scope("dense"):
-        layer_out, payload, weight_part = pl.pallas_call(
+        core = my_core.astype(jnp.int32).reshape(1)
+        layer_out, payload, keep, give = pl.pallas_call(
             dense_kernel,
-            out_shape=(sds((XR, F), bf16), sds((N_REP, XR, F), bf16), sds((F, F), bf16)),
-            in_specs=[vmem] * 3,
-            out_specs=[vmem] * 3,
+            out_shape=(
+                sds((XR, F), bf16),
+                sds((N_REP, XR, F), bf16),
+                sds((TILE, F), bf16),
+                sds((TILE, F), bf16),
+            ),
+            in_specs=[smem] + [vmem] * 3,
+            out_specs=[vmem] * 4,
+            scratch_shapes=[pltpu.VMEM((F, F), f32)],
             compiler_params=params,
             name="dense",
-        )(parts, weight, cotangent[0, 0])
+        )(core, parts, weight, cotangent[0, 0])
     with jax.named_scope("share_gradients"):
         grads = lax.all_to_all(payload, REP, 0, 0, tiled=True)
     with jax.named_scope("weight_z"):
-        w = weight_part
-        for bit in (1, 2, 4):
+        ring = [(2 * z + c, 2 * (z ^ 1) + (c ^ 1)) for z in range(N_Z) for c in range(2)]
+        near_give = xor_swap(give, "core", 2, 1).astype(f32)
+        far_give = lax.ppermute(give, ("z", "core"), ring).astype(f32)
+        far_keep = xor_swap(keep, "z", N_Z, 1).astype(f32)
+        w = ((keep.astype(f32) + near_give) + (far_keep + far_give)).astype(bf16)
+        for bit in (2, 4):
             w = add_swapped(w, "z", N_Z, bit)
         grads, w = lax.optimization_barrier((grads, w))
 
@@ -290,23 +319,25 @@
         home, w, pair_got = lax.optimization_barrier((home, w, pair_got))
         home_got = lax.all_to_all(home, "z", 0, 0, tiled=True)
     with jax.named_scope("grad_features"):
-        pair_sum = jnp.sum(pair_got.astype(f32), axis=0)
+        pair_sum, w = lax.optimization_barrier((jnp.sum(pair_got.astype(f32), axis=0), w))
         back = xor_swap(pair_sum[1].astype(bf16), "xl", 2, 1)
         second_sum = (pair_sum[0] + back.astype(f32)).astype(bf16)
         first_sum = jnp.sum(home_got.astype(f32), axis=0).astype(bf16)
         grad_features = jnp.concatenate([first_sum, second_sum], axis=0)
     with jax.named_scope("weight_rest"):
-        home_small, w = hold(pair_got, w)
-        w = add_swapped(w, "xl", 2, 1)
-        w = add_swapped(w, "xh", 2, 1)
+        def from_x(dh, dl):
+            ring = [(2 * h + l, 2 * (h ^ dh) + (l ^ dl)) for h in range(2) for l in range(2)]
+            return lax.ppermute(w, ("xh", "xl"), ring).astype(f32)
+
+        w = ((w.astype(f32) + from_x(0, 1)) + (from_x(1, 0) + from_x(1, 1))).astype(bf16)
         grad_weight = pl.pallas_call(
             final_weight_kernel,
             out_shape=sds((F, F), f32),
-            in_specs=[vmem] * 3,
+            in_specs=[smem] + [vmem] * 3,
             out_specs=vmem,
             compiler_params=params,
             name="final_weight",
-        )(w, xor_swap(w, "core", 2, 1), home_small)
+        )(core, w, xor_swap(w, "core", 2, 1), pair_sum)
     return layer_out.reshape(1, 1, XR, F), grad_weight, grad_features
 
 

time: 183 us -> 184 us (level)
  Pallas kernels: 16.3 us -> 25.6 us
  waiting for transfers between devices: 83 us -> 76.6 us
  starting transfers between devices: 46.9 us -> 44 us
    ppermute x18 -> x17, waiting for transfers between devices: 46.6 us -> 38.2 us  [xor_swap(): return lax.ppermute(x, axis, [(i, i ^ bit) for i in range(n)])]
    ppermute x18 -> x17, starting transfers between devices: 21.4 us -> 14.8 us  [xor_swap(): return lax.ppermute(x, axis, [(i, i ^ bit) for i in range(n)])]
    ppermute x0 -> x4, starting transfers between devices: none -> 6.04 us  [the longest x3 4.34 us: from_x(): return lax.ppermute(w, ('xh', 'xl'), ring).astype(f32)]
    ppermute x0 -> x4, waiting for transfers between devices: none -> 4.48 us  [the longest x3 2.61 us: from_x(): return lax.ppermute(w, ('xh', 'xl'), ring).astype(f32)]
    pallas_call x3, Pallas kernels: 7 us -> 11.2 us  [call(): pl.pallas_call(kernel, out_shape=out_shape, in_specs=[smem, hbm] + [vmem]...]
    pallas_call x3, Pallas kernels: 7.15 us -> 11.2 us  [backward(): pl.pallas_call(lambda *refs: backward_kernel(ranges, *refs), out_shape=[s...]
    all_to_all x1, starting transfers between devices: 5.95 us -> 3.56 us  [on_device(): lax.all_to_all(pair.reshape(N_Z, 2, TILE, F), 'z', 0, 0, tiled=True)]
    all_to_all x1, waiting for transfers between devices: 9.04 us -> 6.69 us  [on_device(): lax.all_to_all(pair, 'z', 0, 0, tiled=True).reshape(2 * N_Z, TILE, F)]
  transfers between devices with their start and end apart: 23 -> 26, of which waited for: 18 -> 16; matrix products, arithmetic and copies ran while one was open for 4% -> 4% of each run, Pallas kernels for 6% -> 9%
where the time goes in v5:
time: 184 us; the launch traced here: 182 us
  waiting for transfers between devices  76.6 us (42%)
  starting transfers between devices  44 us (24%)
  Pallas kernels  25.6 us (14%)
  blocking collectives  23.7 us (13%)
  other arithmetic  6.6 us (4%)
  local copies, waits for them, and re-layouts  3.49 us (2%)
    ppermute x17, waiting for transfers between devices, xor_swap(): return lax.ppermute(x, axis, [(i, i ^ bit) for i in range(n)])  38.2 us
    all_to_all x1, blocking collectives, on_device(): parts = lax.all_to_all(partial, REP, 0, 0, tiled=True)  23.7 us
    ppermute x17, starting transfers between devices, xor_swap(): return lax.ppermute(x, axis, [(i, i ^ bit) for i in range(n)])  14.8 us
    all_to_all x1, waiting for transfers between devices, on_device(): near0 = lax.all_to_all(first, 'z', 0, 0, tiled=True)  13.8 us
    pallas_call x3, Pallas kernels, backward(): pl.pallas_call(lambda *refs: backward_kernel(ranges, *refs), out_shape=[s...  11.2 us
    pallas_call x3, Pallas kernels, call(): pl.pallas_call(kernel, out_shape=out_shape, in_specs=[smem, hbm] + [vmem]...  11.2 us
    all_to_all x1, starting transfers between devices, on_device(): near0 = lax.all_to_all(first, 'z', 0, 0, tiled=True)  9.01 us
    all_to_all x1, waiting for transfers between devices, on_device(): lax.all_to_all(pair.reshape(N_Z, 2, TILE, F), 'z', 0, 0, tiled=True)  8.39 us
  transfers between devices with their start and end apart: 26, of which 16 were waited for; matrix products, arithmetic and copies ran while one was open for 4% of the time, Pallas kernels for 9%

profile of v5, /device:TPU:1, one launch (start us, length us, event | category | flops | bytes accessed | tf_op | source)
XLA Modules:
  0.0 181.5 jit_solution(15708976687902073799)
XLA Ops:
  2.4 9.0 %all-to-all-start = ((bf16[8,128,256]{2,1,0:T(8,128)(2,1)}), bf16[8,128,256]{2,1,0:T(8,128)(2,1)S(1)}, u32[]{:S(2)}, u32[]{:S(2)}) async-start(bf16[8,128,256]{2,1,0:T(8,128)(2,1)} %broadcast_in_dim.18), calls=%async_computation | async-start | bytes 1048576 | tf_op jit(solution)/shard_map/gather_features/all_to_all | solution.py:225
  15.6 13.8 %all-to-all-done.near0 = bf16[8,128,256]{2,1,0:T(8,128)(2,1)S(1)} async-done(((bf16[8,128,256]{2,1,0:T(8,128)(2,1)}), bf16[8,128,256]{2,1,0:T(8,128)(2,1)S(1)}, u32[]{:S(2)}, u32[]{:S(2)}) %all-to-all-start) | async-done | bytes 524320 | tf_op jit(solution)/shard_map/gather_features/all_to_all | solution.py:225
  29.3 3.6 %all-to-all-start.1 = ((bf16[8,2,128,256]{3,2,1,0:T(8,128)(2,1)}), bf16[8,2,128,256]{3,2,1,0:T(8,128)(2,1)S(1)}, u32[]{:S(2)}, u32[]{:S(2)}) async-start(bf16[8,2,128,256]{3,2,1,0:T(8,128)(2,1)} %pair_copies.1), calls=%async_computation.1 | async-start | bytes 2097152 | tf_op jit(solution)/shard_map/gather_features/all_to_all | solution.py:237
  35.0 11.0 %collective-permute-done.1.near1 = bf16[8,128,256]{2,1,0:T(8,128)(2,1)S(1)} collective-permute-done((bf16[8,128,256]{2,1,0:T(8,128)(2,1)S(1)}, bf16[8,128,256]{2,1,0:T(8,128)(2,1)S(1)}, u32[]{:S(2)}, u32[]{:S(2)}) %collective-permute-start.1) | collective-permute-done | bytes 524320 | tf_op jit(solution)/shard_map/gather_features/ppermute | solution.py:29
  47.3 1.5 collective-permute-done.3.far1
  49.9 5.4 %tile_products_first.1.before = f32[17,128,256]{2,1,0:T(8,128)S(1)} custom-call(s32[2,256]{1,0:T(2,128)S(1)} %concatenate.6.table.refs_0_, bf16[128,128,128]{2,1,0:T(8,128)(2,1)} %bitcast.64, bf16[8,128,256]{2,1,0:T(8,128)(2,1)S(1)} %copy-done.1, bf16[8,128,256]{2,1,0:T(8,128)(2,1)S(1)} %collective-permute-done.1.near1, ...), custom_call_target="tpu_custom_call" | custom-call | flops 1 | bytes 1 | tf_op jit(solution)/shard_map/tile_products/tile_products_first/pallas_call | solution.py:210
  55.4 6.7 %all-to-all-done.1 = bf16[8,2,128,256]{3,2,1,0:T(8,128)(2,1)S(1)} async-done(((bf16[8,2,128,256]{3,2,1,0:T(8,128)(2,1)}), bf16[8,2,128,256]{3,2,1,0:T(8,128)(2,1)S(1)}, u32[]{:S(2)}, u32[]{:S(2)}) %all-to-all-start.1) | async-done | bytes 1048608 | tf_op jit(solution)/shard_map/gather_features/all_to_all | solution.py:237
  62.5 2.8 %tile_products_second.1.before = f32[17,128,256]{2,1,0:T(8,128)S(1)} custom-call(s32[2,256]{1,0:T(2,128)S(1)} %concatenate.6.table.refs_0_, bf16[128,128,128]{2,1,0:T(8,128)(2,1)} %bitcast.65, bf16[16,128,256]{2,1,0:T(8,128)(2,1)S(1)} %bitcast.62, f32[17,128,256]{2,1,0:T(8,128)S(1)} %tile_products_first.1.before), custom_call_target="tpu_custom_call" | custom-call | flops 1 | bytes 1 | tf_op jit(solution)/shard_map/tile_products/tile_products_second/pallas_call | solution.py:210
  65.4 2.9 %tile_products_last.1 = bf16[8,256,256]{2,1,0:T(8,128)(2,1)S(1)} custom-call(s32[2,256]{1,0:T(2,128)S(1)} %concatenate.6.table.refs_0_, bf16[128,128,128]{2,1,0:T(8,128)(2,1)} %bitcast.66, bf16[16,128,256]{2,1,0:T(8,128)(2,1)S(1)} %collective-permute-done.4.feats, f32[17,128,256]{2,1,0:T(8,128)S(1)} %tile_products_second.1.before), custom_call_target="tpu_custom_call" | custom-call | flops 1 | bytes 1 | tf_op jit(solution)/shard_map/tile_products/tile_products_last/pallas_call | solution.py:210
  68.3 23.7 %all_to_all.30.parts = bf16[8,256,256]{2,1,0:T(8,128)(2,1)S(1)} all-to-all(bf16[8,256,256]{2,1,0:T(8,128)(2,1)S(1)} %tile_products_last.1), channel_id=1, replica_groups=mesh['y'=4,'xh'=2,'z'=8,'xl'=2,'core'=2] {'y','xh'}, dimensions={0} | all-to-all | bytes 2097152 | tf_op jit(solution)/shard_map/sum_partials/all_to_all | solution.py:257
  93.4 3.6 %all-to-all-start.3 = ((bf16[8,256,256]{2,1,0:T(8,128)(2,1)}), bf16[8,256,256]{2,1,0:T(8,128)(2,1)S(1)}, u32[]{:S(2)}, u32[]{:S(2)}) async-start(bf16[8,256,256]{2,1,0:T(8,128)(2,1)} %get-tuple-element.29), calls=%async_computation.3 | async-start | bytes 2097152 | tf_op jit(solution)/shard_map/share_gradients/all_to_all | solution.py:275
  97.1 1.7 collective-permute-start.7
  99.0 1.8 collective-permute-done.6
  100.7 1.9 %collective-permute-done.7 = bf16[128,256]{1,0:T(8,128)(2,1)S(1)} collective-permute-done((bf16[128,256]{1,0:T(8,128)(2,1)S(1)}, bf16[128,256]{1,0:T(8,128)(2,1)S(1)}, u32[]{:S(2)}, u32[]{:S(2)}) %collective-permute-start.7) | collective-permute-done | bytes 65568 | tf_op jit(solution)/shard_map/weight_z/ppermute | solution.py:279
  102.8 6.3 %collective-permute-done.8 = bf16[128,256]{1,0:T(8,128)(2,1)S(1)} collective-permute-done((bf16[128,256]{1,0:T(8,128)(2,1)S(1)}, bf16[128,256]{1,0:T(8,128)(2,1)S(1)}, u32[]{:S(2)}, u32[]{:S(2)}) %collective-permute-start.8) | collective-permute-done | bytes 65568 | tf_op jit(solution)/shard_map/weight_z/ppermute | solution.py:29
  109.6 6.6 %collective-permute-done.9 = bf16[128,256]{1,0:T(8,128)(2,1)S(1)} collective-permute-done((bf16[128,256]{1,0:T(8,128)(2,1)S(1)}, bf16[128,256]{1,0:T(8,128)(2,1)S(1)}, u32[]{:S(2)}, u32[]{:S(2)}) %collective-permute-start.9) | collective-permute-done | bytes 65568 | tf_op jit(solution)/shard_map/weight_z/ppermute | solution.py:29
  116.3 5.1 %back_far.1 = (bf16[16,128,256]{2,1,0:T(8,128)(2,1)S(1)}, bf16[16,128,256]{2,1,0:T(8,128)(2,1)S(1)}) custom-call(s32[2,256]{1,0:T(2,128)S(1)} %concatenate.6.table.refs_0_, bf16[128,128,128]{2,1,0:T(8,128)(2,1)} %bitcast.67, bf16[8,256,256]{2,1,0:T(8,128)(2,1)S(1)} %all-to-all-done.3.refs_2_), custom_call_target="tpu_custom_call" | custom-call | flops 1 | bytes 1 | tf_op jit(solution)/shard_map/back_second/back_far/pallas_call | solution.py:288
  122.0 3.1 %back_second_near.1 = bf16[16,128,256]{2,1,0:T(8,128)(2,1)S(1)} custom-call(s32[2,256]{1,0:T(2,128)S(1)} %concatenate.6.table.refs_0_, bf16[128,128,128]{2,1,0:T(8,128)(2,1)} %bitcast.68, bf16[8,256,256]{2,1,0:T(8,128)(2,1)S(1)} %all-to-all-done.3.refs_2_), custom_call_target="tpu_custom_call" | custom-call | flops 1 | bytes 1 | tf_op jit(solution)/shard_map/back_second/back_second_near/pallas_call | solution.py:288
  126.7 3.6 %all-to-all-start.4 = ((bf16[8,2,128,256]{3,2,1,0:T(8,128)(2,1)}), bf16[8,2,128,256]{3,2,1,0:T(8,128)(2,1)S(1)}, u32[]{:S(2)}, u32[]{:S(2)}) async-start(bf16[8,2,128,256]{3,2,1,0:T(8,128)(2,1)} %bitcast.15), calls=%async_computation.4 | async-start | bytes 2097152 | tf_op jit(solution)/shard_map/back_second/all_to_all | solution.py:310
  131.0 3.1 %back_first_near.1 = bf16[16,128,256]{2,1,0:T(8,128)(2,1)S(1)} custom-call(s32[2,256]{1,0:T(2,128)S(1)} %concatenate.6.table.refs_0_, bf16[128,128,128]{2,1,0:T(8,128)(2,1)} %bitcast.69, bf16[8,256,256]{2,1,0:T(8,128)(2,1)S(1)} %all-to-all-done.3.refs_2_, bf16[16,256]{1,0:T(8,128)(2,1)S(1)} %slice.37.refs_3_), custom_call_target="tpu_custom_call" | custom-call | flops 1 | bytes 1 | tf_op jit(solution)/shard_map/back_first/back_first_near/pallas_call | solution.py:288
  135.6 2.9 %collective-permute-start.15 = (bf16[128,256]{1,0:T(8,128)(2,1)S(1)}, bf16[128,256]{1,0:T(8,128)(2,1)S(1)}, u32[]{:S(2)}, u32[]{:S(2)}) collective-permute-start(bf16[128,256]{1,0:T(8,128)(2,1)S(1)} %add_convert_fusion.5), channel_id=1, source_target_pairs={{0,192},{64,128},{128,64},{192,0},{1,193},{65,129},{129,65},{193,1... | collective-permute-start | bytes 196616 | tf_op jit(solution)/shard_map/back_first/ppermute | solution.py:29
  139.2 1.8 collective-permute-done.15
  141.0 2.4 %collective-permute-done.14 = bf16[128,256]{1,0:T(8,128)(2,1)S(1)} collective-permute-done((bf16[128,256]{1,0:T(8,128)(2,1)S(1)}, bf16[128,256]{1,0:T(8,128)(2,1)S(1)}, u32[]{:S(2)}, u32[]{:S(2)}) %collective-permute-start.14) | collective-permute-done | bytes 65568 | tf_op jit(solution)/shard_map/back_first/ppermute | solution.py:29
  143.5 5.5 %collective-permute-done.12 = bf16[8,128,256]{2,1,0:T(8,128)(2,1)S(1)} collective-permute-done((bf16[8,128,256]{2,1,0:T(8,128)(2,1)S(1)}, bf16[8,128,256]{2,1,0:T(8,128)(2,1)S(1)}, u32[]{:S(2)}, u32[]{:S(2)}) %collective-permute-start.12) | collective-permute-done | bytes 524320 | tf_op jit(solution)/shard_map/back_first/ppermute | solution.py:29
  149.0 2.0 %add_convert_fusion.1 = bf16[8,128,256]{2,1,0:T(8,128)(2,1)} fusion(bf16[8,128,256]{2,1,0:T(8,128)(2,1)S(1)} %collective-permute-done.12, bf16[16,128,256]{2,1,0:T(8,128)(2,1)} %collective-permute-done.11, bf16[16,128,256]{2,1,0:T(8,128)(2,1)S(1)} %back_first_near.1), kind=kLoop, calls=%fused_computation.2 | loop fusion | flops 1572864 | bytes 2097152 | tf_op jit(solution)/shard_map/back_first/convert_element_type | solution.py:318
  151.0 8.4 %all-to-all-done.4 = bf16[8,2,128,256]{3,2,1,0:T(8,128)(2,1)S(1)} async-done(((bf16[8,2,128,256]{3,2,1,0:T(8,128)(2,1)}), bf16[8,2,128,256]{3,2,1,0:T(8,128)(2,1)S(1)}, u32[]{:S(2)}, u32[]{:S(2)}) %all-to-all-start.4) | async-done | bytes 1048608 | tf_op jit(solution)/shard_map/back_second/all_to_all | solution.py:310
  159.4 3.5 %all-to-all-start.5 = ((bf16[8,128,256]{2,1,0:T(8,128)(2,1)}), bf16[8,128,256]{2,1,0:T(8,128)(2,1)S(1)}, u32[]{:S(2)}, u32[]{:S(2)}) async-start(bf16[8,128,256]{2,1,0:T(8,128)(2,1)} %add_convert_fusion.1), calls=%async_computation.5 | async-start | bytes 1048576 | tf_op jit(solution)/shard_map/back_first/all_to_all | solution.py:320
  163.1 3.6 %collective-permute-start.18 = (bf16[128,256]{1,0:T(8,128)(2,1)S(1)}, bf16[128,256]{1,0:T(8,128)(2,1)S(1)}, u32[]{:S(2)}, u32[]{:S(2)}) collective-permute-start(bf16[128,256]{1,0:T(8,128)(2,1)S(1)} %add_convert_fusion.4), channel_id=1, source_target_pairs={{0,34},{2,32},{32,2},{34,0},{1,35},{3,33},{33,3},{35,1},{4,38},{6,... | collective-permute-start | bytes 196616 | tf_op jit(solution)/shard_map/weight_rest/ppermute | solution.py:330
  167.4 1.5 collective-permute-start.20
  169.0 2.6 %collective-permute-done.17 = bf16[128,256]{1,0:T(8,128)(2,1)S(1)} collective-permute-done((bf16[128,256]{1,0:T(8,128)(2,1)S(1)}, bf16[128,256]{1,0:T(8,128)(2,1)S(1)}, u32[]{:S(2)}, u32[]{:S(2)}) %collective-permute-start.17) | collective-permute-done | bytes 65568 | tf_op jit(solution)/shard_map/weight_rest/ppermute | solution.py:330
  171.6 2.4 %collective-permute-start.19 = (bf16[128,256]{1,0:T(8,128)(2,1)S(1)}, bf16[128,256]{1,0:T(8,128)(2,1)S(1)}, u32[]{:S(2)}, u32[]{:S(2)}) collective-permute-start(bf16[128,256]{1,0:T(8,128)(2,1)S(1)} %add_convert_fusion.3.mine), channel_id=1, source_target_pairs={{0,1},{1,0},{2,3},{3,2},{4,5},{5,4},{6,7},{7,6},{8,9},{9,8},{10,11... | collective-permute-start | bytes 196616 | tf_op jit(solution)/shard_map/weight_rest/ppermute | solution.py:29
  175.7 5.1 %all-to-all-done.5 = bf16[8,128,256]{2,1,0:T(8,128)(2,1)S(1)} async-done(((bf16[8,128,256]{2,1,0:T(8,128)(2,1)}), bf16[8,128,256]{2,1,0:T(8,128)(2,1)S(1)}, u32[]{:S(2)}, u32[]{:S(2)}) %all-to-all-start.5) | async-done | bytes 524320 | tf_op jit(solution)/shard_map/back_first/all_to_all | solution.py:320
  (59 shorter events, 21.0 us)
Async XLA Ops:
  2.4 27.0 %all-to-all-start = ((bf16[8,128,256]{2,1,0:T(8,128)(2,1)}), bf16[8,128,256]{2,1,0:T(8,128)(2,1)S(1)}, u32[]{:S(2)}, u32[]{:S(2)}) async-start(bf16[8,128,256]{2,1,0:T(8,128)(2,1)} %broadcast_in_dim.18), calls=%async_computation | async-start | bytes 1048576 | tf_op jit(solution)/shard_map/gather_features/all_to_all | solution.py:225
  11.4 3.1 %collective-permute-start = (bf16[128,256]{1,0:T(8,128)(2,1)S(1)}, bf16[128,256]{1,0:T(8,128)(2,1)S(1)}, u32[]{:S(2)}, u32[]{:S(2)}) collective-permute-start(bf16[128,256]{1,0:T(8,128)(2,1)S(1)} %get-tuple-element.45.own), channel_id=1, source_target_pairs={{0,2},{2,0},{1,3},{3,1},{4,6},{6,4},{5,7},{7,5},{8,10},{10,8},{9,1... | collective-permute-start | bytes 196616 | tf_op jit(solution)/shard_map/gather_features/ppermute | solution.py:29
  29.3 19.5 %copy-start = (bf16[8,128,256]{2,1,0:T(8,128)(2,1)}, bf16[8,128,256]{2,1,0:T(8,128)(2,1)S(1)}, u32[]{:S(2)}) copy-start(bf16[8,128,256]{2,1,0:T(8,128)(2,1)S(1)} %all-to-all-done.near0) | copy-start | bytes 1572868
  29.3 32.7 %all-to-all-start.1 = ((bf16[8,2,128,256]{3,2,1,0:T(8,128)(2,1)}), bf16[8,2,128,256]{3,2,1,0:T(8,128)(2,1)S(1)}, u32[]{:S(2)}, u32[]{:S(2)}) async-start(bf16[8,2,128,256]{3,2,1,0:T(8,128)(2,1)} %pair_copies.1), calls=%async_computation.1 | async-start | bytes 2097152 | tf_op jit(solution)/shard_map/gather_features/all_to_all | solution.py:237
  32.9 13.1 %collective-permute-start.1 = (bf16[8,128,256]{2,1,0:T(8,128)(2,1)S(1)}, bf16[8,128,256]{2,1,0:T(8,128)(2,1)S(1)}, u32[]{:S(2)}, u32[]{:S(2)}) collective-permute-start(bf16[8,128,256]{2,1,0:T(8,128)(2,1)S(1)} %all-to-all-done.near0), channel_id=1, source_target_pairs={{0,2},{2,0},{1,3},{3,1},{4,6},{6,4},{5,7},{7,5},{8,10},{10,8},{9,1... | collective-permute-start | bytes 1572872 | tf_op jit(solution)/shard_map/gather_features/ppermute | solution.py:29
  34.2 13.1 %collective-permute-start.2 = (bf16[8,128,256]{2,1,0:T(8,128)(2,1)S(1)}, bf16[8,128,256]{2,1,0:T(8,128)(2,1)S(1)}, u32[]{:S(2)}, u32[]{:S(2)}) collective-permute-start(bf16[8,128,256]{2,1,0:T(8,128)(2,1)S(1)} %all-to-all-done.near0), channel_id=1, source_target_pairs={{0,1},{1,0},{2,3},{3,2},{4,5},{5,4},{6,7},{7,6},{8,9},{9,8},{10,11... | collective-permute-start | bytes 1572872 | tf_op jit(solution)/shard_map/gather_features/ppermute | solution.py:29
  46.0 2.9 %collective-permute-start.3 = (bf16[8,128,256]{2,1,0:T(8,128)(2,1)S(1)}, bf16[8,128,256]{2,1,0:T(8,128)(2,1)S(1)}, u32[]{:S(2)}, u32[]{:S(2)}) collective-permute-start(bf16[8,128,256]{2,1,0:T(8,128)(2,1)S(1)} %collective-permute-done.1.near1), channel_id=1, source_target_pairs={{0,1},{1,0},{2,3},{3,2},{4,5},{5,4},{6,7},{7,6},{8,9},{9,8},{10,11... | collective-permute-start | bytes 1572872 | tf_op jit(solution)/shard_map/gather_features/ppermute | solution.py:29
  48.9 1.0 copy-start.1
  62.0 3.3 %collective-permute-start.4 = (bf16[16,128,256]{2,1,0:T(8,128)(2,1)S(1)}, bf16[16,128,256]{2,1,0:T(8,128)(2,1)S(1)}, u32[]{:S(2)}, u32[]{:S(2)}) collective-permute-start(bf16[16,128,256]{2,1,0:T(8,128)(2,1)S(1)} %bitcast.61), channel_id=1, source_target_pairs={{0,1},{1,0},{2,3},{3,2},{4,5},{5,4},{6,7},{7,6},{8,9},{9,8},{10,11... | collective-permute-start | bytes 3145736 | tf_op jit(solution)/shard_map/tile_products/ppermute | solution.py:29
  68.3 23.7 %copy-start.2 = (bf16[256,256]{1,0:T(8,128)(2,1)S(1)}, bf16[256,256]{1,0:T(8,128)(2,1)}, u32[]{:S(2)}) copy-start(bf16[256,256]{1,0:T(8,128)(2,1)} %weight.1) | copy-start | bytes 393220
  68.3 23.7 %copy-start.3 = (bf16[1,1,256,256]{3,2,1,0:T(8,128)(2,1)S(1)}, bf16[1,1,256,256]{3,2,1,0:T(8,128)(2,1)}, u32[]{:S(2)}) copy-start(bf16[1,1,256,256]{3,2,1,0:T(8,128)(2,1)} %param.13) | copy-start | bytes 393220
  93.4 22.8 %all-to-all-start.3 = ((bf16[8,256,256]{2,1,0:T(8,128)(2,1)}), bf16[8,256,256]{2,1,0:T(8,128)(2,1)S(1)}, u32[]{:S(2)}, u32[]{:S(2)}) async-start(bf16[8,256,256]{2,1,0:T(8,128)(2,1)} %get-tuple-element.29), calls=%async_computation.3 | async-start | bytes 2097152 | tf_op jit(solution)/shard_map/share_gradients/all_to_all | solution.py:275
  97.0 3.7 %collective-permute-start.6 = (bf16[128,256]{1,0:T(8,128)(2,1)S(1)}, bf16[128,256]{1,0:T(8,128)(2,1)S(1)}, u32[]{:S(2)}, u32[]{:S(2)}) collective-permute-start(bf16[128,256]{1,0:T(8,128)(2,1)S(1)} %get-tuple-element.30), channel_id=1, source_target_pairs={{0,4},{4,0},{8,12},{12,8},{16,20},{20,16},{24,28},{28,24},{1,5},{5... | collective-permute-start | bytes 196616 | tf_op jit(solution)/shard_map/weight_z/ppermute | solution.py:29
  97.1 5.5 %collective-permute-start.7 = (bf16[128,256]{1,0:T(8,128)(2,1)S(1)}, bf16[128,256]{1,0:T(8,128)(2,1)S(1)}, u32[]{:S(2)}, u32[]{:S(2)}) collective-permute-start(bf16[128,256]{1,0:T(8,128)(2,1)S(1)} %get-tuple-element.31), channel_id=1, source_target_pairs={{0,5},{1,4},{4,1},{5,0},{8,13},{9,12},{12,9},{13,8},{16,21},{17,20... | collective-permute-start | bytes 196616 | tf_op jit(solution)/shard_map/weight_z/ppermute | solution.py:279
  98.8 3.8 %collective-permute-start.5 = (bf16[128,256]{1,0:T(8,128)(2,1)S(1)}, bf16[128,256]{1,0:T(8,128)(2,1)S(1)}, u32[]{:S(2)}, u32[]{:S(2)}) collective-permute-start(bf16[128,256]{1,0:T(8,128)(2,1)S(1)} %get-tuple-element.31), channel_id=1, source_target_pairs={{0,1},{1,0},{2,3},{3,2},{4,5},{5,4},{6,7},{7,6},{8,9},{9,8},{10,11... | collective-permute-start | bytes 196616 | tf_op jit(solution)/shard_map/weight_z/ppermute | solution.py:29
  102.7 6.4 %collective-permute-start.8 = (bf16[128,256]{1,0:T(8,128)(2,1)S(1)}, bf16[128,256]{1,0:T(8,128)(2,1)S(1)}, u32[]{:S(2)}, u32[]{:S(2)}) collective-permute-start(bf16[128,256]{1,0:T(8,128)(2,1)S(1)} %add_convert_fusion.7), channel_id=1, source_target_pairs={{0,8},{4,12},{8,0},{12,4},{16,24},{20,28},{24,16},{28,20},{1,9},{5... | collective-permute-start | bytes 196616 | tf_op jit(solution)/shard_map/weight_z/ppermute | solution.py:29
  109.1 7.2 %collective-permute-start.9 = (bf16[128,256]{1,0:T(8,128)(2,1)S(1)}, bf16[128,256]{1,0:T(8,128)(2,1)S(1)}, u32[]{:S(2)}, u32[]{:S(2)}) collective-permute-start(bf16[128,256]{1,0:T(8,128)(2,1)S(1)} %add_convert_fusion.6), channel_id=1, source_target_pairs={{0,16},{4,20},{8,24},{12,28},{16,0},{20,4},{24,8},{28,12},{1,17},{... | collective-permute-start | bytes 196616 | tf_op jit(solution)/shard_map/weight_z/ppermute | solution.py:29
  121.4 4.0 %collective-permute-start.10 = (bf16[16,128,256]{2,1,0:T(8,128)(2,1)S(1)}, bf16[16,128,256]{2,1,0:T(8,128)(2,1)S(1)}, u32[]{:S(2)}, u32[]{:S(2)}) collective-permute-start(bf16[16,128,256]{2,1,0:T(8,128)(2,1)S(1)} %get-tuple-element.33), channel_id=1, source_target_pairs={{0,1},{1,0},{2,3},{3,2},{4,5},{5,4},{6,7},{7,6},{8,9},{9,8},{10,11... | collective-permute-start | bytes 3145736 | tf_op jit(solution)/shard_map/back_second/ppermute | solution.py:29
  125.1 9.0 %collective-permute-start.11 = (bf16[16,128,256]{2,1,0:T(8,128)(2,1)S(1)}, bf16[16,128,256]{2,1,0:T(8,128)(2,1)}, u32[]{:S(2)}, u32[]{:S(2)}) collective-permute-start(bf16[16,128,256]{2,1,0:T(8,128)(2,1)S(1)} %get-tuple-element.36), channel_id=1, source_target_pairs={{0,1},{1,0},{2,3},{3,2},{4,5},{5,4},{6,7},{7,6},{8,9},{9,8},{10,11... | collective-permute-start | bytes 3145736 | tf_op jit(solution)/shard_map/back_second/ppermute | solution.py:29
  126.7 32.7 %all-to-all-start.4 = ((bf16[8,2,128,256]{3,2,1,0:T(8,128)(2,1)}), bf16[8,2,128,256]{3,2,1,0:T(8,128)(2,1)S(1)}, u32[]{:S(2)}, u32[]{:S(2)}) async-start(bf16[8,2,128,256]{3,2,1,0:T(8,128)(2,1)} %bitcast.15), calls=%async_computation.4 | async-start | bytes 2097152 | tf_op jit(solution)/shard_map/back_second/all_to_all | solution.py:310
  135.2 13.8 %collective-permute-start.12 = (bf16[8,128,256]{2,1,0:T(8,128)(2,1)S(1)}, bf16[8,128,256]{2,1,0:T(8,128)(2,1)S(1)}, u32[]{:S(2)}, u32[]{:S(2)}) collective-permute-start(bf16[8,128,256]{2,1,0:T(8,128)(2,1)S(1)} %add_convert_fusion.2), channel_id=1, source_target_pairs={{0,2},{2,0},{1,3},{3,1},{4,6},{6,4},{5,7},{7,5},{8,10},{10,8},{9,1... | collective-permute-start | bytes 1572872 | tf_op jit(solution)/shard_map/back_first/ppermute | solution.py:29
  135.6 5.4 %collective-permute-start.15 = (bf16[128,256]{1,0:T(8,128)(2,1)S(1)}, bf16[128,256]{1,0:T(8,128)(2,1)S(1)}, u32[]{:S(2)}, u32[]{:S(2)}) collective-permute-start(bf16[128,256]{1,0:T(8,128)(2,1)S(1)} %add_convert_fusion.5), channel_id=1, source_target_pairs={{0,192},{64,128},{128,64},{192,0},{1,193},{65,129},{129,65},{193,1... | collective-permute-start | bytes 196616 | tf_op jit(solution)/shard_map/back_first/ppermute | solution.py:29
  138.5 4.9 %collective-permute-start.14 = (bf16[128,256]{1,0:T(8,128)(2,1)S(1)}, bf16[128,256]{1,0:T(8,128)(2,1)S(1)}, u32[]{:S(2)}, u32[]{:S(2)}) collective-permute-start(bf16[128,256]{1,0:T(8,128)(2,1)S(1)} %add_convert_fusion.5), channel_id=1, source_target_pairs={{0,128},{64,192},{128,0},{192,64},{1,129},{65,193},{129,1},{193,65... | collective-permute-start | bytes 196616 | tf_op jit(solution)/shard_map/back_first/ppermute | solution.py:29
  139.0 4.4 %collective-permute-start.13 = (bf16[128,256]{1,0:T(8,128)(2,1)S(1)}, bf16[128,256]{1,0:T(8,128)(2,1)S(1)}, u32[]{:S(2)}, u32[]{:S(2)}) collective-permute-start(bf16[128,256]{1,0:T(8,128)(2,1)S(1)} %add_convert_fusion.5), channel_id=1, source_target_pairs={{0,64},{64,0},{128,192},{192,128},{1,65},{65,1},{129,193},{193,129... | collective-permute-start | bytes 196616 | tf_op jit(solution)/shard_map/back_first/ppermute | solution.py:29
  159.4 21.4 %all-to-all-start.5 = ((bf16[8,128,256]{2,1,0:T(8,128)(2,1)}), bf16[8,128,256]{2,1,0:T(8,128)(2,1)S(1)}, u32[]{:S(2)}, u32[]{:S(2)}) async-start(bf16[8,128,256]{2,1,0:T(8,128)(2,1)} %add_convert_fusion.1), calls=%async_computation.5 | async-start | bytes 1048576 | tf_op jit(solution)/shard_map/back_first/all_to_all | solution.py:320
  163.1 5.9 %collective-permute-start.18 = (bf16[128,256]{1,0:T(8,128)(2,1)S(1)}, bf16[128,256]{1,0:T(8,128)(2,1)S(1)}, u32[]{:S(2)}, u32[]{:S(2)}) collective-permute-start(bf16[128,256]{1,0:T(8,128)(2,1)S(1)} %add_convert_fusion.4), channel_id=1, source_target_pairs={{0,34},{2,32},{32,2},{34,0},{1,35},{3,33},{33,3},{35,1},{4,38},{6,... | collective-permute-start | bytes 196616 | tf_op jit(solution)/shard_map/weight_rest/ppermute | solution.py:330
  166.7 4.9 %collective-permute-start.17 = (bf16[128,256]{1,0:T(8,128)(2,1)S(1)}, bf16[128,256]{1,0:T(8,128)(2,1)S(1)}, u32[]{:S(2)}, u32[]{:S(2)}) collective-permute-start(bf16[128,256]{1,0:T(8,128)(2,1)S(1)} %add_convert_fusion.4), channel_id=1, source_target_pairs={{0,32},{2,34},{32,0},{34,2},{1,33},{3,35},{33,1},{35,3},{4,36},{6,... | collective-permute-start | bytes 196616 | tf_op jit(solution)/shard_map/weight_rest/ppermute | solution.py:330
  167.4 4.2 %collective-permute-start.16 = (bf16[128,256]{1,0:T(8,128)(2,1)S(1)}, bf16[128,256]{1,0:T(8,128)(2,1)S(1)}, u32[]{:S(2)}, u32[]{:S(2)}) collective-permute-start(bf16[128,256]{1,0:T(8,128)(2,1)S(1)} %add_convert_fusion.4), channel_id=1, source_target_pairs={{0,2},{2,0},{32,34},{34,32},{1,3},{3,1},{33,35},{35,33},{4,6},{6,4... | collective-permute-start | bytes 196616 | tf_op jit(solution)/shard_map/weight_rest/ppermute | solution.py:330
  167.4 6.6 %collective-permute-start.20 = (bf16[128,256]{1,0:T(8,128)(2,1)S(1)}, bf16[128,256]{1,0:T(8,128)(2,1)S(1)}, u32[]{:S(2)}, u32[]{:S(2)}) collective-permute-start(bf16[128,256]{1,0:T(8,128)(2,1)S(1)} %fusion.1), channel_id=1, source_target_pairs={{0,2},{2,0},{1,3},{3,1},{4,6},{6,4},{5,7},{7,5},{8,10},{10,8},{9,1... | collective-permute-start | bytes 196616 | tf_op jit(solution)/shard_map/grad_features/ppermute | solution.py:29
  171.6 3.3 %collective-permute-start.19 = (bf16[128,256]{1,0:T(8,128)(2,1)S(1)}, bf16[128,256]{1,0:T(8,128)(2,1)S(1)}, u32[]{:S(2)}, u32[]{:S(2)}) collective-permute-start(bf16[128,256]{1,0:T(8,128)(2,1)S(1)} %add_convert_fusion.3.mine), channel_id=1, source_target_pairs={{0,1},{1,0},{2,3},{3,2},{4,5},{5,4},{6,7},{7,6},{8,9},{9,8},{10,11... | collective-permute-start | bytes 196616 | tf_op jit(solution)/shard_map/weight_rest/ppermute | solution.py:29

commit v6 on v5

v6 whole, which is shorter than its diff:
```python
import jax
import jax.numpy as jnp
import numpy as np
from jax import lax
from jax.experimental import pallas as pl
from jax.experimental.pallas import tpu as pltpu
from jax.sharding import Mesh
from jax.sharding import PartitionSpec as P

REP = ("y", "xh")
BLK = ("z", "xl", "core")
N_Z = 8
N_Y = 4
TILE = 128
F = 256
XR = 256
N_REP = 8
SLOTS = 128
ROW_BLOCKS = 16
UNROLL = 8
HALF = XR // 2
CLASSES = 2
CHUNKS = 2 * N_Z

f32 = jnp.float32
bf16 = jnp.bfloat16
VMEM_LIMIT = 16 << 20


def xor_swap(x, axis, n, bit):
    return lax.ppermute(x, axis, [(i, i ^ bit) for i in range(n)])


def add_swapped(x, axis, n, bit):
    return (x.astype(f32) + xor_swap(x, axis, n, bit).astype(f32)).astype(bf16)


def shift(x, step):
    return lax.ppermute(x, "z", [(i, (i + step) % N_Z) for i in range(N_Z)])


def slot_table(rows, cols, count, my_z, my_xl, my_core):
    owner = cols >> 1
    dz = ((owner >> 2) - my_z) & (N_Z - 1)
    dx = ((owner >> 1) & 1) ^ my_xl
    dc = (owner & 1) ^ my_core
    position = jnp.arange(SLOTS, dtype=jnp.int32)
    kind = jnp.where(position < count, dc, CLASSES)
    place = ((dx * N_Z + dz) << 1) | (cols & 1)
    packed = rows | (place << 8) | (position << 16)
    key = kind * SLOTS + position
    rank = jnp.sum((key[None, :] < key[:, None]).astype(jnp.int32), axis=1)
    ordered = jnp.sum(jnp.where(rank[None, :] == position[:, None], packed[None, :], 0), axis=1)
    starts = jnp.sum((kind[None, :] < position[:, None]).astype(jnp.int32), axis=1)
    return jnp.concatenate([jnp.stack([ordered, starts]), jnp.zeros((2, SLOTS), jnp.int32)], axis=1)


def slot_range(table, first, last):
    begin = table[1, first]
    return begin, (table[1, last] - begin + UNROLL - 1) // UNROLL


def start_tiles(table, first, last, tiles_hbm, tiles, sems):
    begin, rounds = slot_range(table, first, last)

    def start(i, carry):
        for u in range(UNROLL):
            at = i * UNROLL + u
            pltpu.make_async_copy(tiles_hbm.at[table[0, begin + at] >> 16], tiles.at[at], sems.at[i]).start()
        return carry

    lax.fori_loop(0, rounds, start, 0)


def slot_loop(table, first, last, tiles_hbm, tiles, sems, one_slot):
    begin, rounds = slot_range(table, first, last)
    end = table[1, last]

    def step(i, carry):
        pltpu.make_async_copy(
            tiles_hbm.at[pl.ds(0, UNROLL)], tiles.at[pl.ds(i * UNROLL, UNROLL)], sems.at[i]
        ).wait()
        for u in range(UNROLL):
            t = begin + i * UNROLL + u
            packed = table[0, t]
            one_slot(t < end, packed & 255, (packed >> 8) & 255, tiles[i * UNROLL + u])
        return carry

    lax.fori_loop(0, rounds, step, 0)


def tile_of(ref, which):
    return ref[which >> 1, pl.ds(pl.multiple_of((which & 1) * TILE, TILE), TILE), :]


def assemble_kernel(*refs):
    out, sems = refs[-2:]
    copies = []
    for n, src in enumerate(refs[:-2]):
        dx, k = divmod(n, N_Z + 1)
        if k < 4:
            dst = out.at[dx * N_Z + k]
        elif k < 6:
            dst = out.at[dx * N_Z + 4, pl.ds((k - 4) * HALF, HALF)]
        else:
            dst = out.at[dx * N_Z + k - 1]
        copies.append(pltpu.make_async_copy(src, dst, sems.at[n]))
    for c in copies:
        c.start()
    for c in copies:
        c.wait()


def add_products(table, first, feats, acc, room):
    def one_slot(live, row, place, tile):
        target = jnp.where(live, row, ROW_BLOCKS)
        acc[target] += jnp.dot(tile, tile_of(feats, place), preferred_element_type=f32)

    slot_loop(table, first, first + 1, *room, one_slot)


def forward_near_kernel(table, tiles_hbm, feats, acc, tiles, sems):
    start_tiles(table, 0, 1, tiles_hbm, tiles, sems)
    acc[...] = jnp.zeros_like(acc)
    add_products(table, 0, feats, acc, (tiles_hbm, tiles, sems))


def forward_far_kernel(table, tiles_hbm, feats, before, out, tiles, sems, acc):
    start_tiles(table, 1, 2, tiles_hbm, tiles, sems)
    acc[...] = before[...]
    add_products(table, 1, feats, acc, (tiles_hbm, tiles, sems))
    for r in range(N_REP):
        for h in range(2):
            out[r, pl.ds(h * TILE, TILE), :] = acc[2 * r + h].astype(bf16)


def backward_kernel(first, table, tiles_hbm, grads, out, tiles, sems, acc):
    start_tiles(table, first, first + 1, tiles_hbm, tiles, sems)
    acc[...] = jnp.zeros_like(acc)

    def one_slot(live, row, place, tile):
        target = jnp.where(live, place, 2 * CHUNKS)
        acc[target] += lax.dot_general(
            tile, tile_of(grads, row), (((0,), (0,)), ((), ())), preferred_element_type=f32
        )

    slot_loop(table, first, first + 1, tiles_hbm, tiles, sems, one_slot)
    for k in range(CHUNKS):
        for h in range(2):
            out[k, pl.ds(h * TILE, TILE), :] = acc[2 * k + h].astype(bf16)


def half_of(core, which):
    return pl.ds(pl.multiple_of((core[0] if which == 0 else 1 - core[0]) * TILE, TILE), TILE)


def final_weight_kernel(core, mine, other, out):
    out[half_of(core, 0), :] = mine[...].astype(f32)
    out[half_of(core, 1), :] = other[...].astype(f32)


def dense_kernel(core, parts, weight, cot, layer_out, payload, keep, give, terms):
    total = parts[0].astype(f32)
    for r in range(1, N_REP):
        total += parts[r].astype(f32)
    hidden = total.astype(bf16)
    w = weight[...]
    preact = jnp.dot(hidden, w, preferred_element_type=f32)
    gating = jax.nn.sigmoid(preact)
    layer_out[...] = (preact * gating).astype(bf16)
    slope = gating * (1.0 + preact * (1.0 - gating))
    grad_pre = (cot[...].astype(f32) * slope).astype(bf16)
    grad_hidden = lax.dot_general(grad_pre, w, (((1,), (1,)), ((), ())), preferred_element_type=f32).astype(bf16)
    for r in range(N_REP):
        payload[r] = grad_hidden
    terms[...] = lax.dot_general(hidden, grad_pre, (((0,), (0,)), ((), ())), preferred_element_type=f32)
    keep[...] = terms[half_of(core, 0), :].astype(bf16)
    give[...] = terms[half_of(core, 1), :].astype(bf16)


def on_device(node_features, tile_values, tile_row, tile_col, tile_count, weight, cotangent):
    sds = jax.ShapeDtypeStruct
    smem = pl.BlockSpec(memory_space=pltpu.SMEM)
    vmem = pl.BlockSpec(memory_space=pltpu.VMEM)
    params = pltpu.CompilerParams(vmem_limit_bytes=VMEM_LIMIT)
    acc_rows = sds((ROW_BLOCKS + 1, TILE, F), f32)
    hbm = pl.BlockSpec(memory_space=pltpu.HBM)
    tiles = pltpu.with_memory_space_constraint(tile_values[0, 0], pltpu.HBM)
    tile_room = [pltpu.VMEM((SLOTS, TILE, TILE), bf16), pltpu.SemaphoreType.DMA((SLOTS // UNROLL,))]
    my_core = lax.axis_index("core")
    my_xl = lax.axis_index("xl")

    def call(kernel, name, out_shape, *args, scratch=()):
        return pl.pallas_call(
            kernel,
            out_shape=out_shape,
            in_specs=[smem, hbm] + [vmem] * (len(args) - 2),
            out_specs=vmem,
            scratch_shapes=tile_room + list(scratch),
            compiler_params=params,
            cost_estimate=pl.CostEstimate(flops=1, transcendentals=0, bytes_accessed=1),
            name=name,
        )(*args)

    with jax.named_scope("gather_features"):
        up = down = node_features
        near = {0: node_features}
        for k in (1, 2, 3):
            up, down = shift(up, 1), shift(down, -1)
            near[N_Z - k], near[k] = up, down
        halves = [shift(up[:HALF], 1), shift(down[HALF:], -1)]
        order = [near[0], near[1], near[2], near[3]] + halves + [near[5], near[6], near[7]]
        chunks = order + [xor_swap(c, "xl", 2, 1) for c in order]
    with jax.named_scope("slot_table"):
        table = slot_table(
            tile_row[0, 0], tile_col[0, 0], tile_count[0, 0], lax.axis_index("z"), my_xl, my_core
        )
    with jax.named_scope("tile_products"):
        near_feats = pl.pallas_call(
            assemble_kernel,
            out_shape=sds((CHUNKS, XR, F), bf16),
            in_specs=[pl.BlockSpec(memory_space=pl.ANY)] * len(chunks),
            out_specs=vmem,
            scratch_shapes=[pltpu.SemaphoreType.DMA((len(chunks),))],
            compiler_params=params,
            name="assemble",
        )(*chunks)
        far_feats = xor_swap(near_feats, "core", 2, 1)
        acc = call(forward_near_kernel, "tile_products_near", acc_rows, table, tiles, near_feats)
        partial = call(
            forward_far_kernel,
            "tile_products_far",
            sds((N_REP, XR, F), bf16),
            table,
            tiles,
            far_feats,
            acc,
            scratch=[pltpu.VMEM((ROW_BLOCKS + 1, TILE, F), f32)],
        )
    with jax.named_scope("sum_partials"):
        parts = lax.all_to_all(partial, REP, 0, 0, tiled=True)
    with jax.named_scope("dense"):
        core = my_core.astype(jnp.int32).reshape(1)
        layer_out, payload, keep, give = pl.pallas_call(
            dense_kernel,
            out_shape=(
                sds((XR, F), bf16),
                sds((N_REP, XR, F), bf16),
                sds((TILE, F), bf16),
                sds((TILE, F), bf16),
            ),
            in_specs=[smem] + [vmem] * 3,
            out_specs=[vmem] * 4,
            scratch_shapes=[pltpu.VMEM((F, F), f32)],
            compiler_params=params,
            name="dense",
        )(core, parts, weight, cotangent[0, 0])
    with jax.named_scope("share_gradients"):
        grads = lax.all_to_all(payload, REP, 0, 0, tiled=True)
    with jax.named_scope("weight_z"):
        ring = [(2 * z + c, 2 * (z ^ 1) + (c ^ 1)) for z in range(N_Z) for c in range(2)]
        near_give = xor_swap(give, "core", 2, 1).astype(f32)
        far_give = lax.ppermute(give, ("z", "core"), ring).astype(f32)
        far_keep = xor_swap(keep, "z", N_Z, 1).astype(f32)
        w = ((keep.astype(f32) + near_give) + (far_keep + far_give)).astype(bf16)
        w = add_swapped(w, "z", N_Z, 2)
        grads, w = lax.optimization_barrier((grads, w))
        w = add_swapped(w, "z", N_Z, 4)

    def backward(first, name):
        return call(
            lambda *refs: backward_kernel(first, *refs),
            name,
            sds((CHUNKS, XR, F), bf16),
            table,
            tiles,
            grads,
            scratch=[pltpu.VMEM((2 * CHUNKS + 1, TILE, F), f32)],
        )

    def total(*terms):
        return sum(t.astype(f32) for t in terms).astype(bf16)

    with jax.named_scope("tile_products_back"):
        far_back = backward(1, "back_far")
        got = xor_swap(far_back, "core", 2, 1)
        back = total(backward(0, "back_near"), got)
        back, w = lax.optimization_barrier((back, w))
    with jax.named_scope("scatter_gradients"):
        away = {d: xor_swap(back[N_Z + d], "xl", 2, 1) for d in (4, 3, 5, 2, 6, 1, 7, 0)}
        far = total(back[4], away[4])
        up, down = shift(far[:HALF], 1), shift(far[HALF:], -1)
        none = jnp.zeros_like(up)
        up, down = jnp.concatenate([up, none], axis=0), jnp.concatenate([none, down], axis=0)
        for d in (3, 2, 1):
            up = shift(total(back[d], away[d], up), 1)
            down = shift(total(back[N_Z - d], away[N_Z - d], down), -1)
        grad_features = total(back[0], away[0], up, down)
    with jax.named_scope("weight_rest"):
        for axis, n, bit in (("y", N_Y, 1), ("y", N_Y, 2), ("xl", 2, 1), ("xh", 2, 1)):
            w = add_swapped(w, axis, n, bit)
        grad_weight = pl.pallas_call(
            final_weight_kernel,
            out_shape=sds((F, F), f32),
            in_specs=[smem] + [vmem] * 2,
            out_specs=vmem,
            compiler_params=params,
            name="final_weight",
        )(core, w, xor_swap(w, "core", 2, 1))
    return layer_out.reshape(1, 1, XR, F), grad_weight, grad_features


def solution(mesh):
    fine = Mesh(np.asarray(mesh.devices).reshape(N_Y, 2, N_Z, 2, 2), REP + BLK)
    placed = (
        P(REP + BLK, None),
        P(REP, BLK, None, None, None),
        P(REP, BLK, None),
        P(REP, BLK, None),
        P(REP, BLK),
        P(),
        P(BLK, REP, None, None),
    )
    return jax.shard_map(
        on_device,
        mesh=fine,
        in_specs=placed,
        out_specs=(P(BLK, REP, None, None), P(), P(REP + BLK, None)),
        check_vma=False,
    )
```

time: 184 us -> 162 us (0.88)
  waiting for transfers between devices: 76.6 us -> 43 us
  starting transfers between devices: 44 us -> 76.4 us
  Pallas kernels: 25.6 us -> 14.3 us
  other arithmetic: 6.6 us -> 2.15 us
  local copies, waits for them, and re-layouts: 3.49 us -> 1.02 us
    ppermute x17 -> x28, starting transfers between devices: 14.8 us -> 49.1 us  [xor_swap(): return lax.ppermute(x, axis, [(i, i ^ bit) for i in range(n)])]
    all_to_all x4 -> x0, waiting for transfers between devices: 34 us -> none  [the longest x1 13.8 us: on_device(): near0 = lax.all_to_all(first, 'z', 0, 0, tiled=True)]
    all_to_all x4 -> x0, starting transfers between devices: 19.6 us -> none  [the longest x1 9.01 us: on_device(): near0 = lax.all_to_all(first, 'z', 0, 0, tiled=True)]
    ppermute x3 -> x16, starting transfers between devices: 4.34 us -> 23.1 us  [shift(): return lax.ppermute(x, 'z', [(i, (i + step) % N_Z) for i in range(N_Z)])]
    pallas_call x4 -> x1, Pallas kernels: 12.3 us -> 2.99 us  [on_device(): pl.pallas_call(assemble_kernel, out_shape=sds((CHUNKS, XR, F), bf16), in_...]
    ppermute x3 -> x16, waiting for transfers between devices: 2.61 us -> 11.9 us  [shift(): return lax.ppermute(x, 'z', [(i, (i + step) % N_Z) for i in range(N_Z)])]
    ppermute x17 -> x28, waiting for transfers between devices: 38.2 us -> 30.4 us  [xor_swap(): return lax.ppermute(x, axis, [(i, i ^ bit) for i in range(n)])]
    convert_element_type x6 -> x8, other arithmetic: 4.66 us -> 1.69 us  [total(): return sum((t.astype(f32) for t in terms)).astype(bf16)]
  transfers between devices with their start and end apart: 26 -> 46, of which waited for: 16 -> 24; matrix products, arithmetic and copies ran while one was open for 4% -> 0% of each run, Pallas kernels for 9% -> 3%
where the time goes in v6:
time: 162 us; the launch traced here: 161 us
  starting transfers between devices  76.4 us (47%)
  waiting for transfers between devices  43 us (27%)
  blocking collectives  22.2 us (14%)
  Pallas kernels  14.3 us (9%)
  other arithmetic  2.15 us (1%)
    ppermute x28, starting transfers between devices, xor_swap(): return lax.ppermute(x, axis, [(i, i ^ bit) for i in range(n)])  49.1 us
    ppermute x28, waiting for transfers between devices, xor_swap(): return lax.ppermute(x, axis, [(i, i ^ bit) for i in range(n)])  30.4 us
    ppermute x16, starting transfers between devices, shift(): return lax.ppermute(x, 'z', [(i, (i + step) % N_Z) for i in range(N_Z)])  23.1 us
    all_to_all x1, blocking collectives, on_device(): parts = lax.all_to_all(partial, REP, 0, 0, tiled=True)  22.2 us
    ppermute x16, waiting for transfers between devices, shift(): return lax.ppermute(x, 'z', [(i, (i + step) % N_Z) for i in range(N_Z)])  11.9 us
    pallas_call x4, Pallas kernels, call(): pl.pallas_call(kernel, out_shape=out_shape, in_specs=[smem, hbm] + [vmem]...  9.23 us
    all_to_all x1, starting transfers between devices, on_device(): grads = lax.all_to_all(payload, REP, 0, 0, tiled=True)  3.56 us
  transfers between devices with their start and end apart: 46, of which 24 were waited for; matrix products, arithmetic and copies ran while one was open for 0% of the time, Pallas kernels for 3%

profile of v6, /device:TPU:1, one launch (start us, length us, event | category | flops | bytes accessed | tf_op | source)
XLA Modules:
  0.0 160.7 jit_solution(6238937190472197314)
XLA Ops:
  0.6 2.5 %collective-permute-start.3 = (bf16[256,256]{1,0:T(8,128)(2,1)}, bf16[256,256]{1,0:T(8,128)(2,1)S(1)}, u32[]{:S(2)}, u32[]{:S(2)}) collective-permute-start(bf16[256,256]{1,0:T(8,128)(2,1)} %refs_0_.1), channel_id=1, source_target_pairs={{0,4},{4,8},{8,12},{12,16},{16,20},{20,24},{24,28},{28,0},{1,5},{5... | collective-permute-start | bytes 393224 | tf_op jit(solution)/shard_map/gather_features/ppermute | solution.py:39
  3.2 4.0 %collective-permute-start = (bf16[256,256]{1,0:T(8,128)(2,1)}, bf16[256,256]{1,0:T(8,128)(2,1)S(1)}, u32[]{:S(2)}, u32[]{:S(2)}) collective-permute-start(bf16[256,256]{1,0:T(8,128)(2,1)} %refs_0_.1), channel_id=1, source_target_pairs={{0,28},{4,0},{8,4},{12,8},{16,12},{20,16},{24,20},{28,24},{1,29},{... | collective-permute-start | bytes 393224 | tf_op jit(solution)/shard_map/gather_features/ppermute | solution.py:39
  7.2 3.3 %collective-permute-done.3.refs_8_ = bf16[256,256]{1,0:T(8,128)(2,1)S(1)} collective-permute-done((bf16[256,256]{1,0:T(8,128)(2,1)}, bf16[256,256]{1,0:T(8,128)(2,1)S(1)}, u32[]{:S(2)}, u32[]{:S(2)}) %collective-permute-start.3) | collective-permute-done | bytes 131104 | tf_op jit(solution)/shard_map/gather_features/ppermute | solution.py:39
  10.6 2.7 %collective-permute-start.1 = (bf16[256,256]{1,0:T(8,128)(2,1)S(1)}, bf16[256,256]{1,0:T(8,128)(2,1)S(1)}, u32[]{:S(2)}, u32[]{:S(2)}) collective-permute-start(bf16[256,256]{1,0:T(8,128)(2,1)S(1)} %collective-permute-done.refs_1_), channel_id=1, source_target_pairs={{0,28},{4,0},{8,4},{12,8},{16,12},{20,16},{24,20},{28,24},{1,29},{... | collective-permute-start | bytes 393224 | tf_op jit(solution)/shard_map/gather_features/ppermute | solution.py:39
  13.2 2.3 %collective-permute-done.4.refs_7_ = bf16[256,256]{1,0:T(8,128)(2,1)S(1)} collective-permute-done((bf16[256,256]{1,0:T(8,128)(2,1)S(1)}, bf16[256,256]{1,0:T(8,128)(2,1)S(1)}, u32[]{:S(2)}, u32[]{:S(2)}) %collective-permute-start.4) | collective-permute-done | bytes 131104 | tf_op jit(solution)/shard_map/gather_features/ppermute | solution.py:39
  15.6 2.7 %collective-permute-start.2 = (bf16[256,256]{1,0:T(8,128)(2,1)S(1)}, bf16[256,256]{1,0:T(8,128)(2,1)S(1)}, u32[]{:S(2)}, u32[]{:S(2)}) collective-permute-start(bf16[256,256]{1,0:T(8,128)(2,1)S(1)} %collective-permute-done.1.refs_2_), channel_id=1, source_target_pairs={{0,28},{4,0},{8,4},{12,8},{16,12},{20,16},{24,20},{28,24},{1,29},{... | collective-permute-start | bytes 393224 | tf_op jit(solution)/shard_map/gather_features/ppermute | solution.py:39
  23.7 1.5 collective-permute-start.7
  27.3 1.6 collective-permute-done.10.refs_11_
  31.8 7.0 %collective-permute-done.12.refs_13_ = bf16[128,256]{1,0:T(8,128)(2,1)S(1)} collective-permute-done((bf16[128,256]{1,0:T(8,128)(2,1)S(1)}, bf16[128,256]{1,0:T(8,128)(2,1)S(1)}, u32[]{:S(2)}, u32[]{:S(2)}) %collective-permute-start.12) | collective-permute-done | bytes 65568 | tf_op jit(solution)/shard_map/gather_features/ppermute | solution.py:31
  41.1 3.0 %assemble.1.feats = bf16[16,256,256]{2,1,0:T(8,128)(2,1)S(1)} custom-call(bf16[256,256]{1,0:T(8,128)(2,1)S(1)} %copy-done, bf16[256,256]{1,0:T(8,128)(2,1)S(1)} %collective-permute-done.refs_1_, bf16[256,256]{1,0:T(8,128)(2,1)S(1)} %collective-permute-done.1.refs_2_, bf16[256,256]{1,0:T(8,128)(2,1)S(1)} %collective-permute-done.2.refs_3_, ...), custom_call_target="tpu_custom_call" | custom-call | tf_op jit(solution)/shard_map/tile_products/assemble/pallas_call | solution.py:219
  44.1 3.9 %collective-permute-start.17 = (bf16[16,256,256]{2,1,0:T(8,128)(2,1)S(1)}, bf16[16,256,256]{2,1,0:T(8,128)(2,1)}, u32[]{:S(2)}, u32[]{:S(2)}) collective-permute-start(bf16[16,256,256]{2,1,0:T(8,128)(2,1)S(1)} %assemble.1.feats), channel_id=1, source_target_pairs={{0,1},{1,0},{2,3},{3,2},{4,5},{5,4},{6,7},{7,6},{8,9},{9,8},{10,11... | collective-permute-start | bytes 6291464 | tf_op jit(solution)/shard_map/tile_products/ppermute | solution.py:31
  49.1 1.9 %tile_products_near.1.before = f32[17,128,256]{2,1,0:T(8,128)S(1)} custom-call(s32[2,256]{1,0:T(2,128)S(1)} %concatenate.9.table.refs_0_, bf16[128,128,128]{2,1,0:T(8,128)(2,1)} %bitcast.54, bf16[16,256,256]{2,1,0:T(8,128)(2,1)S(1)} %assemble.1.feats), custom_call_target="tpu_custom_call" | custom-call | flops 1 | bytes 1 | tf_op jit(solution)/shard_map/tile_products/tile_products_near/pallas_call | solution.py:194
  52.0 3.0 %tile_products_far.1 = bf16[8,256,256]{2,1,0:T(8,128)(2,1)S(1)} custom-call(s32[2,256]{1,0:T(2,128)S(1)} %concatenate.9.table.refs_0_, bf16[128,128,128]{2,1,0:T(8,128)(2,1)} %bitcast.55, bf16[16,256,256]{2,1,0:T(8,128)(2,1)} %collective-permute-done.17.feats, f32[17,128,256]{2,1,0:T(8,128)S(1)} %tile_products_near.1.before), custom_call_target="tpu_custom_call" | custom-call | flops 1 | bytes 1 | tf_op jit(solution)/shard_map/tile_products/tile_products_far/pallas_call | solution.py:194
  55.0 22.2 %all_to_all.10.parts = bf16[8,256,256]{2,1,0:T(8,128)(2,1)S(1)} all-to-all(bf16[8,256,256]{2,1,0:T(8,128)(2,1)S(1)} %tile_products_far.1), channel_id=1, replica_groups=mesh['y'=4,'xh'=2,'z'=8,'xl'=2,'core'=2] {'y','xh'}, dimensions={0} | all-to-all | bytes 2097152 | tf_op jit(solution)/shard_map/sum_partials/all_to_all | solution.py:241
  78.6 3.6 %all-to-all-start.1 = ((bf16[8,256,256]{2,1,0:T(8,128)(2,1)}), bf16[8,256,256]{2,1,0:T(8,128)(2,1)S(1)}, u32[]{:S(2)}, u32[]{:S(2)}) async-start(bf16[8,256,256]{2,1,0:T(8,128)(2,1)} %get-tuple-element.12), calls=%async_computation.1 | async-start | bytes 2097152 | tf_op jit(solution)/shard_map/share_gradients/all_to_all | solution.py:259
  82.9 3.4 %collective-permute-start.19 = (bf16[128,256]{1,0:T(8,128)(2,1)S(1)}, bf16[128,256]{1,0:T(8,128)(2,1)S(1)}, u32[]{:S(2)}, u32[]{:S(2)}) collective-permute-start(bf16[128,256]{1,0:T(8,128)(2,1)S(1)} %get-tuple-element.13), channel_id=1, source_target_pairs={{0,4},{4,0},{8,12},{12,8},{16,20},{20,16},{24,28},{28,24},{1,5},{5... | collective-permute-start | bytes 196616 | tf_op jit(solution)/shard_map/weight_z/ppermute | solution.py:31
  86.3 3.3 %collective-permute-done.19 = bf16[128,256]{1,0:T(8,128)(2,1)S(1)} collective-permute-done((bf16[128,256]{1,0:T(8,128)(2,1)S(1)}, bf16[128,256]{1,0:T(8,128)(2,1)S(1)}, u32[]{:S(2)}, u32[]{:S(2)}) %collective-permute-start.19) | collective-permute-done | bytes 65568 | tf_op jit(solution)/shard_map/weight_z/ppermute | solution.py:31
  89.7 2.6 %collective-permute-start.21 = (bf16[128,256]{1,0:T(8,128)(2,1)S(1)}, bf16[128,256]{1,0:T(8,128)(2,1)S(1)}, u32[]{:S(2)}, u32[]{:S(2)}) collective-permute-start(bf16[128,256]{1,0:T(8,128)(2,1)S(1)} %add_convert_fusion.7), channel_id=1, source_target_pairs={{0,8},{4,12},{8,0},{12,4},{16,24},{20,28},{24,16},{28,20},{1,9},{5... | collective-permute-start | bytes 196616 | tf_op jit(solution)/shard_map/weight_z/ppermute | solution.py:31
  92.3 3.7 %collective-permute-done.21 = bf16[128,256]{1,0:T(8,128)(2,1)S(1)} collective-permute-done((bf16[128,256]{1,0:T(8,128)(2,1)S(1)}, bf16[128,256]{1,0:T(8,128)(2,1)S(1)}, u32[]{:S(2)}, u32[]{:S(2)}) %collective-permute-start.21) | collective-permute-done | bytes 65568 | tf_op jit(solution)/shard_map/weight_z/ppermute | solution.py:31
  96.7 2.1 %back_far.1 = bf16[16,256,256]{2,1,0:T(8,128)(2,1)S(1)} custom-call(s32[2,256]{1,0:T(2,128)S(1)} %concatenate.9.table.refs_0_, bf16[128,128,128]{2,1,0:T(8,128)(2,1)} %bitcast.56, bf16[8,256,256]{2,1,0:T(8,128)(2,1)S(1)} %all-to-all-done.1.refs_2_), custom_call_target="tpu_custom_call" | custom-call | flops 1 | bytes 1 | tf_op jit(solution)/shard_map/tile_products_back/back_far/pallas_call | solution.py:194
  98.8 6.0 %collective-permute-start.22 = (bf16[16,256,256]{2,1,0:T(8,128)(2,1)S(1)}, bf16[16,256,256]{2,1,0:T(8,128)(2,1)S(1)}, u32[]{:S(2)}, u32[]{:S(2)}) collective-permute-start(bf16[16,256,256]{2,1,0:T(8,128)(2,1)S(1)} %back_far.1), channel_id=1, source_target_pairs={{0,1},{1,0},{2,3},{3,2},{4,5},{5,4},{6,7},{7,6},{8,9},{9,8},{10,11... | collective-permute-start | bytes 6291464 | tf_op jit(solution)/shard_map/tile_products_back/ppermute | solution.py:31
  104.9 2.0 %collective-permute-start.23 = (bf16[128,256]{1,0:T(8,128)(2,1)S(1)}, bf16[128,256]{1,0:T(8,128)(2,1)S(1)}, u32[]{:S(2)}, u32[]{:S(2)}) collective-permute-start(bf16[128,256]{1,0:T(8,128)(2,1)S(1)} %add_convert_fusion.6), channel_id=1, source_target_pairs={{0,16},{4,20},{8,24},{12,28},{16,0},{20,4},{24,8},{28,12},{1,17},{... | collective-permute-start | bytes 196616 | tf_op jit(solution)/shard_map/weight_z/ppermute | solution.py:31
  106.9 2.1 %back_near.1 = bf16[16,256,256]{2,1,0:T(8,128)(2,1)S(1)} custom-call(s32[2,256]{1,0:T(2,128)S(1)} %concatenate.9.table.refs_0_, bf16[128,128,128]{2,1,0:T(8,128)(2,1)} %bitcast.57, bf16[8,256,256]{2,1,0:T(8,128)(2,1)S(1)} %all-to-all-done.1.refs_2_), custom_call_target="tpu_custom_call" | custom-call | flops 1 | bytes 1 | tf_op jit(solution)/shard_map/tile_products_back/back_near/pallas_call | solution.py:194
  109.0 4.5 %collective-permute-done.23 = bf16[128,256]{1,0:T(8,128)(2,1)S(1)} collective-permute-done((bf16[128,256]{1,0:T(8,128)(2,1)S(1)}, bf16[128,256]{1,0:T(8,128)(2,1)S(1)}, u32[]{:S(2)}, u32[]{:S(2)}) %collective-permute-start.23) | collective-permute-done | bytes 65568 | tf_op jit(solution)/shard_map/weight_z/ppermute | solution.py:31
  114.3 2.7 %collective-permute-start.33 = (bf16[256,256]{1,0:T(8,128)(2,1)S(1)}, bf16[256,256]{1,0:T(8,128)(2,1)S(1)}, u32[]{:S(2)}, u32[]{:S(2)}) collective-permute-start(bf16[256,256]{1,0:T(8,128)(2,1)S(1)} %get-tuple-element.25), channel_id=1, source_target_pairs={{0,2},{2,0},{1,3},{3,1},{4,6},{6,4},{5,7},{7,5},{8,10},{10,8},{9,1... | collective-permute-start | bytes 393224 | tf_op jit(solution)/shard_map/scatter_gradients/ppermute | solution.py:31
  117.0 2.9 %collective-permute-done.33 = bf16[256,256]{1,0:T(8,128)(2,1)S(1)} collective-permute-done((bf16[256,256]{1,0:T(8,128)(2,1)S(1)}, bf16[256,256]{1,0:T(8,128)(2,1)S(1)}, u32[]{:S(2)}, u32[]{:S(2)}) %collective-permute-start.33) | collective-permute-done | bytes 131104 | tf_op jit(solution)/shard_map/scatter_gradients/ppermute | solution.py:31
  122.8 1.7 %collective-permute-done.34 = bf16[128,256]{1,0:T(8,128)(2,1)S(1)} collective-permute-done((bf16[128,256]{1,0:T(8,128)(2,1)S(1)}, bf16[128,256]{1,0:T(8,128)(2,1)S(1)}, u32[]{:S(2)}, u32[]{:S(2)}) %collective-permute-start.34) | collective-permute-done | bytes 65568 | tf_op jit(solution)/shard_map/scatter_gradients/ppermute | solution.py:39
  127.3 2.2 %collective-permute-done.35 = bf16[256,256]{1,0:T(8,128)(2,1)S(1)} collective-permute-done((bf16[256,256]{1,0:T(8,128)(2,1)S(1)}, bf16[256,256]{1,0:T(8,128)(2,1)S(1)}, u32[]{:S(2)}, u32[]{:S(2)}) %collective-permute-start.35) | collective-permute-done | bytes 131104 | tf_op jit(solution)/shard_map/scatter_gradients/ppermute | solution.py:39
  135.6 1.6 %collective-permute-start.42 = (bf16[256,256]{1,0:T(8,128)(2,1)S(1)}, bf16[256,256]{1,0:T(8,128)(2,1)S(1)}, u32[]{:S(2)}, u32[]{:S(2)}) collective-permute-start(bf16[256,256]{1,0:T(8,128)(2,1)S(1)} %get-tuple-element.30), channel_id=1, source_target_pairs={{0,28},{4,0},{8,4},{12,8},{16,12},{20,16},{24,20},{28,24},{1,29},{... | collective-permute-start | bytes 393224 | tf_op jit(solution)/shard_map/scatter_gradients/ppermute | solution.py:39
  139.5 2.9 %collective-permute-start.43 = (bf16[256,256]{1,0:T(8,128)(2,1)S(1)}, bf16[256,256]{1,0:T(8,128)(2,1)S(1)}, u32[]{:S(2)}, u32[]{:S(2)}) collective-permute-start(bf16[256,256]{1,0:T(8,128)(2,1)S(1)} %fusion.3), channel_id=1, source_target_pairs={{0,28},{4,0},{8,4},{12,8},{16,12},{20,16},{24,20},{28,24},{1,29},{... | collective-permute-start | bytes 393224 | tf_op jit(solution)/shard_map/scatter_gradients/ppermute | solution.py:39
  144.4 3.5 %collective-permute-start.44 = (bf16[256,256]{1,0:T(8,128)(2,1)S(1)}, bf16[256,256]{1,0:T(8,128)(2,1)S(1)}, u32[]{:S(2)}, u32[]{:S(2)}) collective-permute-start(bf16[256,256]{1,0:T(8,128)(2,1)S(1)} %fusion.5), channel_id=1, source_target_pairs={{0,28},{4,0},{8,4},{12,8},{16,12},{20,16},{24,20},{28,24},{1,29},{... | collective-permute-start | bytes 393224 | tf_op jit(solution)/shard_map/scatter_gradients/ppermute | solution.py:39
  147.8 10.5 %collective-permute-start.28 = (bf16[128,256]{1,0:T(8,128)(2,1)S(1)}, bf16[128,256]{1,0:T(8,128)(2,1)S(1)}, u32[]{:S(2)}, u32[]{:S(2)}) collective-permute-start(bf16[128,256]{1,0:T(8,128)(2,1)S(1)} %add_convert_fusion.1.mine), channel_id=1, source_target_pairs={{0,1},{1,0},{2,3},{3,2},{4,5},{5,4},{6,7},{7,6},{8,9},{9,8},{10,11... | collective-permute-start | bytes 196616 | tf_op jit(solution)/shard_map/weight_rest/ppermute | solution.py:31
  (102 shorter events, 36.0 us)
Async XLA Ops:
  0.6 9.9 %collective-permute-start.3 = (bf16[256,256]{1,0:T(8,128)(2,1)}, bf16[256,256]{1,0:T(8,128)(2,1)S(1)}, u32[]{:S(2)}, u32[]{:S(2)}) collective-permute-start(bf16[256,256]{1,0:T(8,128)(2,1)} %refs_0_.1), channel_id=1, source_target_pairs={{0,4},{4,8},{8,12},{12,16},{16,20},{20,24},{24,28},{28,0},{1,5},{5... | collective-permute-start | bytes 393224 | tf_op jit(solution)/shard_map/gather_features/ppermute | solution.py:39
  3.2 7.4 %collective-permute-start = (bf16[256,256]{1,0:T(8,128)(2,1)}, bf16[256,256]{1,0:T(8,128)(2,1)S(1)}, u32[]{:S(2)}, u32[]{:S(2)}) collective-permute-start(bf16[256,256]{1,0:T(8,128)(2,1)} %refs_0_.1), channel_id=1, source_target_pairs={{0,28},{4,0},{8,4},{12,8},{16,12},{20,16},{24,20},{28,24},{1,29},{... | collective-permute-start | bytes 393224 | tf_op jit(solution)/shard_map/gather_features/ppermute | solution.py:39
  15.6 5.4 %collective-permute-start.5 = (bf16[256,256]{1,0:T(8,128)(2,1)S(1)}, bf16[256,256]{1,0:T(8,128)(2,1)S(1)}, u32[]{:S(2)}, u32[]{:S(2)}) collective-permute-start(bf16[256,256]{1,0:T(8,128)(2,1)S(1)} %collective-permute-done.4.refs_7_), channel_id=1, source_target_pairs={{0,4},{4,8},{8,12},{12,16},{16,20},{20,24},{24,28},{28,0},{1,5},{5... | collective-permute-start | bytes 393224 | tf_op jit(solution)/shard_map/gather_features/ppermute | solution.py:39
  15.6 6.2 %collective-permute-start.2 = (bf16[256,256]{1,0:T(8,128)(2,1)S(1)}, bf16[256,256]{1,0:T(8,128)(2,1)S(1)}, u32[]{:S(2)}, u32[]{:S(2)}) collective-permute-start(bf16[256,256]{1,0:T(8,128)(2,1)S(1)} %collective-permute-done.1.refs_2_), channel_id=1, source_target_pairs={{0,28},{4,0},{8,4},{12,8},{16,12},{20,16},{24,20},{28,24},{1,29},{... | collective-permute-start | bytes 393224 | tf_op jit(solution)/shard_map/gather_features/ppermute | solution.py:39
  19.7 6.4 %collective-permute-start.16 = (bf16[256,256]{1,0:T(8,128)(2,1)S(1)}, bf16[256,256]{1,0:T(8,128)(2,1)S(1)}, u32[]{:S(2)}, u32[]{:S(2)}) collective-permute-start(bf16[256,256]{1,0:T(8,128)(2,1)S(1)} %collective-permute-done.3.refs_8_), channel_id=1, source_target_pairs={{0,2},{2,0},{1,3},{3,1},{4,6},{6,4},{5,7},{7,5},{8,10},{10,8},{9,1... | collective-permute-start | bytes 393224 | tf_op jit(solution)/shard_map/gather_features/ppermute | solution.py:31
  20.9 8.0 %collective-permute-start.10 = (bf16[256,256]{1,0:T(8,128)(2,1)S(1)}, bf16[256,256]{1,0:T(8,128)(2,1)S(1)}, u32[]{:S(2)}, u32[]{:S(2)}) collective-permute-start(bf16[256,256]{1,0:T(8,128)(2,1)S(1)} %collective-permute-done.1.refs_2_), channel_id=1, source_target_pairs={{0,2},{2,0},{1,3},{3,1},{4,6},{6,4},{5,7},{7,5},{8,10},{10,8},{9,1... | collective-permute-start | bytes 393224 | tf_op jit(solution)/shard_map/gather_features/ppermute | solution.py:31
  21.8 9.9 %collective-permute-start.15 = (bf16[256,256]{1,0:T(8,128)(2,1)S(1)}, bf16[256,256]{1,0:T(8,128)(2,1)S(1)}, u32[]{:S(2)}, u32[]{:S(2)}) collective-permute-start(bf16[256,256]{1,0:T(8,128)(2,1)S(1)} %collective-permute-done.4.refs_7_), channel_id=1, source_target_pairs={{0,2},{2,0},{1,3},{3,1},{4,6},{6,4},{5,7},{7,5},{8,10},{10,8},{9,1... | collective-permute-start | bytes 393224 | tf_op jit(solution)/shard_map/gather_features/ppermute | solution.py:31
  22.6 7.6 %collective-permute-start.6 = (bf16[128,256]{1,0:T(8,128)(2,1)S(1)}, bf16[128,256]{1,0:T(8,128)(2,1)S(1)}, u32[]{:S(2)}, u32[]{:S(2)}) collective-permute-start(bf16[128,256]{1,0:T(8,128)(2,1)S(1)} %slice.80), channel_id=1, source_target_pairs={{0,4},{4,8},{8,12},{12,16},{16,20},{20,24},{24,28},{28,0},{1,5},{5... | collective-permute-start | bytes 196616 | tf_op jit(solution)/shard_map/gather_features/ppermute | solution.py:39
  23.7 6.7 %collective-permute-start.7 = (bf16[128,256]{1,0:T(8,128)(2,1)S(1)}, bf16[128,256]{1,0:T(8,128)(2,1)S(1)}, u32[]{:S(2)}, u32[]{:S(2)}) collective-permute-start(bf16[128,256]{1,0:T(8,128)(2,1)S(1)} %slice.81), channel_id=1, source_target_pairs={{0,28},{4,0},{8,4},{12,8},{16,12},{20,16},{24,20},{28,24},{1,29},{... | collective-permute-start | bytes 196616 | tf_op jit(solution)/shard_map/gather_features/ppermute | solution.py:39
  26.1 14.0 %collective-permute-start.11 = (bf16[256,256]{1,0:T(8,128)(2,1)S(1)}, bf16[256,256]{1,0:T(8,128)(2,1)S(1)}, u32[]{:S(2)}, u32[]{:S(2)}) collective-permute-start(bf16[256,256]{1,0:T(8,128)(2,1)S(1)} %collective-permute-done.2.refs_3_), channel_id=1, source_target_pairs={{0,2},{2,0},{1,3},{3,1},{4,6},{6,4},{5,7},{7,5},{8,10},{10,8},{9,1... | collective-permute-start | bytes 393224 | tf_op jit(solution)/shard_map/gather_features/ppermute | solution.py:31
  28.9 11.2 %collective-permute-start.14 = (bf16[256,256]{1,0:T(8,128)(2,1)S(1)}, bf16[256,256]{1,0:T(8,128)(2,1)S(1)}, u32[]{:S(2)}, u32[]{:S(2)}) collective-permute-start(bf16[256,256]{1,0:T(8,128)(2,1)S(1)} %collective-permute-done.5.refs_6_), channel_id=1, source_target_pairs={{0,2},{2,0},{1,3},{3,1},{4,6},{6,4},{5,7},{7,5},{8,10},{10,8},{9,1... | collective-permute-start | bytes 393224 | tf_op jit(solution)/shard_map/gather_features/ppermute | solution.py:31
  30.2 8.6 %collective-permute-start.12 = (bf16[128,256]{1,0:T(8,128)(2,1)S(1)}, bf16[128,256]{1,0:T(8,128)(2,1)S(1)}, u32[]{:S(2)}, u32[]{:S(2)}) collective-permute-start(bf16[128,256]{1,0:T(8,128)(2,1)S(1)} %collective-permute-done.6.refs_4_), channel_id=1, source_target_pairs={{0,2},{2,0},{1,3},{3,1},{4,6},{6,4},{5,7},{7,5},{8,10},{10,8},{9,1... | collective-permute-start | bytes 196616 | tf_op jit(solution)/shard_map/gather_features/ppermute | solution.py:31
  30.4 9.8 %collective-permute-start.13 = (bf16[128,256]{1,0:T(8,128)(2,1)S(1)}, bf16[128,256]{1,0:T(8,128)(2,1)S(1)}, u32[]{:S(2)}, u32[]{:S(2)}) collective-permute-start(bf16[128,256]{1,0:T(8,128)(2,1)S(1)} %collective-permute-done.7.refs_5_), channel_id=1, source_target_pairs={{0,2},{2,0},{1,3},{3,1},{4,6},{6,4},{5,7},{7,5},{8,10},{10,8},{9,1... | collective-permute-start | bytes 196616 | tf_op jit(solution)/shard_map/gather_features/ppermute | solution.py:31
  44.1 7.9 %collective-permute-start.17 = (bf16[16,256,256]{2,1,0:T(8,128)(2,1)S(1)}, bf16[16,256,256]{2,1,0:T(8,128)(2,1)}, u32[]{:S(2)}, u32[]{:S(2)}) collective-permute-start(bf16[16,256,256]{2,1,0:T(8,128)(2,1)S(1)} %assemble.1.feats), channel_id=1, source_target_pairs={{0,1},{1,0},{2,3},{3,2},{4,5},{5,4},{6,7},{7,6},{8,9},{9,8},{10,11... | collective-permute-start | bytes 6291464 | tf_op jit(solution)/shard_map/tile_products/ppermute | solution.py:31
  78.6 18.1 %all-to-all-start.1 = ((bf16[8,256,256]{2,1,0:T(8,128)(2,1)}), bf16[8,256,256]{2,1,0:T(8,128)(2,1)S(1)}, u32[]{:S(2)}, u32[]{:S(2)}) async-start(bf16[8,256,256]{2,1,0:T(8,128)(2,1)} %get-tuple-element.12), calls=%async_computation.1 | async-start | bytes 2097152 | tf_op jit(solution)/shard_map/share_gradients/all_to_all | solution.py:259
  82.9 6.8 %collective-permute-start.19 = (bf16[128,256]{1,0:T(8,128)(2,1)S(1)}, bf16[128,256]{1,0:T(8,128)(2,1)S(1)}, u32[]{:S(2)}, u32[]{:S(2)}) collective-permute-start(bf16[128,256]{1,0:T(8,128)(2,1)S(1)} %get-tuple-element.13), channel_id=1, source_target_pairs={{0,4},{4,0},{8,12},{12,8},{16,20},{20,16},{24,28},{28,24},{1,5},{5... | collective-permute-start | bytes 196616 | tf_op jit(solution)/shard_map/weight_z/ppermute | solution.py:31
  89.7 6.3 %collective-permute-start.21 = (bf16[128,256]{1,0:T(8,128)(2,1)S(1)}, bf16[128,256]{1,0:T(8,128)(2,1)S(1)}, u32[]{:S(2)}, u32[]{:S(2)}) collective-permute-start(bf16[128,256]{1,0:T(8,128)(2,1)S(1)} %add_convert_fusion.7), channel_id=1, source_target_pairs={{0,8},{4,12},{8,0},{12,4},{16,24},{20,28},{24,16},{28,20},{1,9},{5... | collective-permute-start | bytes 196616 | tf_op jit(solution)/shard_map/weight_z/ppermute | solution.py:31
  98.8 14.7 %collective-permute-start.22 = (bf16[16,256,256]{2,1,0:T(8,128)(2,1)S(1)}, bf16[16,256,256]{2,1,0:T(8,128)(2,1)S(1)}, u32[]{:S(2)}, u32[]{:S(2)}) collective-permute-start(bf16[16,256,256]{2,1,0:T(8,128)(2,1)S(1)} %back_far.1), channel_id=1, source_target_pairs={{0,1},{1,0},{2,3},{3,2},{4,5},{5,4},{6,7},{7,6},{8,9},{9,8},{10,11... | collective-permute-start | bytes 6291464 | tf_op jit(solution)/shard_map/tile_products_back/ppermute | solution.py:31
  104.9 8.6 %collective-permute-start.23 = (bf16[128,256]{1,0:T(8,128)(2,1)S(1)}, bf16[128,256]{1,0:T(8,128)(2,1)S(1)}, u32[]{:S(2)}, u32[]{:S(2)}) collective-permute-start(bf16[128,256]{1,0:T(8,128)(2,1)S(1)} %add_convert_fusion.6), channel_id=1, source_target_pairs={{0,16},{4,20},{8,24},{12,28},{16,0},{20,4},{24,8},{28,12},{1,17},{... | collective-permute-start | bytes 196616 | tf_op jit(solution)/shard_map/weight_z/ppermute | solution.py:31
  114.3 5.7 %collective-permute-start.33 = (bf16[256,256]{1,0:T(8,128)(2,1)S(1)}, bf16[256,256]{1,0:T(8,128)(2,1)S(1)}, u32[]{:S(2)}, u32[]{:S(2)}) collective-permute-start(bf16[256,256]{1,0:T(8,128)(2,1)S(1)} %get-tuple-element.25), channel_id=1, source_target_pairs={{0,2},{2,0},{1,3},{3,1},{4,6},{6,4},{5,7},{7,5},{8,10},{10,8},{9,1... | collective-permute-start | bytes 393224 | tf_op jit(solution)/shard_map/scatter_gradients/ppermute | solution.py:31
  116.9 5.8 %collective-permute-start.32 = (bf16[256,256]{1,0:T(8,128)(2,1)S(1)}, bf16[256,256]{1,0:T(8,128)(2,1)S(1)}, u32[]{:S(2)}, u32[]{:S(2)}) collective-permute-start(bf16[256,256]{1,0:T(8,128)(2,1)S(1)} %get-tuple-element.26), channel_id=1, source_target_pairs={{0,2},{2,0},{1,3},{3,1},{4,6},{6,4},{5,7},{7,5},{8,10},{10,8},{9,1... | collective-permute-start | bytes 393224 | tf_op jit(solution)/shard_map/scatter_gradients/ppermute | solution.py:31
  120.1 6.1 %collective-permute-start.31 = (bf16[256,256]{1,0:T(8,128)(2,1)S(1)}, bf16[256,256]{1,0:T(8,128)(2,1)S(1)}, u32[]{:S(2)}, u32[]{:S(2)}) collective-permute-start(bf16[256,256]{1,0:T(8,128)(2,1)S(1)} %get-tuple-element.27), channel_id=1, source_target_pairs={{0,2},{2,0},{1,3},{3,1},{4,6},{6,4},{5,7},{7,5},{8,10},{10,8},{9,1... | collective-permute-start | bytes 393224 | tf_op jit(solution)/shard_map/scatter_gradients/ppermute | solution.py:31
  124.5 5.8 %collective-permute-start.24 = (bf16[128,256]{1,0:T(8,128)(2,1)S(1)}, bf16[128,256]{1,0:T(8,128)(2,1)S(1)}, u32[]{:S(2)}, u32[]{:S(2)}) collective-permute-start(bf16[128,256]{1,0:T(8,128)(2,1)S(1)} %add_convert_fusion.5), channel_id=1, source_target_pairs={{0,64},{64,0},{128,192},{192,128},{1,65},{65,1},{129,193},{193,129... | collective-permute-start | bytes 196616 | tf_op jit(solution)/shard_map/weight_rest/ppermute | solution.py:31
  124.7 6.5 %collective-permute-start.30 = (bf16[256,256]{1,0:T(8,128)(2,1)S(1)}, bf16[256,256]{1,0:T(8,128)(2,1)S(1)}, u32[]{:S(2)}, u32[]{:S(2)}) collective-permute-start(bf16[256,256]{1,0:T(8,128)(2,1)S(1)} %get-tuple-element.28), channel_id=1, source_target_pairs={{0,2},{2,0},{1,3},{3,1},{4,6},{6,4},{5,7},{7,5},{8,10},{10,8},{9,1... | collective-permute-start | bytes 393224 | tf_op jit(solution)/shard_map/scatter_gradients/ppermute | solution.py:31
  125.9 6.6 %collective-permute-start.40 = (bf16[256,256]{1,0:T(8,128)(2,1)S(1)}, bf16[256,256]{1,0:T(8,128)(2,1)S(1)}, u32[]{:S(2)}, u32[]{:S(2)}) collective-permute-start(bf16[256,256]{1,0:T(8,128)(2,1)S(1)} %get-tuple-element.22), channel_id=1, source_target_pairs={{0,2},{2,0},{1,3},{3,1},{4,6},{6,4},{5,7},{7,5},{8,10},{10,8},{9,1... | collective-permute-start | bytes 393224 | tf_op jit(solution)/shard_map/scatter_gradients/ppermute | solution.py:31
  126.2 12.6 %collective-permute-start.39 = (bf16[256,256]{1,0:T(8,128)(2,1)S(1)}, bf16[256,256]{1,0:T(8,128)(2,1)S(1)}, u32[]{:S(2)}, u32[]{:S(2)}) collective-permute-start(bf16[256,256]{1,0:T(8,128)(2,1)S(1)} %get-tuple-element.23), channel_id=1, source_target_pairs={{0,2},{2,0},{1,3},{3,1},{4,6},{6,4},{5,7},{7,5},{8,10},{10,8},{9,1... | collective-permute-start | bytes 393224 | tf_op jit(solution)/shard_map/scatter_gradients/ppermute | solution.py:31
  131.2 12.7 %collective-permute-start.38 = (bf16[256,256]{1,0:T(8,128)(2,1)S(1)}, bf16[256,256]{1,0:T(8,128)(2,1)S(1)}, u32[]{:S(2)}, u32[]{:S(2)}) collective-permute-start(bf16[256,256]{1,0:T(8,128)(2,1)S(1)} %get-tuple-element.24), channel_id=1, source_target_pairs={{0,2},{2,0},{1,3},{3,1},{4,6},{6,4},{5,7},{7,5},{8,10},{10,8},{9,1... | collective-permute-start | bytes 393224 | tf_op jit(solution)/shard_map/scatter_gradients/ppermute | solution.py:31
  132.4 27.5 %collective-permute-start.29 = (bf16[256,256]{1,0:T(8,128)(2,1)S(1)}, bf16[256,256]{1,0:T(8,128)(2,1)S(1)}, u32[]{:S(2)}, u32[]{:S(2)}) collective-permute-start(bf16[256,256]{1,0:T(8,128)(2,1)S(1)} %get-tuple-element.21), channel_id=1, source_target_pairs={{0,2},{2,0},{1,3},{3,1},{4,6},{6,4},{5,7},{7,5},{8,10},{10,8},{9,1... | collective-permute-start | bytes 393224 | tf_op jit(solution)/shard_map/scatter_gradients/ppermute | solution.py:31
  142.4 5.4 %collective-permute-start.27 = (bf16[128,256]{1,0:T(8,128)(2,1)S(1)}, bf16[128,256]{1,0:T(8,128)(2,1)S(1)}, u32[]{:S(2)}, u32[]{:S(2)}) collective-permute-start(bf16[128,256]{1,0:T(8,128)(2,1)S(1)} %add_convert_fusion.2), channel_id=1, source_target_pairs={{0,32},{32,0},{1,33},{33,1},{2,34},{34,2},{3,35},{35,3},{4,36},{36... | collective-permute-start | bytes 196616 | tf_op jit(solution)/shard_map/weight_rest/ppermute | solution.py:31
  143.9 16.0 %collective-permute-start.37 = (bf16[256,256]{1,0:T(8,128)(2,1)S(1)}, bf16[256,256]{1,0:T(8,128)(2,1)S(1)}, u32[]{:S(2)}, u32[]{:S(2)}) collective-permute-start(bf16[256,256]{1,0:T(8,128)(2,1)S(1)} %get-tuple-element.29), channel_id=1, source_target_pairs={{0,4},{4,8},{8,12},{12,16},{16,20},{20,24},{24,28},{28,0},{1,5},{5... | collective-permute-start | bytes 393224 | tf_op jit(solution)/shard_map/scatter_gradients/ppermute | solution.py:39
  144.4 15.6 %collective-permute-start.44 = (bf16[256,256]{1,0:T(8,128)(2,1)S(1)}, bf16[256,256]{1,0:T(8,128)(2,1)S(1)}, u32[]{:S(2)}, u32[]{:S(2)}) collective-permute-start(bf16[256,256]{1,0:T(8,128)(2,1)S(1)} %fusion.5), channel_id=1, source_target_pairs={{0,28},{4,0},{8,4},{12,8},{16,12},{20,16},{24,20},{28,24},{1,29},{... | collective-permute-start | bytes 393224 | tf_op jit(solution)/shard_map/scatter_gradients/ppermute | solution.py:39
  147.8 11.4 %collective-permute-start.28 = (bf16[128,256]{1,0:T(8,128)(2,1)S(1)}, bf16[128,256]{1,0:T(8,128)(2,1)S(1)}, u32[]{:S(2)}, u32[]{:S(2)}) collective-permute-start(bf16[128,256]{1,0:T(8,128)(2,1)S(1)} %add_convert_fusion.1.mine), channel_id=1, source_target_pairs={{0,1},{1,0},{2,3},{3,2},{4,5},{5,4},{6,7},{7,6},{8,9},{9,8},{10,11... | collective-permute-start | bytes 196616 | tf_op jit(solution)/shard_map/weight_rest/ppermute | solution.py:31
  (19 other events, 159.9 us)

commit v7 on v6

--- a/solution.py
+++ b/solution.py
@@ -19,8 +19,8 @@
 ROW_BLOCKS = 16
 UNROLL = 8
 HALF = XR // 2
-CLASSES = 2
-CHUNKS = 2 * N_Z
+CLASSES = 4
+SPOT = {4: 0, 3: 1, 5: 2, 2: 3, 6: 4, 1: 5, 7: 6, 0: 7}
 
 f32 = jnp.float32
 bf16 = jnp.bfloat16
@@ -45,8 +45,9 @@
     dx = ((owner >> 1) & 1) ^ my_xl
     dc = (owner & 1) ^ my_core
     position = jnp.arange(SLOTS, dtype=jnp.int32)
-    kind = jnp.where(position < count, dc, CLASSES)
-    place = ((dx * N_Z + dz) << 1) | (cols & 1)
+    kind = jnp.where(position < count, 2 * dx + dc, CLASSES)
+    spot = jnp.maximum(2 * (4 - jnp.minimum(dz, N_Z - dz)) - 1 + (dz > 4).astype(jnp.int32), 0)
+    place = (spot << 1) | (cols & 1)
     packed = rows | (place << 8) | (position << 16)
     key = kind * SLOTS + position
     rank = jnp.sum((key[None, :] < key[:, None]).astype(jnp.int32), axis=1)
@@ -93,61 +94,96 @@
     return ref[which >> 1, pl.ds(pl.multiple_of((which & 1) * TILE, TILE), TILE), :]
 
 
+def blocks(n, one):
+    def step(i, carry):
+        one(i)
+        return carry
+
+    lax.fori_loop(0, n, step, 0)
+
+
+def clear(acc):
+    zero = jnp.zeros((TILE, F), f32)
+
+    def one(i):
+        acc[i] = zero
+
+    blocks(acc.shape[0] - 1, one)
+
+
+def carry_over(before, acc):
+    def one(i):
+        acc[i] = before[i]
+
+    blocks(acc.shape[0] - 1, one)
+
+
+def round_out(acc, out):
+    def one(i):
+        for h in range(2):
+            out[i, pl.ds(h * TILE, TILE), :] = acc[2 * i + h].astype(bf16)
+
+    blocks(out.shape[0], one)
+
+
 def assemble_kernel(*refs):
     out, sems = refs[-2:]
     copies = []
-    for n, src in enumerate(refs[:-2]):
-        dx, k = divmod(n, N_Z + 1)
+    for k, src in enumerate(refs[:-2]):
         if k < 4:
-            dst = out.at[dx * N_Z + k]
+            dst = out.at[SPOT[k]]
         elif k < 6:
-            dst = out.at[dx * N_Z + 4, pl.ds((k - 4) * HALF, HALF)]
+            dst = out.at[SPOT[4], pl.ds((k - 4) * HALF, HALF)]
         else:
-            dst = out.at[dx * N_Z + k - 1]
-        copies.append(pltpu.make_async_copy(src, dst, sems.at[n]))
+            dst = out.at[SPOT[k - 1]]
+        copies.append(pltpu.make_async_copy(src, dst, sems.at[k]))
     for c in copies:
         c.start()
     for c in copies:
         c.wait()
 
 
-def add_products(table, first, feats, acc, room):
+def add_products(table, kind, feats, acc, room):
     def one_slot(live, row, place, tile):
         target = jnp.where(live, row, ROW_BLOCKS)
         acc[target] += jnp.dot(tile, tile_of(feats, place), preferred_element_type=f32)
 
-    slot_loop(table, first, first + 1, *room, one_slot)
-
-
-def forward_near_kernel(table, tiles_hbm, feats, acc, tiles, sems):
-    start_tiles(table, 0, 1, tiles_hbm, tiles, sems)
-    acc[...] = jnp.zeros_like(acc)
-    add_products(table, 0, feats, acc, (tiles_hbm, tiles, sems))
+    slot_loop(table, kind, kind + 1, *room, one_slot)
+
+
+def forward_first_kernel(table, tiles_hbm, near, far, acc, tiles, sems):
+    for k in range(2):
+        start_tiles(table, k, k + 1, tiles_hbm, tiles.at[k], sems.at[k])
+    clear(acc)
+    for k, feats in enumerate((near, far)):
+        add_products(table, k, feats, acc, (tiles_hbm, tiles.at[k], sems.at[k]))
+
+
+def forward_near_kernel(table, tiles_hbm, feats, before, acc, tiles, sems):
+    start_tiles(table, 2, 3, tiles_hbm, tiles.at[0], sems.at[0])
+    carry_over(before, acc)
+    add_products(table, 2, feats, acc, (tiles_hbm, tiles.at[0], sems.at[0]))
 
 
 def forward_far_kernel(table, tiles_hbm, feats, before, out, tiles, sems, acc):
-    start_tiles(table, 1, 2, tiles_hbm, tiles, sems)
-    acc[...] = before[...]
-    add_products(table, 1, feats, acc, (tiles_hbm, tiles, sems))
-    for r in range(N_REP):
-        for h in range(2):
-            out[r, pl.ds(h * TILE, TILE), :] = acc[2 * r + h].astype(bf16)
-
-
-def backward_kernel(first, table, tiles_hbm, grads, out, tiles, sems, acc):
-    start_tiles(table, first, first + 1, tiles_hbm, tiles, sems)
-    acc[...] = jnp.zeros_like(acc)
+    start_tiles(table, 3, 4, tiles_hbm, tiles.at[0], sems.at[0])
+    carry_over(before, acc)
+    add_products(table, 3, feats, acc, (tiles_hbm, tiles.at[0], sems.at[0]))
+    round_out(acc, out)
+
+
+def backward_kernel(kind, table, tiles_hbm, grads, out, tiles, sems, acc):
+    start_tiles(table, kind, kind + 1, tiles_hbm, tiles.at[0], sems.at[0])
+    clear(acc)
 
     def one_slot(live, row, place, tile):
-        target = jnp.where(live, place, 2 * CHUNKS)
+        target = jnp.where(live, place, 2 * N_Z)
         acc[target] += lax.dot_general(
             tile, tile_of(grads, row), (((0,), (0,)), ((), ())), preferred_element_type=f32
         )
 
-    slot_loop(table, first, first + 1, tiles_hbm, tiles, sems, one_slot)
-    for k in range(CHUNKS):
-        for h in range(2):
-            out[k, pl.ds(h * TILE, TILE), :] = acc[2 * k + h].astype(bf16)
+    slot_loop(table, kind, kind + 1, tiles_hbm, tiles.at[0], sems.at[0], one_slot)
+    round_out(acc, out)
 
 
 def half_of(core, which):
@@ -186,54 +222,69 @@
     acc_rows = sds((ROW_BLOCKS + 1, TILE, F), f32)
     hbm = pl.BlockSpec(memory_space=pltpu.HBM)
     tiles = pltpu.with_memory_space_constraint(tile_values[0, 0], pltpu.HBM)
-    tile_room = [pltpu.VMEM((SLOTS, TILE, TILE), bf16), pltpu.SemaphoreType.DMA((SLOTS // UNROLL,))]
+
+    def tile_room(n):
+        return [pltpu.VMEM((n, SLOTS, TILE, TILE), bf16), pltpu.SemaphoreType.DMA((n, SLOTS // UNROLL))]
+
     my_core = lax.axis_index("core")
     my_xl = lax.axis_index("xl")
 
-    def call(kernel, name, out_shape, *args, scratch=()):
+    def call(kernel, name, out_shape, *args, scratch=(), rooms=1):
         return pl.pallas_call(
             kernel,
             out_shape=out_shape,
             in_specs=[smem, hbm] + [vmem] * (len(args) - 2),
             out_specs=vmem,
-            scratch_shapes=tile_room + list(scratch),
+            scratch_shapes=tile_room(rooms) + list(scratch),
             compiler_params=params,
             cost_estimate=pl.CostEstimate(flops=1, transcendentals=0, bytes_accessed=1),
             name=name,
         )(*args)
 
+    def across(x):
+        return xor_swap(x, "xl", 2, 1)
+
+    def assemble(chunks, name):
+        return pl.pallas_call(
+            assemble_kernel,
+            out_shape=sds((N_Z, XR, F), bf16),
+            in_specs=[pl.BlockSpec(memory_space=pl.ANY)] * len(chunks),
+            out_specs=vmem,
+            scratch_shapes=[pltpu.SemaphoreType.DMA((len(chunks),))],
+            compiler_params=params,
+            name=name,
+        )(*chunks)
+
     with jax.named_scope("gather_features"):
-        up = down = node_features
-        near = {0: node_features}
-        for k in (1, 2, 3):
-            up, down = shift(up, 1), shift(down, -1)
-            near[N_Z - k], near[k] = up, down
-        halves = [shift(up[:HALF], 1), shift(down[HALF:], -1)]
-        order = [near[0], near[1], near[2], near[3]] + halves + [near[5], near[6], near[7]]
-        chunks = order + [xor_swap(c, "xl", 2, 1) for c in order]
+        own = node_features
+        up1, down1 = shift(own, 1), shift(own, -1)
+        own_x = across(own)
+        up2, down2 = shift(up1, 1), shift(down1, -1)
+        up1_x, down1_x = across(up1), across(down1)
+        up2, own_x = lax.optimization_barrier((up2, own_x))
+        up3, down3 = shift(up2, 1), shift(down2, -1)
+        up2_x, down2_x = across(up2), across(down2)
+        up3, up1_x, down1_x = lax.optimization_barrier((up3, up1_x, down1_x))
+        low, high = shift(up3[:HALF], 1), shift(down3[HALF:], -1)
+        near0 = assemble((pltpu.with_memory_space_constraint(own, pltpu.HBM), down1, down2, down3, low, high, up3, up2, up1), "assemble_own")
+        far0 = xor_swap(near0, "core", 2, 1)
+        crossed = (own_x, down1_x, down2_x, across(down3), across(low), across(high), across(up3), up2_x, up1_x)
+        near1 = assemble(crossed, "assemble_crossed")
+        far1 = xor_swap(near1, "core", 2, 1)
     with jax.named_scope("slot_table"):
         table = slot_table(
             tile_row[0, 0], tile_col[0, 0], tile_count[0, 0], lax.axis_index("z"), my_xl, my_core
         )
     with jax.named_scope("tile_products"):
-        near_feats = pl.pallas_call(
-            assemble_kernel,
-            out_shape=sds((CHUNKS, XR, F), bf16),
-            in_specs=[pl.BlockSpec(memory_space=pl.ANY)] * len(chunks),
-            out_specs=vmem,
-            scratch_shapes=[pltpu.SemaphoreType.DMA((len(chunks),))],
-            compiler_params=params,
-            name="assemble",
-        )(*chunks)
-        far_feats = xor_swap(near_feats, "core", 2, 1)
-        acc = call(forward_near_kernel, "tile_products_near", acc_rows, table, tiles, near_feats)
+        acc = call(forward_first_kernel, "tile_products_first", acc_rows, table, tiles, near0, far0, rooms=2)
+        acc = call(forward_near_kernel, "tile_products_near", acc_rows, table, tiles, near1, acc)
         partial = call(
             forward_far_kernel,
             "tile_products_far",
             sds((N_REP, XR, F), bf16),
             table,
             tiles,
-            far_feats,
+            far1,
             acc,
             scratch=[pltpu.VMEM((ROW_BLOCKS + 1, TILE, F), f32)],
         )
@@ -265,39 +316,40 @@
         w = ((keep.astype(f32) + near_give) + (far_keep + far_give)).astype(bf16)
         w = add_swapped(w, "z", N_Z, 2)
         grads, w = lax.optimization_barrier((grads, w))
-        w = add_swapped(w, "z", N_Z, 4)
-
-    def backward(first, name):
+
+    def backward(kind, grads, name):
         return call(
-            lambda *refs: backward_kernel(first, *refs),
+            lambda *refs: backward_kernel(kind, *refs),
             name,
-            sds((CHUNKS, XR, F), bf16),
+            sds((N_Z, XR, F), bf16),
             table,
             tiles,
             grads,
-            scratch=[pltpu.VMEM((2 * CHUNKS + 1, TILE, F), f32)],
+            scratch=[pltpu.VMEM((2 * N_Z + 1, TILE, F), f32)],
         )
 
     def total(*terms):
         return sum(t.astype(f32) for t in terms).astype(bf16)
 
-    with jax.named_scope("tile_products_back"):
-        far_back = backward(1, "back_far")
-        got = xor_swap(far_back, "core", 2, 1)
-        back = total(backward(0, "back_near"), got)
-        back, w = lax.optimization_barrier((back, w))
+    with jax.named_scope("back_crossed"):
+        got = xor_swap(backward(3, grads, "back_crossed_far"), "core", 2, 1)
+        crossed = total(backward(2, grads, "back_crossed_near"), got)
+        crossed, w, grads = lax.optimization_barrier((crossed, w, grads))
+    with jax.named_scope("back_own"):
+        got = xor_swap(backward(1, grads, "back_own_far"), "core", 2, 1)
+        back = total(backward(0, grads, "back_own_near"), got)
     with jax.named_scope("scatter_gradients"):
-        away = {d: xor_swap(back[N_Z + d], "xl", 2, 1) for d in (4, 3, 5, 2, 6, 1, 7, 0)}
-        far = total(back[4], away[4])
+        away = [across(crossed[a:b]) for a, b in ((0, 1), (1, 3), (3, 5), (5, N_Z))]
+        far = total(back[0], away[0][0])
         up, down = shift(far[:HALF], 1), shift(far[HALF:], -1)
         none = jnp.zeros_like(up)
         up, down = jnp.concatenate([up, none], axis=0), jnp.concatenate([none, down], axis=0)
         for d in (3, 2, 1):
-            up = shift(total(back[d], away[d], up), 1)
-            down = shift(total(back[N_Z - d], away[N_Z - d], down), -1)
-        grad_features = total(back[0], away[0], up, down)
+            up = shift(total(back[SPOT[d]], away[4 - d][0], up), 1)
+            down = shift(total(back[SPOT[N_Z - d]], away[4 - d][1], down), -1)
+        grad_features = total(back[SPOT[0]], away[3][2], up, down)
     with jax.named_scope("weight_rest"):
-        for axis, n, bit in (("y", N_Y, 1), ("y", N_Y, 2), ("xl", 2, 1), ("xh", 2, 1)):
+        for axis, n, bit in (("xl", 2, 1), ("z", N_Z, 4), ("xh", 2, 1), ("y", N_Y, 1), ("y", N_Y, 2)):
             w = add_swapped(w, axis, n, bit)
         grad_weight = pl.pallas_call(
             final_weight_kernel,

time: 162 us -> 152 us (0.938)
  starting transfers between devices: 76.4 us -> 65.9 us
  waiting for transfers between devices: 43 us -> 33 us
  Pallas kernels: 14.3 us -> 23.9 us
  blocking collectives: 22.2 us -> 24.5 us
    ppermute x28 -> x26, starting transfers between devices: 49.1 us -> 30.9 us  [xor_swap(): return lax.ppermute(x, axis, [(i, i ^ bit) for i in range(n)])]
    ppermute x28 -> x26, waiting for transfers between devices: 30.4 us -> 18.1 us  [xor_swap(): return lax.ppermute(x, axis, [(i, i ^ bit) for i in range(n)])]
    pallas_call x4 -> x7, Pallas kernels: 9.23 us -> 19.1 us  [call(): pl.pallas_call(kernel, out_shape=out_shape, in_specs=[smem, hbm] + [vmem]...]
    ppermute x16, starting transfers between devices: 23.1 us -> 28.7 us  [shift(): return lax.ppermute(x, 'z', [(i, (i + step) % N_Z) for i in range(N_Z)])]
    ppermute x16, waiting for transfers between devices: 11.9 us -> 8.37 us  [shift(): return lax.ppermute(x, 'z', [(i, (i + step) % N_Z) for i in range(N_Z)])]
    all_to_all x1, waiting for transfers between devices: 0.69 us -> 3.72 us  [on_device(): grads = lax.all_to_all(payload, REP, 0, 0, tiled=True)]
    ppermute x1, waiting for transfers between devices: 0.01 us -> 2.8 us  [on_device(): far_give = lax.ppermute(give, ('z', 'core'), ring).astype(f32)]
    all_to_all x1, blocking collectives: 22.2 us -> 24.5 us  [on_device(): parts = lax.all_to_all(partial, REP, 0, 0, tiled=True)]
  transfers between devices with their start and end apart: 46 -> 44, of which waited for: 24 -> 14; matrix products, arithmetic and copies ran while one was open for 0% -> 1% of each run, Pallas kernels for 3% -> 9%
where the time goes in v7:
time: 152 us; the launch traced here: 151 us
  starting transfers between devices  65.9 us (43%)
  waiting for transfers between devices  33 us (22%)
  blocking collectives  24.5 us (16%)
  Pallas kernels  23.9 us (16%)
  other arithmetic  2.08 us (1%)
  between operations  1.72 us (1%)
    ppermute x26, starting transfers between devices, xor_swap(): return lax.ppermute(x, axis, [(i, i ^ bit) for i in range(n)])  30.9 us
    ppermute x16, starting transfers between devices, shift(): return lax.ppermute(x, 'z', [(i, (i + step) % N_Z) for i in range(N_Z)])  28.7 us
    all_to_all x1, blocking collectives, on_device(): parts = lax.all_to_all(partial, REP, 0, 0, tiled=True)  24.5 us
    pallas_call x7, Pallas kernels, call(): pl.pallas_call(kernel, out_shape=out_shape, in_specs=[smem, hbm] + [vmem]...  19.1 us
    ppermute x26, waiting for transfers between devices, xor_swap(): return lax.ppermute(x, axis, [(i, i ^ bit) for i in range(n)])  18.1 us
    ppermute x16, waiting for transfers between devices, shift(): return lax.ppermute(x, 'z', [(i, (i + step) % N_Z) for i in range(N_Z)])  8.37 us
    all_to_all x1, waiting for transfers between devices, on_device(): grads = lax.all_to_all(payload, REP, 0, 0, tiled=True)  3.72 us
    all_to_all x1, starting transfers between devices, on_device(): grads = lax.all_to_all(payload, REP, 0, 0, tiled=True)  3.56 us
  transfers between devices with their start and end apart: 44, of which 14 were waited for; matrix products, arithmetic and copies ran while one was open for 1% of the time, Pallas kernels for 9%

profile of v7, /device:TPU:1, one launch (start us, length us, event | category | flops | bytes accessed | tf_op | source)
XLA Modules:
  0.0 151.2 jit_solution(3763537389568253150)
XLA Ops:
  0.6 6.5 %collective-permute-start.5 = (bf16[256,256]{1,0:T(8,128)(2,1)}, bf16[256,256]{1,0:T(8,128)(2,1)S(1)}, u32[]{:S(2)}, u32[]{:S(2)}) collective-permute-start(bf16[256,256]{1,0:T(8,128)(2,1)} %refs_0_.1), channel_id=1, source_target_pairs={{0,28},{4,0},{8,4},{12,8},{16,12},{20,16},{24,20},{28,24},{1,29},{... | collective-permute-start | bytes 393224 | tf_op jit(solution)/shard_map/gather_features/ppermute | solution.py:39
  7.1 2.5 %collective-permute-done.5.refs_1_ = bf16[256,256]{1,0:T(8,128)(2,1)S(1)} collective-permute-done((bf16[256,256]{1,0:T(8,128)(2,1)}, bf16[256,256]{1,0:T(8,128)(2,1)S(1)}, u32[]{:S(2)}, u32[]{:S(2)}) %collective-permute-start.5) | collective-permute-done | bytes 131104 | tf_op jit(solution)/shard_map/gather_features/ppermute | solution.py:39
  9.6 3.3 %collective-permute-start.7 = (bf16[256,256]{1,0:T(8,128)(2,1)S(1)}, bf16[256,256]{1,0:T(8,128)(2,1)S(1)}, u32[]{:S(2)}, u32[]{:S(2)}) collective-permute-start(bf16[256,256]{1,0:T(8,128)(2,1)S(1)} %collective-permute-done.5.refs_1_), channel_id=1, source_target_pairs={{0,28},{4,0},{8,4},{12,8},{16,12},{20,16},{24,20},{28,24},{1,29},{... | collective-permute-start | bytes 393224 | tf_op jit(solution)/shard_map/gather_features/ppermute | solution.py:39
  15.6 2.7 %collective-permute-start.9 = (bf16[256,256]{1,0:T(8,128)(2,1)S(1)}, bf16[256,256]{1,0:T(8,128)(2,1)S(1)}, u32[]{:S(2)}, u32[]{:S(2)}) collective-permute-start(bf16[256,256]{1,0:T(8,128)(2,1)S(1)} %collective-permute-done.7.refs_2_), channel_id=1, source_target_pairs={{0,28},{4,0},{8,4},{12,8},{16,12},{20,16},{24,20},{28,24},{1,29},{... | collective-permute-start | bytes 393224 | tf_op jit(solution)/shard_map/gather_features/ppermute | solution.py:39
  21.1 3.2 %collective-permute-start.13 = (bf16[128,256]{1,0:T(8,128)(2,1)S(1)}, bf16[128,256]{1,0:T(8,128)(2,1)S(1)}, u32[]{:S(2)}, u32[]{:S(2)}) collective-permute-start(bf16[128,256]{1,0:T(8,128)(2,1)S(1)} %slice.100), channel_id=1, source_target_pairs={{0,28},{4,0},{8,4},{12,8},{16,12},{20,16},{24,20},{28,24},{1,29},{... | collective-permute-start | bytes 196616 | tf_op jit(solution)/shard_map/gather_features/ppermute | solution.py:39
  26.5 2.2 %collective-permute-done.11.refs_4_ = bf16[128,256]{1,0:T(8,128)(2,1)S(1)} collective-permute-done((bf16[128,256]{1,0:T(8,128)(2,1)S(1)}, bf16[128,256]{1,0:T(8,128)(2,1)S(1)}, u32[]{:S(2)}, u32[]{:S(2)}) %collective-permute-start.11) | collective-permute-done | bytes 65568 | tf_op jit(solution)/shard_map/gather_features/ppermute | solution.py:39
  30.6 6.2 %collective-permute-start.18 = (bf16[8,256,256]{2,1,0:T(8,128)(2,1)S(1)}, bf16[8,256,256]{2,1,0:T(8,128)(2,1)S(1)}, u32[]{:S(2)}, u32[]{:S(2)}) collective-permute-start(bf16[8,256,256]{2,1,0:T(8,128)(2,1)S(1)} %assemble_own.1.near), channel_id=1, source_target_pairs={{0,1},{1,0},{2,3},{3,2},{4,5},{5,4},{6,7},{7,6},{8,9},{9,8},{10,11... | collective-permute-start | bytes 3145736 | tf_op jit(solution)/shard_map/gather_features/ppermute | solution.py:31
  38.2 2.2 %collective-permute-start.17 = (bf16[8,256,256]{2,1,0:T(8,128)(2,1)S(1)}, bf16[8,256,256]{2,1,0:T(8,128)(2,1)}, u32[]{:S(2)}, u32[]{:S(2)}) collective-permute-start(bf16[8,256,256]{2,1,0:T(8,128)(2,1)S(1)} %assemble_crossed.1.feats), channel_id=1, source_target_pairs={{0,1},{1,0},{2,3},{3,2},{4,5},{5,4},{6,7},{7,6},{8,9},{9,8},{10,11... | collective-permute-start | bytes 3145736 | tf_op jit(solution)/shard_map/gather_features/ppermute | solution.py:31
  41.4 3.3 %tile_products_first.1.before = f32[17,128,256]{2,1,0:T(8,128)S(1)} custom-call(s32[2,256]{1,0:T(2,128)S(1)} %concatenate.9.table.refs_0_, bf16[128,128,128]{2,1,0:T(8,128)(2,1)} %bitcast.58, bf16[8,256,256]{2,1,0:T(8,128)(2,1)S(1)} %assemble_own.1.near, bf16[8,256,256]{2,1,0:T(8,128)(2,1)S(1)} %collective-permute-done.18.far), custom_call_target="tpu_custom_call" | custom-call | flops 1 | bytes 1 | tf_op jit(solution)/shard_map/tile_products/tile_products_first/pallas_call | solution.py:233
  44.7 2.5 %tile_products_near.1.before = f32[17,128,256]{2,1,0:T(8,128)S(1)} custom-call(s32[2,256]{1,0:T(2,128)S(1)} %concatenate.9.table.refs_0_, bf16[128,128,128]{2,1,0:T(8,128)(2,1)} %bitcast.59, bf16[8,256,256]{2,1,0:T(8,128)(2,1)S(1)} %assemble_crossed.1.feats, f32[17,128,256]{2,1,0:T(8,128)S(1)} %tile_products_first.1.before), custom_call_target="tpu_custom_call" | custom-call | flops 1 | bytes 1 | tf_op jit(solution)/shard_map/tile_products/tile_products_near/pallas_call | solution.py:233
  47.3 3.0 %tile_products_far.1 = bf16[8,256,256]{2,1,0:T(8,128)(2,1)S(1)} custom-call(s32[2,256]{1,0:T(2,128)S(1)} %concatenate.9.table.refs_0_, bf16[128,128,128]{2,1,0:T(8,128)(2,1)} %bitcast.60, bf16[8,256,256]{2,1,0:T(8,128)(2,1)} %collective-permute-done.17.feats, f32[17,128,256]{2,1,0:T(8,128)S(1)} %tile_products_near.1.before), custom_call_target="tpu_custom_call" | custom-call | flops 1 | bytes 1 | tf_op jit(solution)/shard_map/tile_products/tile_products_far/pallas_call | solution.py:233
  50.3 24.5 %all_to_all.10.parts = bf16[8,256,256]{2,1,0:T(8,128)(2,1)S(1)} all-to-all(bf16[8,256,256]{2,1,0:T(8,128)(2,1)S(1)} %tile_products_far.1), channel_id=1, replica_groups=mesh['y'=4,'xh'=2,'z'=8,'xl'=2,'core'=2] {'y','xh'}, dimensions={0} | all-to-all | bytes 2097152 | tf_op jit(solution)/shard_map/sum_partials/all_to_all | solution.py:292
  76.2 3.6 %all-to-all-start.1 = ((bf16[8,256,256]{2,1,0:T(8,128)(2,1)}), bf16[8,256,256]{2,1,0:T(8,128)(2,1)S(1)}, u32[]{:S(2)}, u32[]{:S(2)}) async-start(bf16[8,256,256]{2,1,0:T(8,128)(2,1)} %get-tuple-element.23), calls=%async_computation.1 | async-start | bytes 2097152 | tf_op jit(solution)/shard_map/share_gradients/all_to_all | solution.py:310
  79.8 2.7 %collective-permute-start.21 = (bf16[128,256]{1,0:T(8,128)(2,1)S(1)}, bf16[128,256]{1,0:T(8,128)(2,1)S(1)}, u32[]{:S(2)}, u32[]{:S(2)}) collective-permute-start(bf16[128,256]{1,0:T(8,128)(2,1)S(1)} %get-tuple-element.25), channel_id=1, source_target_pairs={{0,5},{1,4},{4,1},{5,0},{8,13},{9,12},{12,9},{13,8},{16,21},{17,20... | collective-permute-start | bytes 196616 | tf_op jit(solution)/shard_map/weight_z/ppermute | solution.py:314
  82.9 2.8 %collective-permute-done.21 = bf16[128,256]{1,0:T(8,128)(2,1)S(1)} collective-permute-done((bf16[128,256]{1,0:T(8,128)(2,1)S(1)}, bf16[128,256]{1,0:T(8,128)(2,1)S(1)}, u32[]{:S(2)}, u32[]{:S(2)}) %collective-permute-start.21) | collective-permute-done | bytes 65568 | tf_op jit(solution)/shard_map/weight_z/ppermute | solution.py:314
  86.9 4.8 %collective-permute-done.22 = bf16[128,256]{1,0:T(8,128)(2,1)S(1)} collective-permute-done((bf16[128,256]{1,0:T(8,128)(2,1)S(1)}, bf16[128,256]{1,0:T(8,128)(2,1)S(1)}, u32[]{:S(2)}, u32[]{:S(2)}) %collective-permute-start.22) | collective-permute-done | bytes 65568 | tf_op jit(solution)/shard_map/weight_z/ppermute | solution.py:31
  91.8 3.7 %all-to-all-done.1.refs_2_ = bf16[8,256,256]{2,1,0:T(8,128)(2,1)S(1)} async-done(((bf16[8,256,256]{2,1,0:T(8,128)(2,1)}), bf16[8,256,256]{2,1,0:T(8,128)(2,1)S(1)}, u32[]{:S(2)}, u32[]{:S(2)}) %all-to-all-start.1) | async-done | bytes 1048608 | tf_op jit(solution)/shard_map/share_gradients/all_to_all | solution.py:310
  95.5 2.4 %back_crossed_far.1 = bf16[8,256,256]{2,1,0:T(8,128)(2,1)S(1)} custom-call(s32[2,256]{1,0:T(2,128)S(1)} %concatenate.9.table.refs_0_, bf16[128,128,128]{2,1,0:T(8,128)(2,1)} %bitcast.61, bf16[8,256,256]{2,1,0:T(8,128)(2,1)S(1)} %all-to-all-done.1.refs_2_), custom_call_target="tpu_custom_call" | custom-call | flops 1 | bytes 1 | tf_op jit(solution)/shard_map/back_crossed/back_crossed_far/pallas_call | solution.py:233
  97.9 2.8 %collective-permute-start.23 = (bf16[8,256,256]{2,1,0:T(8,128)(2,1)S(1)}, bf16[8,256,256]{2,1,0:T(8,128)(2,1)S(1)}, u32[]{:S(2)}, u32[]{:S(2)}) collective-permute-start(bf16[8,256,256]{2,1,0:T(8,128)(2,1)S(1)} %back_crossed_far.1), channel_id=1, source_target_pairs={{0,1},{1,0},{2,3},{3,2},{4,5},{5,4},{6,7},{7,6},{8,9},{9,8},{10,11... | collective-permute-start | bytes 3145736 | tf_op jit(solution)/shard_map/back_crossed/ppermute | solution.py:31
  100.7 2.7 %back_crossed_near.1 = bf16[8,256,256]{2,1,0:T(8,128)(2,1)S(1)} custom-call(s32[2,256]{1,0:T(2,128)S(1)} %concatenate.9.table.refs_0_, bf16[128,128,128]{2,1,0:T(8,128)(2,1)} %bitcast.62, bf16[8,256,256]{2,1,0:T(8,128)(2,1)S(1)} %all-to-all-done.1.refs_2_), custom_call_target="tpu_custom_call" | custom-call | flops 1 | bytes 1 | tf_op jit(solution)/shard_map/back_crossed/back_crossed_near/pallas_call | solution.py:233
  103.7 2.7 %back_own_far.1 = bf16[8,256,256]{2,1,0:T(8,128)(2,1)S(1)} custom-call(s32[2,256]{1,0:T(2,128)S(1)} %concatenate.9.table.refs_0_, bf16[128,128,128]{2,1,0:T(8,128)(2,1)} %bitcast.63, bf16[8,256,256]{2,1,0:T(8,128)(2,1)S(1)} %all-to-all-done.1.refs_2_), custom_call_target="tpu_custom_call" | custom-call | flops 1 | bytes 1 | tf_op jit(solution)/shard_map/back_own/back_own_far/pallas_call | solution.py:233
  106.7 2.4 %back_own_near.1 = bf16[8,256,256]{2,1,0:T(8,128)(2,1)S(1)} custom-call(s32[2,256]{1,0:T(2,128)S(1)} %concatenate.9.table.refs_0_, bf16[128,128,128]{2,1,0:T(8,128)(2,1)} %bitcast.64, bf16[8,256,256]{2,1,0:T(8,128)(2,1)S(1)} %all-to-all-done.1.refs_2_), custom_call_target="tpu_custom_call" | custom-call | flops 1 | bytes 1 | tf_op jit(solution)/shard_map/back_own/back_own_near/pallas_call | solution.py:233
  115.0 2.5 %collective-permute-start.35 = (bf16[128,256]{1,0:T(8,128)(2,1)S(1)}, bf16[128,256]{1,0:T(8,128)(2,1)S(1)}, u32[]{:S(2)}, u32[]{:S(2)}) collective-permute-start(bf16[128,256]{1,0:T(8,128)(2,1)S(1)} %get-tuple-element.41), channel_id=1, source_target_pairs={{0,4},{4,8},{8,12},{12,16},{16,20},{20,24},{24,28},{28,0},{1,5},{5... | collective-permute-start | bytes 196616 | tf_op jit(solution)/shard_map/scatter_gradients/ppermute | solution.py:39
  117.5 3.0 %collective-permute-done.25 = bf16[128,256]{1,0:T(8,128)(2,1)S(1)} collective-permute-done((bf16[128,256]{1,0:T(8,128)(2,1)S(1)}, bf16[128,256]{1,0:T(8,128)(2,1)S(1)}, u32[]{:S(2)}, u32[]{:S(2)}) %collective-permute-start.25) | collective-permute-done | bytes 65568 | tf_op jit(solution)/shard_map/weight_rest/ppermute | solution.py:31
  120.6 2.1 %collective-permute-start.39 = (bf16[128,256]{1,0:T(8,128)(2,1)S(1)}, bf16[128,256]{1,0:T(8,128)(2,1)S(1)}, u32[]{:S(2)}, u32[]{:S(2)}) collective-permute-start(bf16[128,256]{1,0:T(8,128)(2,1)S(1)} %get-tuple-element.42), channel_id=1, source_target_pairs={{0,28},{4,0},{8,4},{12,8},{16,12},{20,16},{24,20},{28,24},{1,29},{... | collective-permute-start | bytes 196616 | tf_op jit(solution)/shard_map/scatter_gradients/ppermute | solution.py:39
  122.7 2.2 %collective-permute-done.33 = bf16[2,256,256]{2,1,0:T(8,128)(2,1)S(1)} collective-permute-done((bf16[2,256,256]{2,1,0:T(8,128)(2,1)S(1)}, bf16[2,256,256]{2,1,0:T(8,128)(2,1)S(1)}, u32[]{:S(2)}, u32[]{:S(2)}) %collective-permute-start.33) | collective-permute-done | bytes 262176 | tf_op jit(solution)/shard_map/scatter_gradients/ppermute | solution.py:31
  124.9 3.4 %collective-permute-start.26 = (bf16[128,256]{1,0:T(8,128)(2,1)S(1)}, bf16[128,256]{1,0:T(8,128)(2,1)S(1)}, u32[]{:S(2)}, u32[]{:S(2)}) collective-permute-start(bf16[128,256]{1,0:T(8,128)(2,1)S(1)} %add_convert_fusion.6), channel_id=1, source_target_pairs={{0,32},{32,0},{1,33},{33,1},{2,34},{34,2},{3,35},{35,3},{4,36},{36... | collective-permute-start | bytes 196616 | tf_op jit(solution)/shard_map/weight_rest/ppermute | solution.py:31
  128.5 2.7 %collective-permute-start.40 = (bf16[256,256]{1,0:T(8,128)(2,1)S(1)}, bf16[256,256]{1,0:T(8,128)(2,1)S(1)}, u32[]{:S(2)}, u32[]{:S(2)}) collective-permute-start(bf16[256,256]{1,0:T(8,128)(2,1)S(1)} %get-tuple-element.38), channel_id=1, source_target_pairs={{0,28},{4,0},{8,4},{12,8},{16,12},{20,16},{24,20},{28,24},{1,29},{... | collective-permute-start | bytes 393224 | tf_op jit(solution)/shard_map/scatter_gradients/ppermute | solution.py:39
  131.1 6.5 %collective-permute-done.26 = bf16[128,256]{1,0:T(8,128)(2,1)S(1)} collective-permute-done((bf16[128,256]{1,0:T(8,128)(2,1)S(1)}, bf16[128,256]{1,0:T(8,128)(2,1)S(1)}, u32[]{:S(2)}, u32[]{:S(2)}) %collective-permute-start.26) | collective-permute-done | bytes 65568 | tf_op jit(solution)/shard_map/weight_rest/ppermute | solution.py:31
  138.0 2.7 %collective-permute-start.41 = (bf16[256,256]{1,0:T(8,128)(2,1)S(1)}, bf16[256,256]{1,0:T(8,128)(2,1)S(1)}, u32[]{:S(2)}, u32[]{:S(2)}) collective-permute-start(bf16[256,256]{1,0:T(8,128)(2,1)S(1)} %get-tuple-element.36), channel_id=1, source_target_pairs={{0,28},{4,0},{8,4},{12,8},{16,12},{20,16},{24,20},{28,24},{1,29},{... | collective-permute-start | bytes 393224 | tf_op jit(solution)/shard_map/scatter_gradients/ppermute | solution.py:39
  143.2 2.7 %collective-permute-start.42 = (bf16[256,256]{1,0:T(8,128)(2,1)S(1)}, bf16[256,256]{1,0:T(8,128)(2,1)S(1)}, u32[]{:S(2)}, u32[]{:S(2)}) collective-permute-start(bf16[256,256]{1,0:T(8,128)(2,1)S(1)} %get-tuple-element.34), channel_id=1, source_target_pairs={{0,28},{4,0},{8,4},{12,8},{16,12},{20,16},{24,20},{28,24},{1,29},{... | collective-permute-start | bytes 393224 | tf_op jit(solution)/shard_map/scatter_gradients/ppermute | solution.py:39
  146.0 2.8 %collective-permute-start.29 = (bf16[128,256]{1,0:T(8,128)(2,1)S(1)}, bf16[128,256]{1,0:T(8,128)(2,1)S(1)}, u32[]{:S(2)}, u32[]{:S(2)}) collective-permute-start(bf16[128,256]{1,0:T(8,128)(2,1)S(1)} %add_convert_fusion.3.mine), channel_id=1, source_target_pairs={{0,1},{1,0},{2,3},{3,2},{4,5},{5,4},{6,7},{7,6},{8,9},{9,8},{10,11... | collective-permute-start | bytes 196616 | tf_op jit(solution)/shard_map/weight_rest/ppermute | solution.py:31
  (101 shorter events, 26.2 us)
Async XLA Ops:
  0.6 9.0 %collective-permute-start.5 = (bf16[256,256]{1,0:T(8,128)(2,1)}, bf16[256,256]{1,0:T(8,128)(2,1)S(1)}, u32[]{:S(2)}, u32[]{:S(2)}) collective-permute-start(bf16[256,256]{1,0:T(8,128)(2,1)} %refs_0_.1), channel_id=1, source_target_pairs={{0,28},{4,0},{8,4},{12,8},{16,12},{20,16},{24,20},{28,24},{1,29},{... | collective-permute-start | bytes 393224 | tf_op jit(solution)/shard_map/gather_features/ppermute | solution.py:39
  7.1 7.0 %collective-permute-start = (bf16[256,256]{1,0:T(8,128)(2,1)}, bf16[256,256]{1,0:T(8,128)(2,1)S(1)}, u32[]{:S(2)}, u32[]{:S(2)}) collective-permute-start(bf16[256,256]{1,0:T(8,128)(2,1)} %refs_0_.1), channel_id=1, source_target_pairs={{0,4},{4,8},{8,12},{12,16},{16,20},{20,24},{24,28},{28,0},{1,5},{5... | collective-permute-start | bytes 393224 | tf_op jit(solution)/shard_map/gather_features/ppermute | solution.py:39
  9.6 6.0 %collective-permute-start.7 = (bf16[256,256]{1,0:T(8,128)(2,1)S(1)}, bf16[256,256]{1,0:T(8,128)(2,1)S(1)}, u32[]{:S(2)}, u32[]{:S(2)}) collective-permute-start(bf16[256,256]{1,0:T(8,128)(2,1)S(1)} %collective-permute-done.5.refs_1_), channel_id=1, source_target_pairs={{0,28},{4,0},{8,4},{12,8},{16,12},{20,16},{24,20},{28,24},{1,29},{... | collective-permute-start | bytes 393224 | tf_op jit(solution)/shard_map/gather_features/ppermute | solution.py:39
  12.9 5.4 %collective-permute-start.2 = (bf16[256,256]{1,0:T(8,128)(2,1)}, bf16[256,256]{1,0:T(8,128)(2,1)S(1)}, u32[]{:S(2)}, u32[]{:S(2)}) collective-permute-start(bf16[256,256]{1,0:T(8,128)(2,1)} %refs_0_.1), channel_id=1, source_target_pairs={{0,2},{2,0},{1,3},{3,1},{4,6},{6,4},{5,7},{7,5},{8,10},{10,8},{9,1... | collective-permute-start | bytes 393224 | tf_op jit(solution)/shard_map/gather_features/ppermute | solution.py:31
  14.1 7.0 %collective-permute-start.4 = (bf16[256,256]{1,0:T(8,128)(2,1)S(1)}, bf16[256,256]{1,0:T(8,128)(2,1)S(1)}, u32[]{:S(2)}, u32[]{:S(2)}) collective-permute-start(bf16[256,256]{1,0:T(8,128)(2,1)S(1)} %collective-permute-done.refs_8_), channel_id=1, source_target_pairs={{0,2},{2,0},{1,3},{3,1},{4,6},{6,4},{5,7},{7,5},{8,10},{10,8},{9,1... | collective-permute-start | bytes 393224 | tf_op jit(solution)/shard_map/gather_features/ppermute | solution.py:31
  14.4 9.9 %collective-permute-start.6 = (bf16[256,256]{1,0:T(8,128)(2,1)S(1)}, bf16[256,256]{1,0:T(8,128)(2,1)S(1)}, u32[]{:S(2)}, u32[]{:S(2)}) collective-permute-start(bf16[256,256]{1,0:T(8,128)(2,1)S(1)} %collective-permute-done.5.refs_1_), channel_id=1, source_target_pairs={{0,2},{2,0},{1,3},{3,1},{4,6},{6,4},{5,7},{7,5},{8,10},{10,8},{9,1... | collective-permute-start | bytes 393224 | tf_op jit(solution)/shard_map/gather_features/ppermute | solution.py:31
  19.1 5.9 %collective-permute-start.16 = (bf16[256,256]{1,0:T(8,128)(2,1)S(1)}, bf16[256,256]{1,0:T(8,128)(2,1)S(1)}, u32[]{:S(2)}, u32[]{:S(2)}) collective-permute-start(bf16[256,256]{1,0:T(8,128)(2,1)S(1)} %collective-permute-done.1.refs_7_), channel_id=1, source_target_pairs={{0,2},{2,0},{1,3},{3,1},{4,6},{6,4},{5,7},{7,5},{8,10},{10,8},{9,1... | collective-permute-start | bytes 393224 | tf_op jit(solution)/shard_map/gather_features/ppermute | solution.py:31
  20.2 10.3 %collective-permute-start.8 = (bf16[256,256]{1,0:T(8,128)(2,1)S(1)}, bf16[256,256]{1,0:T(8,128)(2,1)S(1)}, u32[]{:S(2)}, u32[]{:S(2)}) collective-permute-start(bf16[256,256]{1,0:T(8,128)(2,1)S(1)} %collective-permute-done.7.refs_2_), channel_id=1, source_target_pairs={{0,2},{2,0},{1,3},{3,1},{4,6},{6,4},{5,7},{7,5},{8,10},{10,8},{9,1... | collective-permute-start | bytes 393224 | tf_op jit(solution)/shard_map/gather_features/ppermute | solution.py:31
  24.4 12.3 %collective-permute-start.10 = (bf16[256,256]{1,0:T(8,128)(2,1)S(1)}, bf16[256,256]{1,0:T(8,128)(2,1)S(1)}, u32[]{:S(2)}, u32[]{:S(2)}) collective-permute-start(bf16[256,256]{1,0:T(8,128)(2,1)S(1)} %collective-permute-done.9.refs_3_), channel_id=1, source_target_pairs={{0,2},{2,0},{1,3},{3,1},{4,6},{6,4},{5,7},{7,5},{8,10},{10,8},{9,1... | collective-permute-start | bytes 393224 | tf_op jit(solution)/shard_map/gather_features/ppermute | solution.py:31
  25.1 11.7 %collective-permute-start.15 = (bf16[256,256]{1,0:T(8,128)(2,1)S(1)}, bf16[256,256]{1,0:T(8,128)(2,1)S(1)}, u32[]{:S(2)}, u32[]{:S(2)}) collective-permute-start(bf16[256,256]{1,0:T(8,128)(2,1)S(1)} %collective-permute-done.3.refs_6_), channel_id=1, source_target_pairs={{0,2},{2,0},{1,3},{3,1},{4,6},{6,4},{5,7},{7,5},{8,10},{10,8},{9,1... | collective-permute-start | bytes 393224 | tf_op jit(solution)/shard_map/gather_features/ppermute | solution.py:31
  25.9 10.8 %collective-permute-start.14 = (bf16[128,256]{1,0:T(8,128)(2,1)S(1)}, bf16[128,256]{1,0:T(8,128)(2,1)S(1)}, u32[]{:S(2)}, u32[]{:S(2)}) collective-permute-start(bf16[128,256]{1,0:T(8,128)(2,1)S(1)} %collective-permute-done.13.refs_5_), channel_id=1, source_target_pairs={{0,2},{2,0},{1,3},{3,1},{4,6},{6,4},{5,7},{7,5},{8,10},{10,8},{9,1... | collective-permute-start | bytes 196616 | tf_op jit(solution)/shard_map/gather_features/ppermute | solution.py:31
  28.7 8.0 %collective-permute-start.12 = (bf16[128,256]{1,0:T(8,128)(2,1)S(1)}, bf16[128,256]{1,0:T(8,128)(2,1)S(1)}, u32[]{:S(2)}, u32[]{:S(2)}) collective-permute-start(bf16[128,256]{1,0:T(8,128)(2,1)S(1)} %collective-permute-done.11.refs_4_), channel_id=1, source_target_pairs={{0,2},{2,0},{1,3},{3,1},{4,6},{6,4},{5,7},{7,5},{8,10},{10,8},{9,1... | collective-permute-start | bytes 196616 | tf_op jit(solution)/shard_map/gather_features/ppermute | solution.py:31
  30.6 10.9 %collective-permute-start.18 = (bf16[8,256,256]{2,1,0:T(8,128)(2,1)S(1)}, bf16[8,256,256]{2,1,0:T(8,128)(2,1)S(1)}, u32[]{:S(2)}, u32[]{:S(2)}) collective-permute-start(bf16[8,256,256]{2,1,0:T(8,128)(2,1)S(1)} %assemble_own.1.near), channel_id=1, source_target_pairs={{0,1},{1,0},{2,3},{3,2},{4,5},{5,4},{6,7},{7,6},{8,9},{9,8},{10,11... | collective-permute-start | bytes 3145736 | tf_op jit(solution)/shard_map/gather_features/ppermute | solution.py:31
  38.2 9.0 %collective-permute-start.17 = (bf16[8,256,256]{2,1,0:T(8,128)(2,1)S(1)}, bf16[8,256,256]{2,1,0:T(8,128)(2,1)}, u32[]{:S(2)}, u32[]{:S(2)}) collective-permute-start(bf16[8,256,256]{2,1,0:T(8,128)(2,1)S(1)} %assemble_crossed.1.feats), channel_id=1, source_target_pairs={{0,1},{1,0},{2,3},{3,2},{4,5},{5,4},{6,7},{7,6},{8,9},{9,8},{10,11... | collective-permute-start | bytes 3145736 | tf_op jit(solution)/shard_map/gather_features/ppermute | solution.py:31
  76.2 19.3 %all-to-all-start.1 = ((bf16[8,256,256]{2,1,0:T(8,128)(2,1)}), bf16[8,256,256]{2,1,0:T(8,128)(2,1)S(1)}, u32[]{:S(2)}, u32[]{:S(2)}) async-start(bf16[8,256,256]{2,1,0:T(8,128)(2,1)} %get-tuple-element.23), calls=%async_computation.1 | async-start | bytes 2097152 | tf_op jit(solution)/shard_map/share_gradients/all_to_all | solution.py:310
  79.8 5.9 %collective-permute-start.21 = (bf16[128,256]{1,0:T(8,128)(2,1)S(1)}, bf16[128,256]{1,0:T(8,128)(2,1)S(1)}, u32[]{:S(2)}, u32[]{:S(2)}) collective-permute-start(bf16[128,256]{1,0:T(8,128)(2,1)S(1)} %get-tuple-element.25), channel_id=1, source_target_pairs={{0,5},{1,4},{4,1},{5,0},{8,13},{9,12},{12,9},{13,8},{16,21},{17,20... | collective-permute-start | bytes 196616 | tf_op jit(solution)/shard_map/weight_z/ppermute | solution.py:314
  85.8 6.0 %collective-permute-start.22 = (bf16[128,256]{1,0:T(8,128)(2,1)S(1)}, bf16[128,256]{1,0:T(8,128)(2,1)S(1)}, u32[]{:S(2)}, u32[]{:S(2)}) collective-permute-start(bf16[128,256]{1,0:T(8,128)(2,1)S(1)} %add_convert_fusion.9), channel_id=1, source_target_pairs={{0,8},{4,12},{8,0},{12,4},{16,24},{20,28},{24,16},{28,20},{1,9},{5... | collective-permute-start | bytes 196616 | tf_op jit(solution)/shard_map/weight_z/ppermute | solution.py:31
  97.9 5.5 %collective-permute-start.23 = (bf16[8,256,256]{2,1,0:T(8,128)(2,1)S(1)}, bf16[8,256,256]{2,1,0:T(8,128)(2,1)S(1)}, u32[]{:S(2)}, u32[]{:S(2)}) collective-permute-start(bf16[8,256,256]{2,1,0:T(8,128)(2,1)S(1)} %back_crossed_far.1), channel_id=1, source_target_pairs={{0,1},{1,0},{2,3},{3,2},{4,5},{5,4},{6,7},{7,6},{8,9},{9,8},{10,11... | collective-permute-start | bytes 3145736 | tf_op jit(solution)/shard_map/back_crossed/ppermute | solution.py:31
  106.5 6.2 %collective-permute-start.30 = (bf16[8,256,256]{2,1,0:T(8,128)(2,1)S(1)}, bf16[8,256,256]{2,1,0:T(8,128)(2,1)S(1)}, u32[]{:S(2)}, u32[]{:S(2)}) collective-permute-start(bf16[8,256,256]{2,1,0:T(8,128)(2,1)S(1)} %back_own_far.1), channel_id=1, source_target_pairs={{0,1},{1,0},{2,3},{3,2},{4,5},{5,4},{6,7},{7,6},{8,9},{9,8},{10,11... | collective-permute-start | bytes 3145736 | tf_op jit(solution)/shard_map/back_own/ppermute | solution.py:31
  106.6 6.0 %collective-permute-start.24 = (bf16[128,256]{1,0:T(8,128)(2,1)S(1)}, bf16[128,256]{1,0:T(8,128)(2,1)S(1)}, u32[]{:S(2)}, u32[]{:S(2)}) collective-permute-start(bf16[128,256]{1,0:T(8,128)(2,1)S(1)} %add_convert_fusion.8), channel_id=1, source_target_pairs={{0,2},{2,0},{1,3},{3,1},{4,6},{6,4},{5,7},{7,5},{8,10},{10,8},{9,1... | collective-permute-start | bytes 196616 | tf_op jit(solution)/shard_map/weight_rest/ppermute | solution.py:31
  109.2 5.8 %collective-permute-start.34 = (bf16[1,256,256]{2,1,0:T(8,128)(2,1)S(1)}, bf16[1,256,256]{2,1,0:T(8,128)(2,1)S(1)}, u32[]{:S(2)}, u32[]{:S(2)}) collective-permute-start(bf16[1,256,256]{2,1,0:T(8,128)(2,1)S(1)} %slice.89), channel_id=1, source_target_pairs={{0,2},{2,0},{1,3},{3,1},{4,6},{6,4},{5,7},{7,5},{8,10},{10,8},{9,1... | collective-permute-start | bytes 393224 | tf_op jit(solution)/shard_map/scatter_gradients/ppermute | solution.py:31
  111.0 26.8 %collective-permute-start.32 = (bf16[2,256,256]{2,1,0:T(8,128)(2,1)S(1)}, bf16[2,256,256]{2,1,0:T(8,128)(2,1)S(1)}, u32[]{:S(2)}, u32[]{:S(2)}) collective-permute-start(bf16[2,256,256]{2,1,0:T(8,128)(2,1)S(1)} %get-tuple-element.39), channel_id=1, source_target_pairs={{0,2},{2,0},{1,3},{3,1},{4,6},{6,4},{5,7},{7,5},{8,10},{10,8},{9,1... | collective-permute-start | bytes 786440 | tf_op jit(solution)/shard_map/scatter_gradients/ppermute | solution.py:31
  111.1 13.8 %collective-permute-start.33 = (bf16[2,256,256]{2,1,0:T(8,128)(2,1)S(1)}, bf16[2,256,256]{2,1,0:T(8,128)(2,1)S(1)}, u32[]{:S(2)}, u32[]{:S(2)}) collective-permute-start(bf16[2,256,256]{2,1,0:T(8,128)(2,1)S(1)} %get-tuple-element.40), channel_id=1, source_target_pairs={{0,2},{2,0},{1,3},{3,1},{4,6},{6,4},{5,7},{7,5},{8,10},{10,8},{9,1... | collective-permute-start | bytes 786440 | tf_op jit(solution)/shard_map/scatter_gradients/ppermute | solution.py:31
  112.5 28.5 %collective-permute-start.31 = (bf16[3,256,256]{2,1,0:T(8,128)(2,1)S(1)}, bf16[3,256,256]{2,1,0:T(8,128)(2,1)S(1)}, u32[]{:S(2)}, u32[]{:S(2)}) collective-permute-start(bf16[3,256,256]{2,1,0:T(8,128)(2,1)S(1)} %slice.78), channel_id=1, source_target_pairs={{0,2},{2,0},{1,3},{3,1},{4,6},{6,4},{5,7},{7,5},{8,10},{10,8},{9,1... | collective-permute-start | bytes 1179656 | tf_op jit(solution)/shard_map/scatter_gradients/ppermute | solution.py:31
  112.6 7.9 %collective-permute-start.25 = (bf16[128,256]{1,0:T(8,128)(2,1)S(1)}, bf16[128,256]{1,0:T(8,128)(2,1)S(1)}, u32[]{:S(2)}, u32[]{:S(2)}) collective-permute-start(bf16[128,256]{1,0:T(8,128)(2,1)S(1)} %add_convert_fusion.7), channel_id=1, source_target_pairs={{0,16},{4,20},{8,24},{12,28},{16,0},{20,4},{24,8},{28,12},{1,17},{... | collective-permute-start | bytes 196616 | tf_op jit(solution)/shard_map/weight_rest/ppermute | solution.py:31
  115.0 13.3 %collective-permute-start.35 = (bf16[128,256]{1,0:T(8,128)(2,1)S(1)}, bf16[128,256]{1,0:T(8,128)(2,1)S(1)}, u32[]{:S(2)}, u32[]{:S(2)}) collective-permute-start(bf16[128,256]{1,0:T(8,128)(2,1)S(1)} %get-tuple-element.41), channel_id=1, source_target_pairs={{0,4},{4,8},{8,12},{12,16},{16,20},{20,24},{24,28},{28,0},{1,5},{5... | collective-permute-start | bytes 196616 | tf_op jit(solution)/shard_map/scatter_gradients/ppermute | solution.py:39
  120.6 7.7 %collective-permute-start.39 = (bf16[128,256]{1,0:T(8,128)(2,1)S(1)}, bf16[128,256]{1,0:T(8,128)(2,1)S(1)}, u32[]{:S(2)}, u32[]{:S(2)}) collective-permute-start(bf16[128,256]{1,0:T(8,128)(2,1)S(1)} %get-tuple-element.42), channel_id=1, source_target_pairs={{0,28},{4,0},{8,4},{12,8},{16,12},{20,16},{24,20},{28,24},{1,29},{... | collective-permute-start | bytes 196616 | tf_op jit(solution)/shard_map/scatter_gradients/ppermute | solution.py:39
  124.9 12.8 %collective-permute-start.26 = (bf16[128,256]{1,0:T(8,128)(2,1)S(1)}, bf16[128,256]{1,0:T(8,128)(2,1)S(1)}, u32[]{:S(2)}, u32[]{:S(2)}) collective-permute-start(bf16[128,256]{1,0:T(8,128)(2,1)S(1)} %add_convert_fusion.6), channel_id=1, source_target_pairs={{0,32},{32,0},{1,33},{33,1},{2,34},{34,2},{3,35},{35,3},{4,36},{36... | collective-permute-start | bytes 196616 | tf_op jit(solution)/shard_map/weight_rest/ppermute | solution.py:31
  128.4 9.4 %collective-permute-start.36 = (bf16[256,256]{1,0:T(8,128)(2,1)S(1)}, bf16[256,256]{1,0:T(8,128)(2,1)S(1)}, u32[]{:S(2)}, u32[]{:S(2)}) collective-permute-start(bf16[256,256]{1,0:T(8,128)(2,1)S(1)} %get-tuple-element.37), channel_id=1, source_target_pairs={{0,4},{4,8},{8,12},{12,16},{16,20},{20,24},{24,28},{28,0},{1,5},{5... | collective-permute-start | bytes 393224 | tf_op jit(solution)/shard_map/scatter_gradients/ppermute | solution.py:39
  128.5 9.4 %collective-permute-start.40 = (bf16[256,256]{1,0:T(8,128)(2,1)S(1)}, bf16[256,256]{1,0:T(8,128)(2,1)S(1)}, u32[]{:S(2)}, u32[]{:S(2)}) collective-permute-start(bf16[256,256]{1,0:T(8,128)(2,1)S(1)} %get-tuple-element.38), channel_id=1, source_target_pairs={{0,28},{4,0},{8,4},{12,8},{16,12},{20,16},{24,20},{28,24},{1,29},{... | collective-permute-start | bytes 393224 | tf_op jit(solution)/shard_map/scatter_gradients/ppermute | solution.py:39
  143.2 7.3 %collective-permute-start.38 = (bf16[256,256]{1,0:T(8,128)(2,1)S(1)}, bf16[256,256]{1,0:T(8,128)(2,1)S(1)}, u32[]{:S(2)}, u32[]{:S(2)}) collective-permute-start(bf16[256,256]{1,0:T(8,128)(2,1)S(1)} %get-tuple-element.33), channel_id=1, source_target_pairs={{0,4},{4,8},{8,12},{12,16},{16,20},{20,24},{24,28},{28,0},{1,5},{5... | collective-permute-start | bytes 393224 | tf_op jit(solution)/shard_map/scatter_gradients/ppermute | solution.py:39
  143.2 7.2 %collective-permute-start.42 = (bf16[256,256]{1,0:T(8,128)(2,1)S(1)}, bf16[256,256]{1,0:T(8,128)(2,1)S(1)}, u32[]{:S(2)}, u32[]{:S(2)}) collective-permute-start(bf16[256,256]{1,0:T(8,128)(2,1)S(1)} %get-tuple-element.34), channel_id=1, source_target_pairs={{0,28},{4,0},{8,4},{12,8},{16,12},{20,16},{24,20},{28,24},{1,29},{... | collective-permute-start | bytes 393224 | tf_op jit(solution)/shard_map/scatter_gradients/ppermute | solution.py:39
  (16 other events, 135.0 us)

commit v8 on v7

--- a/solution.py
+++ b/solution.py
@@ -349,7 +349,7 @@
             down = shift(total(back[SPOT[N_Z - d]], away[4 - d][1], down), -1)
         grad_features = total(back[SPOT[0]], away[3][2], up, down)
     with jax.named_scope("weight_rest"):
-        for axis, n, bit in (("xl", 2, 1), ("z", N_Z, 4), ("xh", 2, 1), ("y", N_Y, 1), ("y", N_Y, 2)):
+        for axis, n, bit in (("xl", 2, 1), ("z", N_Z, 4), ("y", N_Y, 1), ("y", N_Y, 2), ("xh", 2, 1)):
             w = add_swapped(w, axis, n, bit)
         grad_weight = pl.pallas_call(
             final_weight_kernel,

time: 152 us -> 151 us (level); the launches traced: 151 us -> 148 us
  waiting for transfers between devices: 33 us -> 27.7 us
  Pallas kernels: 23.9 us -> 20.7 us
  starting transfers between devices: 65.9 us -> 68.8 us
  blocking collectives: 24.5 us -> 27.1 us
    ppermute x26, waiting for transfers between devices: 18.1 us -> 12.6 us  [xor_swap(): return lax.ppermute(x, axis, [(i, i ^ bit) for i in range(n)])]
    ppermute x26, starting transfers between devices: 30.9 us -> 35.2 us  [xor_swap(): return lax.ppermute(x, axis, [(i, i ^ bit) for i in range(n)])]
    pallas_call x7, Pallas kernels: 19.1 us -> 15.9 us  [call(): pl.pallas_call(kernel, out_shape=out_shape, in_specs=[smem, hbm] + [vmem]...]
    all_to_all x1, blocking collectives: 24.5 us -> 27.1 us  [on_device(): parts = lax.all_to_all(partial, REP, 0, 0, tiled=True)]
  transfers between devices with their start and end apart: 44 -> 44, of which waited for: 14 -> 13; matrix products, arithmetic and copies ran while one was open for 1% -> 1% of each run, Pallas kernels for 9% -> 8%
where the time goes in v8:
time: 151 us; the launch traced here: 148 us
  starting transfers between devices  68.8 us (46%)
  waiting for transfers between devices  27.7 us (18%)
  blocking collectives  27.1 us (18%)
  Pallas kernels  20.7 us (14%)
  other arithmetic  2.08 us (1%)
  between operations  1.67 us (1%)
    ppermute x26, starting transfers between devices, xor_swap(): return lax.ppermute(x, axis, [(i, i ^ bit) for i in range(n)])  35.2 us
    ppermute x16, starting transfers between devices, shift(): return lax.ppermute(x, 'z', [(i, (i + step) % N_Z) for i in range(N_Z)])  27.2 us
    all_to_all x1, blocking collectives, on_device(): parts = lax.all_to_all(partial, REP, 0, 0, tiled=True)  27.1 us
    pallas_call x7, Pallas kernels, call(): pl.pallas_call(kernel, out_shape=out_shape, in_specs=[smem, hbm] + [vmem]...  15.9 us
    ppermute x26, waiting for transfers between devices, xor_swap(): return lax.ppermute(x, axis, [(i, i ^ bit) for i in range(n)])  12.6 us
    ppermute x16, waiting for transfers between devices, shift(): return lax.ppermute(x, 'z', [(i, (i + step) % N_Z) for i in range(N_Z)])  8.4 us
    all_to_all x1, waiting for transfers between devices, on_device(): grads = lax.all_to_all(payload, REP, 0, 0, tiled=True)  3.75 us
    all_to_all x1, starting transfers between devices, on_device(): grads = lax.all_to_all(payload, REP, 0, 0, tiled=True)  3.56 us
  transfers between devices with their start and end apart: 44, of which 13 were waited for; matrix products, arithmetic and copies ran while one was open for 1% of the time, Pallas kernels for 8%

profile of v8, /device:TPU:1, one launch (start us, length us, event | category | flops | bytes accessed | tf_op | source)
XLA Modules:
  0.0 148.2 jit_solution(6713788928590863290)
XLA Ops:
  0.6 6.5 %collective-permute-start.5 = (bf16[256,256]{1,0:T(8,128)(2,1)}, bf16[256,256]{1,0:T(8,128)(2,1)S(1)}, u32[]{:S(2)}, u32[]{:S(2)}) collective-permute-start(bf16[256,256]{1,0:T(8,128)(2,1)} %refs_0_.1), channel_id=1, source_target_pairs={{0,28},{4,0},{8,4},{12,8},{16,12},{20,16},{24,20},{28,24},{1,29},{... | collective-permute-start | bytes 393224 | tf_op jit(solution)/shard_map/gather_features/ppermute | solution.py:39
  7.1 2.5 %collective-permute-done.5.refs_1_ = bf16[256,256]{1,0:T(8,128)(2,1)S(1)} collective-permute-done((bf16[256,256]{1,0:T(8,128)(2,1)}, bf16[256,256]{1,0:T(8,128)(2,1)S(1)}, u32[]{:S(2)}, u32[]{:S(2)}) %collective-permute-start.5) | collective-permute-done | bytes 131104 | tf_op jit(solution)/shard_map/gather_features/ppermute | solution.py:39
  9.6 3.3 %collective-permute-start.7 = (bf16[256,256]{1,0:T(8,128)(2,1)S(1)}, bf16[256,256]{1,0:T(8,128)(2,1)S(1)}, u32[]{:S(2)}, u32[]{:S(2)}) collective-permute-start(bf16[256,256]{1,0:T(8,128)(2,1)S(1)} %collective-permute-done.5.refs_1_), channel_id=1, source_target_pairs={{0,28},{4,0},{8,4},{12,8},{16,12},{20,16},{24,20},{28,24},{1,29},{... | collective-permute-start | bytes 393224 | tf_op jit(solution)/shard_map/gather_features/ppermute | solution.py:39
  15.6 2.7 %collective-permute-start.9 = (bf16[256,256]{1,0:T(8,128)(2,1)S(1)}, bf16[256,256]{1,0:T(8,128)(2,1)S(1)}, u32[]{:S(2)}, u32[]{:S(2)}) collective-permute-start(bf16[256,256]{1,0:T(8,128)(2,1)S(1)} %collective-permute-done.7.refs_2_), channel_id=1, source_target_pairs={{0,28},{4,0},{8,4},{12,8},{16,12},{20,16},{24,20},{28,24},{1,29},{... | collective-permute-start | bytes 393224 | tf_op jit(solution)/shard_map/gather_features/ppermute | solution.py:39
  21.1 3.2 %collective-permute-start.13 = (bf16[128,256]{1,0:T(8,128)(2,1)S(1)}, bf16[128,256]{1,0:T(8,128)(2,1)S(1)}, u32[]{:S(2)}, u32[]{:S(2)}) collective-permute-start(bf16[128,256]{1,0:T(8,128)(2,1)S(1)} %slice.100), channel_id=1, source_target_pairs={{0,28},{4,0},{8,4},{12,8},{16,12},{20,16},{24,20},{28,24},{1,29},{... | collective-permute-start | bytes 196616 | tf_op jit(solution)/shard_map/gather_features/ppermute | solution.py:39
  26.5 2.2 %collective-permute-done.11.refs_4_ = bf16[128,256]{1,0:T(8,128)(2,1)S(1)} collective-permute-done((bf16[128,256]{1,0:T(8,128)(2,1)S(1)}, bf16[128,256]{1,0:T(8,128)(2,1)S(1)}, u32[]{:S(2)}, u32[]{:S(2)}) %collective-permute-start.11) | collective-permute-done | bytes 65568 | tf_op jit(solution)/shard_map/gather_features/ppermute | solution.py:39
  30.6 6.2 %collective-permute-start.18 = (bf16[8,256,256]{2,1,0:T(8,128)(2,1)S(1)}, bf16[8,256,256]{2,1,0:T(8,128)(2,1)S(1)}, u32[]{:S(2)}, u32[]{:S(2)}) collective-permute-start(bf16[8,256,256]{2,1,0:T(8,128)(2,1)S(1)} %assemble_own.1.near), channel_id=1, source_target_pairs={{0,1},{1,0},{2,3},{3,2},{4,5},{5,4},{6,7},{7,6},{8,9},{9,8},{10,11... | collective-permute-start | bytes 3145736 | tf_op jit(solution)/shard_map/gather_features/ppermute | solution.py:31
  38.2 2.2 %collective-permute-start.17 = (bf16[8,256,256]{2,1,0:T(8,128)(2,1)S(1)}, bf16[8,256,256]{2,1,0:T(8,128)(2,1)}, u32[]{:S(2)}, u32[]{:S(2)}) collective-permute-start(bf16[8,256,256]{2,1,0:T(8,128)(2,1)S(1)} %assemble_crossed.1.feats), channel_id=1, source_target_pairs={{0,1},{1,0},{2,3},{3,2},{4,5},{5,4},{6,7},{7,6},{8,9},{9,8},{10,11... | collective-permute-start | bytes 3145736 | tf_op jit(solution)/shard_map/gather_features/ppermute | solution.py:31
  41.4 2.7 %tile_products_first.1.before = f32[17,128,256]{2,1,0:T(8,128)S(1)} custom-call(s32[2,256]{1,0:T(2,128)S(1)} %concatenate.9.table.refs_0_, bf16[128,128,128]{2,1,0:T(8,128)(2,1)} %bitcast.58, bf16[8,256,256]{2,1,0:T(8,128)(2,1)S(1)} %assemble_own.1.near, bf16[8,256,256]{2,1,0:T(8,128)(2,1)S(1)} %collective-permute-done.18.far), custom_call_target="tpu_custom_call" | custom-call | flops 1 | bytes 1 | tf_op jit(solution)/shard_map/tile_products/tile_products_first/pallas_call | solution.py:233
  44.1 1.9 %tile_products_near.1.before = f32[17,128,256]{2,1,0:T(8,128)S(1)} custom-call(s32[2,256]{1,0:T(2,128)S(1)} %concatenate.9.table.refs_0_, bf16[128,128,128]{2,1,0:T(8,128)(2,1)} %bitcast.59, bf16[8,256,256]{2,1,0:T(8,128)(2,1)S(1)} %assemble_crossed.1.feats, f32[17,128,256]{2,1,0:T(8,128)S(1)} %tile_products_first.1.before), custom_call_target="tpu_custom_call" | custom-call | flops 1 | bytes 1 | tf_op jit(solution)/shard_map/tile_products/tile_products_near/pallas_call | solution.py:233
  46.0 2.7 %tile_products_far.1 = bf16[8,256,256]{2,1,0:T(8,128)(2,1)S(1)} custom-call(s32[2,256]{1,0:T(2,128)S(1)} %concatenate.9.table.refs_0_, bf16[128,128,128]{2,1,0:T(8,128)(2,1)} %bitcast.60, bf16[8,256,256]{2,1,0:T(8,128)(2,1)} %collective-permute-done.17.feats, f32[17,128,256]{2,1,0:T(8,128)S(1)} %tile_products_near.1.before), custom_call_target="tpu_custom_call" | custom-call | flops 1 | bytes 1 | tf_op jit(solution)/shard_map/tile_products/tile_products_far/pallas_call | solution.py:233
  48.8 27.1 %all_to_all.10.parts = bf16[8,256,256]{2,1,0:T(8,128)(2,1)S(1)} all-to-all(bf16[8,256,256]{2,1,0:T(8,128)(2,1)S(1)} %tile_products_far.1), channel_id=1, replica_groups=mesh['y'=4,'xh'=2,'z'=8,'xl'=2,'core'=2] {'y','xh'}, dimensions={0} | all-to-all | bytes 2097152 | tf_op jit(solution)/shard_map/sum_partials/all_to_all | solution.py:292
  77.3 3.6 %all-to-all-start.1 = ((bf16[8,256,256]{2,1,0:T(8,128)(2,1)}), bf16[8,256,256]{2,1,0:T(8,128)(2,1)S(1)}, u32[]{:S(2)}, u32[]{:S(2)}) async-start(bf16[8,256,256]{2,1,0:T(8,128)(2,1)} %get-tuple-element.23), calls=%async_computation.1 | async-start | bytes 2097152 | tf_op jit(solution)/shard_map/share_gradients/all_to_all | solution.py:310
  81.0 2.9 %collective-permute-start.21 = (bf16[128,256]{1,0:T(8,128)(2,1)S(1)}, bf16[128,256]{1,0:T(8,128)(2,1)S(1)}, u32[]{:S(2)}, u32[]{:S(2)}) collective-permute-start(bf16[128,256]{1,0:T(8,128)(2,1)S(1)} %get-tuple-element.25), channel_id=1, source_target_pairs={{0,5},{1,4},{4,1},{5,0},{8,13},{9,12},{12,9},{13,8},{16,21},{17,20... | collective-permute-start | bytes 196616 | tf_op jit(solution)/shard_map/weight_z/ppermute | solution.py:314
  84.1 3.0 %collective-permute-done.21 = bf16[128,256]{1,0:T(8,128)(2,1)S(1)} collective-permute-done((bf16[128,256]{1,0:T(8,128)(2,1)S(1)}, bf16[128,256]{1,0:T(8,128)(2,1)S(1)}, u32[]{:S(2)}, u32[]{:S(2)}) %collective-permute-start.21) | collective-permute-done | bytes 65568 | tf_op jit(solution)/shard_map/weight_z/ppermute | solution.py:314
  87.2 5.5 %collective-permute-done.22 = bf16[128,256]{1,0:T(8,128)(2,1)S(1)} collective-permute-done((bf16[128,256]{1,0:T(8,128)(2,1)S(1)}, bf16[128,256]{1,0:T(8,128)(2,1)S(1)}, u32[]{:S(2)}, u32[]{:S(2)}) %collective-permute-start.22) | collective-permute-done | bytes 65568 | tf_op jit(solution)/shard_map/weight_z/ppermute | solution.py:31
  92.8 3.7 %all-to-all-done.1.refs_2_ = bf16[8,256,256]{2,1,0:T(8,128)(2,1)S(1)} async-done(((bf16[8,256,256]{2,1,0:T(8,128)(2,1)}), bf16[8,256,256]{2,1,0:T(8,128)(2,1)S(1)}, u32[]{:S(2)}, u32[]{:S(2)}) %all-to-all-start.1) | async-done | bytes 1048608 | tf_op jit(solution)/shard_map/share_gradients/all_to_all | solution.py:310
  96.5 2.1 %back_crossed_far.1 = bf16[8,256,256]{2,1,0:T(8,128)(2,1)S(1)} custom-call(s32[2,256]{1,0:T(2,128)S(1)} %concatenate.9.table.refs_0_, bf16[128,128,128]{2,1,0:T(8,128)(2,1)} %bitcast.61, bf16[8,256,256]{2,1,0:T(8,128)(2,1)S(1)} %all-to-all-done.1.refs_2_), custom_call_target="tpu_custom_call" | custom-call | flops 1 | bytes 1 | tf_op jit(solution)/shard_map/back_crossed/back_crossed_far/pallas_call | solution.py:233
  98.6 2.6 %collective-permute-start.23 = (bf16[8,256,256]{2,1,0:T(8,128)(2,1)S(1)}, bf16[8,256,256]{2,1,0:T(8,128)(2,1)S(1)}, u32[]{:S(2)}, u32[]{:S(2)}) collective-permute-start(bf16[8,256,256]{2,1,0:T(8,128)(2,1)S(1)} %back_crossed_far.1), channel_id=1, source_target_pairs={{0,1},{1,0},{2,3},{3,2},{4,5},{5,4},{6,7},{7,6},{8,9},{9,8},{10,11... | collective-permute-start | bytes 3145736 | tf_op jit(solution)/shard_map/back_crossed/ppermute | solution.py:31
  101.1 2.1 %back_crossed_near.1 = bf16[8,256,256]{2,1,0:T(8,128)(2,1)S(1)} custom-call(s32[2,256]{1,0:T(2,128)S(1)} %concatenate.9.table.refs_0_, bf16[128,128,128]{2,1,0:T(8,128)(2,1)} %bitcast.62, bf16[8,256,256]{2,1,0:T(8,128)(2,1)S(1)} %all-to-all-done.1.refs_2_), custom_call_target="tpu_custom_call" | custom-call | flops 1 | bytes 1 | tf_op jit(solution)/shard_map/back_crossed/back_crossed_near/pallas_call | solution.py:233
  103.7 2.1 %back_own_far.1 = bf16[8,256,256]{2,1,0:T(8,128)(2,1)S(1)} custom-call(s32[2,256]{1,0:T(2,128)S(1)} %concatenate.9.table.refs_0_, bf16[128,128,128]{2,1,0:T(8,128)(2,1)} %bitcast.63, bf16[8,256,256]{2,1,0:T(8,128)(2,1)S(1)} %all-to-all-done.1.refs_2_), custom_call_target="tpu_custom_call" | custom-call | flops 1 | bytes 1 | tf_op jit(solution)/shard_map/back_own/back_own_far/pallas_call | solution.py:233
  106.9 2.4 %back_own_near.1 = bf16[8,256,256]{2,1,0:T(8,128)(2,1)S(1)} custom-call(s32[2,256]{1,0:T(2,128)S(1)} %concatenate.9.table.refs_0_, bf16[128,128,128]{2,1,0:T(8,128)(2,1)} %bitcast.64, bf16[8,256,256]{2,1,0:T(8,128)(2,1)S(1)} %all-to-all-done.1.refs_2_), custom_call_target="tpu_custom_call" | custom-call | flops 1 | bytes 1 | tf_op jit(solution)/shard_map/back_own/back_own_near/pallas_call | solution.py:233
  112.4 4.7 %collective-permute-start.25 = (bf16[128,256]{1,0:T(8,128)(2,1)S(1)}, bf16[128,256]{1,0:T(8,128)(2,1)S(1)}, u32[]{:S(2)}, u32[]{:S(2)}) collective-permute-start(bf16[128,256]{1,0:T(8,128)(2,1)S(1)} %add_convert_fusion.7), channel_id=1, source_target_pairs={{0,16},{4,20},{8,24},{12,28},{16,0},{20,4},{24,8},{28,12},{1,17},{... | collective-permute-start | bytes 196616 | tf_op jit(solution)/shard_map/weight_rest/ppermute | solution.py:31
  117.8 2.5 %collective-permute-done.25 = bf16[128,256]{1,0:T(8,128)(2,1)S(1)} collective-permute-done((bf16[128,256]{1,0:T(8,128)(2,1)S(1)}, bf16[128,256]{1,0:T(8,128)(2,1)S(1)}, u32[]{:S(2)}, u32[]{:S(2)}) %collective-permute-start.25) | collective-permute-done | bytes 65568 | tf_op jit(solution)/shard_map/weight_rest/ppermute | solution.py:31
  120.3 1.7 %collective-permute-start.39 = (bf16[128,256]{1,0:T(8,128)(2,1)S(1)}, bf16[128,256]{1,0:T(8,128)(2,1)S(1)}, u32[]{:S(2)}, u32[]{:S(2)}) collective-permute-start(bf16[128,256]{1,0:T(8,128)(2,1)S(1)} %get-tuple-element.42), channel_id=1, source_target_pairs={{0,28},{4,0},{8,4},{12,8},{16,12},{20,16},{24,20},{28,24},{1,29},{... | collective-permute-start | bytes 196616 | tf_op jit(solution)/shard_map/scatter_gradients/ppermute | solution.py:39
  122.0 3.2 %collective-permute-done.33 = bf16[2,256,256]{2,1,0:T(8,128)(2,1)S(1)} collective-permute-done((bf16[2,256,256]{2,1,0:T(8,128)(2,1)S(1)}, bf16[2,256,256]{2,1,0:T(8,128)(2,1)S(1)}, u32[]{:S(2)}, u32[]{:S(2)}) %collective-permute-start.33) | collective-permute-done | bytes 262176 | tf_op jit(solution)/shard_map/scatter_gradients/ppermute | solution.py:31
  125.4 3.8 %collective-permute-start.40 = (bf16[256,256]{1,0:T(8,128)(2,1)S(1)}, bf16[256,256]{1,0:T(8,128)(2,1)S(1)}, u32[]{:S(2)}, u32[]{:S(2)}) collective-permute-start(bf16[256,256]{1,0:T(8,128)(2,1)S(1)} %get-tuple-element.38), channel_id=1, source_target_pairs={{0,28},{4,0},{8,4},{12,8},{16,12},{20,16},{24,20},{28,24},{1,29},{... | collective-permute-start | bytes 393224 | tf_op jit(solution)/shard_map/scatter_gradients/ppermute | solution.py:39
  129.2 4.1 %collective-permute-start.27 = (bf16[128,256]{1,0:T(8,128)(2,1)S(1)}, bf16[128,256]{1,0:T(8,128)(2,1)S(1)}, u32[]{:S(2)}, u32[]{:S(2)}) collective-permute-start(bf16[128,256]{1,0:T(8,128)(2,1)S(1)} %add_convert_fusion.5), channel_id=1, source_target_pairs={{0,128},{64,192},{128,0},{192,64},{1,129},{65,193},{129,1},{193,65... | collective-permute-start | bytes 196616 | tf_op jit(solution)/shard_map/weight_rest/ppermute | solution.py:31
  133.6 2.7 %collective-permute-start.41 = (bf16[256,256]{1,0:T(8,128)(2,1)S(1)}, bf16[256,256]{1,0:T(8,128)(2,1)S(1)}, u32[]{:S(2)}, u32[]{:S(2)}) collective-permute-start(bf16[256,256]{1,0:T(8,128)(2,1)S(1)} %get-tuple-element.36), channel_id=1, source_target_pairs={{0,28},{4,0},{8,4},{12,8},{16,12},{20,16},{24,20},{28,24},{1,29},{... | collective-permute-start | bytes 393224 | tf_op jit(solution)/shard_map/scatter_gradients/ppermute | solution.py:39
  136.6 2.0 %collective-permute-done.37 = bf16[256,256]{1,0:T(8,128)(2,1)S(1)} collective-permute-done((bf16[256,256]{1,0:T(8,128)(2,1)S(1)}, bf16[256,256]{1,0:T(8,128)(2,1)S(1)}, u32[]{:S(2)}, u32[]{:S(2)}) %collective-permute-start.37) | collective-permute-done | bytes 131104 | tf_op jit(solution)/shard_map/scatter_gradients/ppermute | solution.py:39
  138.8 2.7 %collective-permute-start.42 = (bf16[256,256]{1,0:T(8,128)(2,1)S(1)}, bf16[256,256]{1,0:T(8,128)(2,1)S(1)}, u32[]{:S(2)}, u32[]{:S(2)}) collective-permute-start(bf16[256,256]{1,0:T(8,128)(2,1)S(1)} %get-tuple-element.34), channel_id=1, source_target_pairs={{0,28},{4,0},{8,4},{12,8},{16,12},{20,16},{24,20},{28,24},{1,29},{... | collective-permute-start | bytes 393224 | tf_op jit(solution)/shard_map/scatter_gradients/ppermute | solution.py:39
  141.6 4.3 %collective-permute-start.29 = (bf16[128,256]{1,0:T(8,128)(2,1)S(1)}, bf16[128,256]{1,0:T(8,128)(2,1)S(1)}, u32[]{:S(2)}, u32[]{:S(2)}) collective-permute-start(bf16[128,256]{1,0:T(8,128)(2,1)S(1)} %add_convert_fusion.3.mine), channel_id=1, source_target_pairs={{0,1},{1,0},{2,3},{3,2},{4,5},{5,4},{6,7},{7,6},{8,9},{9,8},{10,11... | collective-permute-start | bytes 196616 | tf_op jit(solution)/shard_map/weight_rest/ppermute | solution.py:31
  (101 shorter events, 21.9 us)
Async XLA Ops:
  0.6 9.0 %collective-permute-start.5 = (bf16[256,256]{1,0:T(8,128)(2,1)}, bf16[256,256]{1,0:T(8,128)(2,1)S(1)}, u32[]{:S(2)}, u32[]{:S(2)}) collective-permute-start(bf16[256,256]{1,0:T(8,128)(2,1)} %refs_0_.1), channel_id=1, source_target_pairs={{0,28},{4,0},{8,4},{12,8},{16,12},{20,16},{24,20},{28,24},{1,29},{... | collective-permute-start | bytes 393224 | tf_op jit(solution)/shard_map/gather_features/ppermute | solution.py:39
  7.1 7.0 %collective-permute-start = (bf16[256,256]{1,0:T(8,128)(2,1)}, bf16[256,256]{1,0:T(8,128)(2,1)S(1)}, u32[]{:S(2)}, u32[]{:S(2)}) collective-permute-start(bf16[256,256]{1,0:T(8,128)(2,1)} %refs_0_.1), channel_id=1, source_target_pairs={{0,4},{4,8},{8,12},{12,16},{16,20},{20,24},{24,28},{28,0},{1,5},{5... | collective-permute-start | bytes 393224 | tf_op jit(solution)/shard_map/gather_features/ppermute | solution.py:39
  9.6 6.0 %collective-permute-start.7 = (bf16[256,256]{1,0:T(8,128)(2,1)S(1)}, bf16[256,256]{1,0:T(8,128)(2,1)S(1)}, u32[]{:S(2)}, u32[]{:S(2)}) collective-permute-start(bf16[256,256]{1,0:T(8,128)(2,1)S(1)} %collective-permute-done.5.refs_1_), channel_id=1, source_target_pairs={{0,28},{4,0},{8,4},{12,8},{16,12},{20,16},{24,20},{28,24},{1,29},{... | collective-permute-start | bytes 393224 | tf_op jit(solution)/shard_map/gather_features/ppermute | solution.py:39
  12.9 5.4 %collective-permute-start.2 = (bf16[256,256]{1,0:T(8,128)(2,1)}, bf16[256,256]{1,0:T(8,128)(2,1)S(1)}, u32[]{:S(2)}, u32[]{:S(2)}) collective-permute-start(bf16[256,256]{1,0:T(8,128)(2,1)} %refs_0_.1), channel_id=1, source_target_pairs={{0,2},{2,0},{1,3},{3,1},{4,6},{6,4},{5,7},{7,5},{8,10},{10,8},{9,1... | collective-permute-start | bytes 393224 | tf_op jit(solution)/shard_map/gather_features/ppermute | solution.py:31
  14.1 7.0 %collective-permute-start.4 = (bf16[256,256]{1,0:T(8,128)(2,1)S(1)}, bf16[256,256]{1,0:T(8,128)(2,1)S(1)}, u32[]{:S(2)}, u32[]{:S(2)}) collective-permute-start(bf16[256,256]{1,0:T(8,128)(2,1)S(1)} %collective-permute-done.refs_8_), channel_id=1, source_target_pairs={{0,2},{2,0},{1,3},{3,1},{4,6},{6,4},{5,7},{7,5},{8,10},{10,8},{9,1... | collective-permute-start | bytes 393224 | tf_op jit(solution)/shard_map/gather_features/ppermute | solution.py:31
  14.4 9.9 %collective-permute-start.6 = (bf16[256,256]{1,0:T(8,128)(2,1)S(1)}, bf16[256,256]{1,0:T(8,128)(2,1)S(1)}, u32[]{:S(2)}, u32[]{:S(2)}) collective-permute-start(bf16[256,256]{1,0:T(8,128)(2,1)S(1)} %collective-permute-done.5.refs_1_), channel_id=1, source_target_pairs={{0,2},{2,0},{1,3},{3,1},{4,6},{6,4},{5,7},{7,5},{8,10},{10,8},{9,1... | collective-permute-start | bytes 393224 | tf_op jit(solution)/shard_map/gather_features/ppermute | solution.py:31
  19.1 5.9 %collective-permute-start.16 = (bf16[256,256]{1,0:T(8,128)(2,1)S(1)}, bf16[256,256]{1,0:T(8,128)(2,1)S(1)}, u32[]{:S(2)}, u32[]{:S(2)}) collective-permute-start(bf16[256,256]{1,0:T(8,128)(2,1)S(1)} %collective-permute-done.1.refs_7_), channel_id=1, source_target_pairs={{0,2},{2,0},{1,3},{3,1},{4,6},{6,4},{5,7},{7,5},{8,10},{10,8},{9,1... | collective-permute-start | bytes 393224 | tf_op jit(solution)/shard_map/gather_features/ppermute | solution.py:31
  20.2 10.3 %collective-permute-start.8 = (bf16[256,256]{1,0:T(8,128)(2,1)S(1)}, bf16[256,256]{1,0:T(8,128)(2,1)S(1)}, u32[]{:S(2)}, u32[]{:S(2)}) collective-permute-start(bf16[256,256]{1,0:T(8,128)(2,1)S(1)} %collective-permute-done.7.refs_2_), channel_id=1, source_target_pairs={{0,2},{2,0},{1,3},{3,1},{4,6},{6,4},{5,7},{7,5},{8,10},{10,8},{9,1... | collective-permute-start | bytes 393224 | tf_op jit(solution)/shard_map/gather_features/ppermute | solution.py:31
  24.4 12.3 %collective-permute-start.10 = (bf16[256,256]{1,0:T(8,128)(2,1)S(1)}, bf16[256,256]{1,0:T(8,128)(2,1)S(1)}, u32[]{:S(2)}, u32[]{:S(2)}) collective-permute-start(bf16[256,256]{1,0:T(8,128)(2,1)S(1)} %collective-permute-done.9.refs_3_), channel_id=1, source_target_pairs={{0,2},{2,0},{1,3},{3,1},{4,6},{6,4},{5,7},{7,5},{8,10},{10,8},{9,1... | collective-permute-start | bytes 393224 | tf_op jit(solution)/shard_map/gather_features/ppermute | solution.py:31
  25.1 11.7 %collective-permute-start.15 = (bf16[256,256]{1,0:T(8,128)(2,1)S(1)}, bf16[256,256]{1,0:T(8,128)(2,1)S(1)}, u32[]{:S(2)}, u32[]{:S(2)}) collective-permute-start(bf16[256,256]{1,0:T(8,128)(2,1)S(1)} %collective-permute-done.3.refs_6_), channel_id=1, source_target_pairs={{0,2},{2,0},{1,3},{3,1},{4,6},{6,4},{5,7},{7,5},{8,10},{10,8},{9,1... | collective-permute-start | bytes 393224 | tf_op jit(solution)/shard_map/gather_features/ppermute | solution.py:31
  25.9 10.8 %collective-permute-start.14 = (bf16[128,256]{1,0:T(8,128)(2,1)S(1)}, bf16[128,256]{1,0:T(8,128)(2,1)S(1)}, u32[]{:S(2)}, u32[]{:S(2)}) collective-permute-start(bf16[128,256]{1,0:T(8,128)(2,1)S(1)} %collective-permute-done.13.refs_5_), channel_id=1, source_target_pairs={{0,2},{2,0},{1,3},{3,1},{4,6},{6,4},{5,7},{7,5},{8,10},{10,8},{9,1... | collective-permute-start | bytes 196616 | tf_op jit(solution)/shard_map/gather_features/ppermute | solution.py:31
  28.7 8.0 %collective-permute-start.12 = (bf16[128,256]{1,0:T(8,128)(2,1)S(1)}, bf16[128,256]{1,0:T(8,128)(2,1)S(1)}, u32[]{:S(2)}, u32[]{:S(2)}) collective-permute-start(bf16[128,256]{1,0:T(8,128)(2,1)S(1)} %collective-permute-done.11.refs_4_), channel_id=1, source_target_pairs={{0,2},{2,0},{1,3},{3,1},{4,6},{6,4},{5,7},{7,5},{8,10},{10,8},{9,1... | collective-permute-start | bytes 196616 | tf_op jit(solution)/shard_map/gather_features/ppermute | solution.py:31
  30.6 10.9 %collective-permute-start.18 = (bf16[8,256,256]{2,1,0:T(8,128)(2,1)S(1)}, bf16[8,256,256]{2,1,0:T(8,128)(2,1)S(1)}, u32[]{:S(2)}, u32[]{:S(2)}) collective-permute-start(bf16[8,256,256]{2,1,0:T(8,128)(2,1)S(1)} %assemble_own.1.near), channel_id=1, source_target_pairs={{0,1},{1,0},{2,3},{3,2},{4,5},{5,4},{6,7},{7,6},{8,9},{9,8},{10,11... | collective-permute-start | bytes 3145736 | tf_op jit(solution)/shard_map/gather_features/ppermute | solution.py:31
  38.2 7.8 %collective-permute-start.17 = (bf16[8,256,256]{2,1,0:T(8,128)(2,1)S(1)}, bf16[8,256,256]{2,1,0:T(8,128)(2,1)}, u32[]{:S(2)}, u32[]{:S(2)}) collective-permute-start(bf16[8,256,256]{2,1,0:T(8,128)(2,1)S(1)} %assemble_crossed.1.feats), channel_id=1, source_target_pairs={{0,1},{1,0},{2,3},{3,2},{4,5},{5,4},{6,7},{7,6},{8,9},{9,8},{10,11... | collective-permute-start | bytes 3145736 | tf_op jit(solution)/shard_map/gather_features/ppermute | solution.py:31
  77.3 19.2 %all-to-all-start.1 = ((bf16[8,256,256]{2,1,0:T(8,128)(2,1)}), bf16[8,256,256]{2,1,0:T(8,128)(2,1)S(1)}, u32[]{:S(2)}, u32[]{:S(2)}) async-start(bf16[8,256,256]{2,1,0:T(8,128)(2,1)} %get-tuple-element.23), calls=%async_computation.1 | async-start | bytes 2097152 | tf_op jit(solution)/shard_map/share_gradients/all_to_all | solution.py:310
  81.0 6.1 %collective-permute-start.21 = (bf16[128,256]{1,0:T(8,128)(2,1)S(1)}, bf16[128,256]{1,0:T(8,128)(2,1)S(1)}, u32[]{:S(2)}, u32[]{:S(2)}) collective-permute-start(bf16[128,256]{1,0:T(8,128)(2,1)S(1)} %get-tuple-element.25), channel_id=1, source_target_pairs={{0,5},{1,4},{4,1},{5,0},{8,13},{9,12},{12,9},{13,8},{16,21},{17,20... | collective-permute-start | bytes 196616 | tf_op jit(solution)/shard_map/weight_z/ppermute | solution.py:314
  87.1 5.6 %collective-permute-start.22 = (bf16[128,256]{1,0:T(8,128)(2,1)S(1)}, bf16[128,256]{1,0:T(8,128)(2,1)S(1)}, u32[]{:S(2)}, u32[]{:S(2)}) collective-permute-start(bf16[128,256]{1,0:T(8,128)(2,1)S(1)} %add_convert_fusion.9), channel_id=1, source_target_pairs={{0,8},{4,12},{8,0},{12,4},{16,24},{20,28},{24,16},{28,20},{1,9},{5... | collective-permute-start | bytes 196616 | tf_op jit(solution)/shard_map/weight_z/ppermute | solution.py:31
  105.8 6.6 %collective-permute-start.30 = (bf16[8,256,256]{2,1,0:T(8,128)(2,1)S(1)}, bf16[8,256,256]{2,1,0:T(8,128)(2,1)S(1)}, u32[]{:S(2)}, u32[]{:S(2)}) collective-permute-start(bf16[8,256,256]{2,1,0:T(8,128)(2,1)S(1)} %back_own_far.1), channel_id=1, source_target_pairs={{0,1},{1,0},{2,3},{3,2},{4,5},{5,4},{6,7},{7,6},{8,9},{9,8},{10,11... | collective-permute-start | bytes 3145736 | tf_op jit(solution)/shard_map/back_own/ppermute | solution.py:31
  106.2 5.5 %collective-permute-start.24 = (bf16[128,256]{1,0:T(8,128)(2,1)S(1)}, bf16[128,256]{1,0:T(8,128)(2,1)S(1)}, u32[]{:S(2)}, u32[]{:S(2)}) collective-permute-start(bf16[128,256]{1,0:T(8,128)(2,1)S(1)} %add_convert_fusion.8), channel_id=1, source_target_pairs={{0,2},{2,0},{1,3},{3,1},{4,6},{6,4},{5,7},{7,5},{8,10},{10,8},{9,1... | collective-permute-start | bytes 196616 | tf_op jit(solution)/shard_map/weight_rest/ppermute | solution.py:31
  109.4 8.0 %collective-permute-start.34 = (bf16[1,256,256]{2,1,0:T(8,128)(2,1)S(1)}, bf16[1,256,256]{2,1,0:T(8,128)(2,1)S(1)}, u32[]{:S(2)}, u32[]{:S(2)}) collective-permute-start(bf16[1,256,256]{2,1,0:T(8,128)(2,1)S(1)} %slice.89), channel_id=1, source_target_pairs={{0,2},{2,0},{1,3},{3,1},{4,6},{6,4},{5,7},{7,5},{8,10},{10,8},{9,1... | collective-permute-start | bytes 393224 | tf_op jit(solution)/shard_map/scatter_gradients/ppermute | solution.py:31
  110.3 23.1 %collective-permute-start.32 = (bf16[2,256,256]{2,1,0:T(8,128)(2,1)S(1)}, bf16[2,256,256]{2,1,0:T(8,128)(2,1)S(1)}, u32[]{:S(2)}, u32[]{:S(2)}) collective-permute-start(bf16[2,256,256]{2,1,0:T(8,128)(2,1)S(1)} %get-tuple-element.39), channel_id=1, source_target_pairs={{0,2},{2,0},{1,3},{3,1},{4,6},{6,4},{5,7},{7,5},{8,10},{10,8},{9,1... | collective-permute-start | bytes 786440 | tf_op jit(solution)/shard_map/scatter_gradients/ppermute | solution.py:31
  110.9 14.3 %collective-permute-start.33 = (bf16[2,256,256]{2,1,0:T(8,128)(2,1)S(1)}, bf16[2,256,256]{2,1,0:T(8,128)(2,1)S(1)}, u32[]{:S(2)}, u32[]{:S(2)}) collective-permute-start(bf16[2,256,256]{2,1,0:T(8,128)(2,1)S(1)} %get-tuple-element.40), channel_id=1, source_target_pairs={{0,2},{2,0},{1,3},{3,1},{4,6},{6,4},{5,7},{7,5},{8,10},{10,8},{9,1... | collective-permute-start | bytes 786440 | tf_op jit(solution)/shard_map/scatter_gradients/ppermute | solution.py:31
  111.8 24.8 %collective-permute-start.31 = (bf16[3,256,256]{2,1,0:T(8,128)(2,1)S(1)}, bf16[3,256,256]{2,1,0:T(8,128)(2,1)S(1)}, u32[]{:S(2)}, u32[]{:S(2)}) collective-permute-start(bf16[3,256,256]{2,1,0:T(8,128)(2,1)S(1)} %slice.78), channel_id=1, source_target_pairs={{0,2},{2,0},{1,3},{3,1},{4,6},{6,4},{5,7},{7,5},{8,10},{10,8},{9,1... | collective-permute-start | bytes 1179656 | tf_op jit(solution)/shard_map/scatter_gradients/ppermute | solution.py:31
  112.4 7.9 %collective-permute-start.25 = (bf16[128,256]{1,0:T(8,128)(2,1)S(1)}, bf16[128,256]{1,0:T(8,128)(2,1)S(1)}, u32[]{:S(2)}, u32[]{:S(2)}) collective-permute-start(bf16[128,256]{1,0:T(8,128)(2,1)S(1)} %add_convert_fusion.7), channel_id=1, source_target_pairs={{0,16},{4,20},{8,24},{12,28},{16,0},{20,4},{24,8},{28,12},{1,17},{... | collective-permute-start | bytes 196616 | tf_op jit(solution)/shard_map/weight_rest/ppermute | solution.py:31
  117.5 7.7 %collective-permute-start.35 = (bf16[128,256]{1,0:T(8,128)(2,1)S(1)}, bf16[128,256]{1,0:T(8,128)(2,1)S(1)}, u32[]{:S(2)}, u32[]{:S(2)}) collective-permute-start(bf16[128,256]{1,0:T(8,128)(2,1)S(1)} %get-tuple-element.41), channel_id=1, source_target_pairs={{0,4},{4,8},{8,12},{12,16},{16,20},{20,24},{24,28},{28,0},{1,5},{5... | collective-permute-start | bytes 196616 | tf_op jit(solution)/shard_map/scatter_gradients/ppermute | solution.py:39
  125.3 8.1 %collective-permute-start.36 = (bf16[256,256]{1,0:T(8,128)(2,1)S(1)}, bf16[256,256]{1,0:T(8,128)(2,1)S(1)}, u32[]{:S(2)}, u32[]{:S(2)}) collective-permute-start(bf16[256,256]{1,0:T(8,128)(2,1)S(1)} %get-tuple-element.37), channel_id=1, source_target_pairs={{0,4},{4,8},{8,12},{12,16},{16,20},{20,24},{24,28},{28,0},{1,5},{5... | collective-permute-start | bytes 393224 | tf_op jit(solution)/shard_map/scatter_gradients/ppermute | solution.py:39
  125.4 8.0 %collective-permute-start.40 = (bf16[256,256]{1,0:T(8,128)(2,1)S(1)}, bf16[256,256]{1,0:T(8,128)(2,1)S(1)}, u32[]{:S(2)}, u32[]{:S(2)}) collective-permute-start(bf16[256,256]{1,0:T(8,128)(2,1)S(1)} %get-tuple-element.38), channel_id=1, source_target_pairs={{0,28},{4,0},{8,4},{12,8},{16,12},{20,16},{24,20},{28,24},{1,29},{... | collective-permute-start | bytes 393224 | tf_op jit(solution)/shard_map/scatter_gradients/ppermute | solution.py:39
  129.2 7.0 %collective-permute-start.27 = (bf16[128,256]{1,0:T(8,128)(2,1)S(1)}, bf16[128,256]{1,0:T(8,128)(2,1)S(1)}, u32[]{:S(2)}, u32[]{:S(2)}) collective-permute-start(bf16[128,256]{1,0:T(8,128)(2,1)S(1)} %add_convert_fusion.5), channel_id=1, source_target_pairs={{0,128},{64,192},{128,0},{192,64},{1,129},{65,193},{129,1},{193,65... | collective-permute-start | bytes 196616 | tf_op jit(solution)/shard_map/weight_rest/ppermute | solution.py:31
  136.3 5.3 %collective-permute-start.28 = (bf16[128,256]{1,0:T(8,128)(2,1)S(1)}, bf16[128,256]{1,0:T(8,128)(2,1)S(1)}, u32[]{:S(2)}, u32[]{:S(2)}) collective-permute-start(bf16[128,256]{1,0:T(8,128)(2,1)S(1)} %add_convert_fusion.4), channel_id=1, source_target_pairs={{0,32},{32,0},{1,33},{33,1},{2,34},{34,2},{3,35},{35,3},{4,36},{36... | collective-permute-start | bytes 196616 | tf_op jit(solution)/shard_map/weight_rest/ppermute | solution.py:31
  138.7 8.8 %collective-permute-start.38 = (bf16[256,256]{1,0:T(8,128)(2,1)S(1)}, bf16[256,256]{1,0:T(8,128)(2,1)S(1)}, u32[]{:S(2)}, u32[]{:S(2)}) collective-permute-start(bf16[256,256]{1,0:T(8,128)(2,1)S(1)} %get-tuple-element.33), channel_id=1, source_target_pairs={{0,4},{4,8},{8,12},{12,16},{16,20},{20,24},{24,28},{28,0},{1,5},{5... | collective-permute-start | bytes 393224 | tf_op jit(solution)/shard_map/scatter_gradients/ppermute | solution.py:39
  138.8 8.7 %collective-permute-start.42 = (bf16[256,256]{1,0:T(8,128)(2,1)S(1)}, bf16[256,256]{1,0:T(8,128)(2,1)S(1)}, u32[]{:S(2)}, u32[]{:S(2)}) collective-permute-start(bf16[256,256]{1,0:T(8,128)(2,1)S(1)} %get-tuple-element.34), channel_id=1, source_target_pairs={{0,28},{4,0},{8,4},{12,8},{16,12},{20,16},{24,20},{28,24},{1,29},{... | collective-permute-start | bytes 393224 | tf_op jit(solution)/shard_map/scatter_gradients/ppermute | solution.py:39
  141.6 5.2 %collective-permute-start.29 = (bf16[128,256]{1,0:T(8,128)(2,1)S(1)}, bf16[128,256]{1,0:T(8,128)(2,1)S(1)}, u32[]{:S(2)}, u32[]{:S(2)}) collective-permute-start(bf16[128,256]{1,0:T(8,128)(2,1)S(1)} %add_convert_fusion.3.mine), channel_id=1, source_target_pairs={{0,1},{1,0},{2,3},{3,2},{4,5},{5,4},{6,7},{7,6},{8,9},{9,8},{10,11... | collective-permute-start | bytes 196616 | tf_op jit(solution)/shard_map/weight_rest/ppermute | solution.py:31
  (16 other events, 142.2 us)
